TPU v7x, 32 devices: a whole 2x2x4 slice. The times are simulated.
32 devices in a mesh: groups: 2 (over y), row: 16 (over z, x, core).
Axes of the slice: x: 2, y: 2, z: 4, core: 2. Of those that a mesh axis runs over, the one named last changes fastest.
Arguments:
- displacement: float32 [16, 3, 512, 512], P('groups', None, 'row'), parts along dimension 0, may hold values from -6 to 6
- loads: float32 [16, 3, 512, 512], P('groups', None, 'row'), parts along dimension 0, may hold values from -6 to 6
- section_stiffness: float32 [6, 512, 512], P('groups'), parts along dimension 0, may hold values from -0.125 to 2.5, as said below
- modulus: float32 [512, 1024], P('row', 'groups'), parts along dimension 1, may hold values from 0.3 to 3
- aggregate: int32 [6, 512, 512], P('groups', 'row'), parts along dimension 0, may hold values from 0 to 127
- basis_weight: float32 [6, 512, 512], P('groups', 'row'), parts along dimension 0, may hold values from 0.02 to 0.2
- diag_inverse: float32 [2048, 256], P('row', 'groups'), parts along dimension 1, may hold values from -0.031 to 0.3, as said below
- sub_factor: float32 [2048, 256], P('row', 'groups'), parts along dimension 1, may hold values from -1.35 to 1.35
Outputs:
- updated: float32 [16, 3, 512, 512], P('groups', None, 'row'), parts along dimension 0
- coarse_solution: float32 [2048, 16], P('row', 'groups'), parts along dimension 1
There are 2 independent parts, one for each index of `groups`. A program takes and returns all parts, laid end to end along the dimension named above; each array names one. Nothing has to cross between parts.
Inputs may be any that keep to these rules, and one draw needn't show every extreme that they name: `section_stiffness`: each cross-section operator is symmetric, with diagonal entries in 1.5 to 2.5. `diag_inverse`: each block is lower triangular, with diagonal entries in 0.2 to 0.3.
All inputs are finite; a program needn't handle non-finite values.
Results may differ from a plain program's by a relative error of at most 0.00017.
Values sent between devices are 32-bit elements; how exact they have to be, the bound alone decides.
No kernel may reach another device: no remote copies, remote signals or barrier semaphores. Data moves between devices by JAX's collectives and lax.ppermute only.
A program may use at most 320 MiB of HBM per device.

v0:
```python
import jax
import jax.numpy as jnp
from jax import lax
from jax.sharding import PartitionSpec as P

highest = lax.Precision.HIGHEST
span_weights = (1.5, -0.15, 1.0 / 90.0)


def padded_2(block, sides, width):
    for axis, dim in sides:
        count = lax.axis_size(axis)
        forward = [(i, i + 1) for i in range(count - 1)]
        backward = [(target, source) for source, target in forward]
        low = lax.ppermute(
            lax.slice_in_dim(block, block.shape[dim] - width, None, axis=dim), axis, forward
        )
        high = lax.ppermute(lax.slice_in_dim(block, 0, width, axis=dim), axis, backward)
        block = jnp.concatenate([low, block, high], axis=dim)
    return block


def prefix(value, axis, join, neutral, backward):
    count, mine = (lax.axis_size(axis), lax.axis_index(axis))
    pieces = jax.tree.map(lambda part: lax.all_gather(part, axis), value)
    if backward:
        pieces = jax.tree.map(lambda part: part[::-1], pieces)
        mine = count - 1 - mine
    running = jax.tree.map(
        lambda part, zero: jnp.full_like(part, 0) + jnp.asarray(zero, part.dtype), value, neutral
    )

    def lap(position, running):
        longer = join(running, jax.tree.map(lambda part: part[position], pieces))
        return jax.tree.map(lambda new, old: jnp.where(position < mine, new, old), longer, running)

    return lax.fori_loop(0, count - 1, lap, running)


def from_behind(value, axis, steps):
    count = lax.axis_size(axis)
    first, last = (max(0, -steps), min(count, count - steps))
    return lax.ppermute(value, axis, [(source, source + steps) for source in range(first, last)])


def matmul(left, right):
    return jnp.dot(left, right, precision=highest, preferred_element_type=jnp.float32)


def compose(first_map, second_map):
    return (
        matmul(second_map[0], first_map[0]),
        matmul(second_map[0], first_map[1]) + second_map[1],
    )


def per_device(
    displacement,
    loads,
    section_stiffness,
    modulus,
    aggregate,
    basis_weight,
    diag_inverse,
    sub_factor,
):
    num_cases, num_comps, layers, section = displacement.shape
    coarse = diag_inverse.shape[1]
    padded = padded_2(displacement, (("row", 2),), 3)
    span_sum = jnp.zeros_like(displacement)
    for offset in range(1, 4):
        layer_below = padded[:, :, 3 - offset : 3 - offset + layers]
        layer_above = padded[:, :, 3 + offset : 3 + offset + layers]
        span_sum = span_sum + span_weights[offset - 1] * (
            2.0 * displacement - layer_below - layer_above
        )
    products = [matmul(displacement[:, comp], section_stiffness[comp]) for comp in range(num_comps)]
    across = jnp.stack(products, axis=1)
    residual = loads - (modulus * span_sum + across)
    diag_total = (
        modulus * (2.0 * sum(span_weights))
        + jnp.diagonal(section_stiffness, axis1=1, axis2=2)[:, None, :]
    )
    smoothed = residual / diag_total
    cells = num_comps * layers * section
    weighted = (basis_weight * residual).reshape(num_cases, cells)
    labels = aggregate.reshape(cells)
    step_layers = 8
    block_rows = section * step_layers
    num_blocks = cells // block_rows
    columns = lax.broadcasted_iota(jnp.int32, (block_rows, coarse), 1)
    coarse_rows_iota = lax.broadcasted_iota(jnp.int32, (coarse, block_rows), 0)

    def restrict(step_index, running):
        first_row = step_index * block_rows
        values_block = lax.dynamic_slice_in_dim(weighted, first_row, block_rows, 1)
        labels_block = lax.dynamic_slice_in_dim(labels, first_row, block_rows, 0)
        onehot = (labels_block[:, None] == columns).astype(jnp.float32)
        return running + matmul(values_block, onehot)

    coarse_rows = lax.fori_loop(
        0, num_blocks, restrict, jnp.zeros((num_cases, coarse), jnp.float32)
    )
    coarse_block = coarse_rows.T
    identity_map = jnp.eye(coarse, dtype=jnp.float32)
    zero_rhs = jnp.zeros((coarse, num_cases), jnp.float32)
    forward_map = -matmul(diag_inverse, sub_factor)
    forward_shift = matmul(diag_inverse, coarse_block)
    preceding = prefix(
        (forward_map, forward_shift), "row", compose, (identity_map, zero_rhs), False
    )
    forward_value = matmul(forward_map, preceding[1]) + forward_shift
    transposed = diag_inverse.T
    next_block = from_behind(sub_factor, "row", -1)
    back_map = -matmul(transposed, next_block.T)
    back_shift = matmul(transposed, forward_value)
    following = prefix((back_map, back_shift), "row", compose, (identity_map, zero_rhs), True)
    coarse_solution = matmul(back_map, following[1]) + back_shift
    solution_rows = coarse_solution.T

    def prolong(step_index, spread_rows):
        first_row = step_index * block_rows
        labels_block = lax.dynamic_slice_in_dim(labels, first_row, block_rows, 0)
        onehot_rows = (coarse_rows_iota == labels_block[None, :]).astype(jnp.float32)
        values_block = matmul(solution_rows, onehot_rows)
        return lax.dynamic_update_slice_in_dim(spread_rows, values_block, first_row, 1)

    spread_flat = lax.fori_loop(0, num_blocks, prolong, jnp.zeros((num_cases, cells), jnp.float32))
    spread = spread_flat.reshape(num_cases, num_comps, layers, section)
    correction = basis_weight * spread
    updated = displacement + smoothed + correction
    return (updated, coarse_solution)


def solution(mesh):
    placed = (
        P("groups", None, "row", None),
        P("groups", None, "row", None),
        P("groups", None, None),
        P("row", "groups"),
        P("groups", "row", None),
        P("groups", "row", None),
        P("row", "groups"),
        P("row", "groups"),
    )
    return jax.shard_map(
        per_device,
        mesh=mesh,
        in_specs=placed,
        out_specs=(P("groups", None, "row", None), P("row", "groups")),
        check_vma=False,
    )
```

profile of v0, /device:TPU:0, one launch (start us, length us, event | category | flops | bytes accessed | tf_op | source)
XLA Modules:
  0.0 218.2 jit_solution(15782571765662988016)
XLA Ops:
  7.2 0.8 copy-done
  8.0 1.7 convolution_negate_fusion
  9.7 1.3 collective-permute-start.2
  11.0 1.6 constant_dynamic-update-slice_fusion.1
  12.7 1.1 copy-done.1
  13.8 0.8 fusion.50
  14.7 1.3 collective-permute-start.1
  16.0 4.4 %collective-permute-start = (f32[8,3,3,512]{3,2,0,1:T(4,128)}, f32[8,3,3,512]{3,2,0,1:T(4,128)}, u32[]{:S(2)}, u32[]{:S(2)}) collective-permute-start(f32[8,3,3,512]{3,2,0,1:T(4,128)} %get-tuple-element.487), channel_id=1, source_target_pairs={{0,1},{1,2},{2,3},{3,4},{4,5},{5,6},{6,7},{7,8},{8,9},{9,10},{10,1... | collective-permute-start | bytes 442376 | tf_op jit(solution)/shard_map/ppermute | solution.py:15
  20.3 60.1 %copy.32 = f32[3,512,512]{0,2,1:T(8,128)} copy(f32[3,512,512]{2,1,0:T(8,128)} %param.18) | data formatting | bytes 6291456 | tf_op args[2]
  80.4 5.5 %gather_fusion = f32[512,3]{1,0:T(8,128)S(1)} fusion(f32[3,512,512]{0,2,1:T(8,128)} %copy.32, s32[512]{0:T(512)S(1)} %bitcast.86), kind=kCustom, calls=%fused_computation | custom fusion | bytes 16384 | tf_op jit(solution)/shard_map/jit(diagonal)/gather | solution.py:82
  86.0 2.6 %convolution_bitcast_fusion.1 = f32[8,1,32,512]{3,2,0,1:T(8,128)S(1)} fusion(f32[3,512,512]{2,1,0:T(8,128)} %param.18, f32[8,3,32,512]{3,2,0,1:T(8,128)} %copy-done.1), kind=kOutput, calls=%fused_computation.54 | convolution fusion | flops 805306368 | bytes 2097152 | tf_op jit(solution)/shard_map/dot_general | solution.py:47
  88.6 2.3 %convolution_bitcast_fusion.2 = f32[8,1,32,512]{3,2,0,1:T(8,128)S(1)} fusion(f32[3,512,512]{2,1,0:T(8,128)} %param.18, f32[8,3,32,512]{3,2,0,1:T(8,128)S(1)} %copy-done.2), kind=kOutput, calls=%fused_computation.55 | convolution fusion | flops 805306368 | bytes 2097152 | tf_op jit(solution)/shard_map/dot_general | solution.py:47
  91.0 3.1 %convolution_bitcast_fusion.3 = f32[8,1,32,512]{3,2,0,1:T(8,128)} fusion(f32[3,512,512]{2,1,0:T(8,128)} %param.18, f32[8,3,32,512]{3,2,0,1:T(8,128)S(1)} %copy-done.2), kind=kOutput, calls=%fused_computation.56 | convolution fusion | flops 805306368 | bytes 2097152 | tf_op jit(solution)/shard_map/dot_general | solution.py:47
  94.1 1.6 copy.38
  95.8 1.7 convolution_negate_fusion.1
  97.5 1.0 constant_dynamic-update-slice_fusion
  98.6 5.9 %broadcast_multiply_fusion = (f32[8,3,32,512]{3,2,0,1:T(8,128)S(1)}, f32[8,3,32,512]{3,2,0,1:T(8,128)}) fusion(f32[3,32,512]{2,1,0:T(8,128)S(1)} %copy-done.5, f32[8,1,32,512]{3,2,0,1:T(8,128)S(1)} %convolution_bitcast_fusion.1, f32[8,1,32,512]{3,2,0,1:T(8,128)S(1)} %convolution_bitcast_fusion.2, f32[8,1,32,512]{3,2,0,1:T(8,128)} %convolution_bitcast_fusion.3, ...), kind=kLoop, calls=%fused_computation.67 | loop fusion | flops 8257536 | bytes 12992512 | tf_op jit(solution)/shard_map/mul | solution.py:86
  104.6 0.9 copy.39
  105.5 20.7 %while.57 = (s32[]{:T(128)}, f32[8,128]{1,0:T(8,128)S(1)}, f32[8,49152]{1,0:T(8,128)S(1)}, s32[49152]{0:T(1024)}, s32[]{:T(128)}, /*index=5*/s32[]{:T(128)}, s32[]{:T(128)}, s32[]{:T(128)}) while((s32[]{:T(128)}, f32[8,128]{1,0:T(8,128)S(1)}, f32[8,49152]{1,0:T(8,128)S(1)}, s32[49152]{0:T(1024)}, s32[]{:T(128)}, ...), condition=%wide.region_1.2_spmd.clone, body=%wide.region_0.1_spmd.clone.sunk | while | flops 50857992 | bytes 188565 | solution.py:101
  106.3 1.0 fusion.78
  108.0 1.0 fusion.78
  109.7 1.0 fusion.78
  111.5 1.0 fusion.78
  113.2 1.0 fusion.78
  114.9 1.0 fusion.78
  116.6 1.0 fusion.78
  118.4 1.0 fusion.78
  120.1 1.0 fusion.78
  121.8 1.0 fusion.78
  123.6 1.0 fusion.78
  125.3 1.0 fusion.78
  126.5 23.3 %all-gather.2 = f32[2048,8]{0,1:T(8,128)S(1)} all-gather(f32[128,8]{0,1:T(8,128)S(1)} %convolution_bitcast_fusion.4), channel_id=4, replica_groups=mesh['groups'=2,'row'=16] {'row'}, dimensions={0}, use_global_device_ids=true | all-gather | bytes 69632 | tf_op jit(solution)/shard_map/all_gather | solution.py:25
  149.7 16.0 %while.58 = (s32[]{:T(128)}, f32[128,8]{0,1:T(8,128)S(1)}, s32[]{:T(128)}, f32[16,128,128]{2,1,0:T(8,128)}, f32[16,128,8]{1,2,0:T(8,128)S(1)}, /*index=5*/s32[]{:T(128)}, s32[]{:T(128)}) while((s32[]{:T(128)}, f32[128,8]{0,1:T(8,128)S(1)}, s32[]{:T(128)}, f32[16,128,128]{2,1,0:T(8,128)}, f32[16,128,8]{1,2,0:T(8,128)S(1)}, ...), condition=%wide.region_3.4_spmd.clone, body=%wide.region_2.3_spmd.clone.sunk | while | flops 1576964 | bytes 92767 | solution.py:37
  149.7 1.0 fusion.81
  150.8 1.1 fusion.81
  151.8 1.1 fusion.81
  152.9 1.1 fusion.81
  154.0 1.1 fusion.81
  155.0 1.1 fusion.81
  156.1 1.1 fusion.81
  157.2 1.1 fusion.81
  158.2 1.1 fusion.81
  159.3 1.1 fusion.81
  160.4 1.1 fusion.81
  161.4 1.1 fusion.81
  162.5 1.1 fusion.81
  163.6 1.1 fusion.81
  164.7 1.1 fusion.81
  166.1 17.8 %all-gather.3 = f32[2048,8]{0,1:T(8,128)S(1)} all-gather(f32[128,8]{0,1:T(8,128)S(1)} %bitcast.98), channel_id=5, replica_groups=mesh['groups'=2,'row'=16] {'row'}, dimensions={0}, use_global_device_ids=true | all-gather | bytes 69632 | tf_op jit(solution)/shard_map/all_gather | solution.py:25
  183.9 1.3 rev.6
  185.2 3.5 %while.59 = (s32[]{:T(128)}, f32[128,8]{0,1:T(8,128)S(1)}, s32[]{:T(128)}, f32[16,128,128]{2,1,0:T(8,128)S(1)}, f32[16,128,8]{1,2,0:T(8,128)S(1)}, /*index=5*/s32[]{:T(128)}, s32[]{:T(128)}) while((s32[]{:T(128)}, f32[128,8]{0,1:T(8,128)S(1)}, s32[]{:T(128)}, f32[16,128,128]{2,1,0:T(8,128)S(1)}, f32[16,128,8]{1,2,0:T(8,128)S(1)}, ...), condition=%wide.region_5.6_spmd.clone, body=%wide.region_4.5_spmd.clone.sunk | while | flops 1576964 | bytes 92767 | solution.py:37
  189.1 17.7 %while.56 = (s32[]{:T(128)}, f32[8,49152]{1,0:T(8,128)S(1)}, s32[49152]{0:T(1024)}, f32[8,128]{1,0:T(8,128)S(1)}, s32[]{:T(128)}, /*index=5*/s32[]{:T(128)}, s32[]{:T(128)}, s32[]{:T(128)}) while((s32[]{:T(128)}, f32[8,49152]{1,0:T(8,128)S(1)}, s32[49152]{0:T(1024)}, f32[8,128]{1,0:T(8,128)S(1)}, s32[]{:T(128)}, ...), condition=%wide.region_7.8_spmd.clone, body=%wide.region_6.7_spmd.clone.sunk | while | flops 50855940 | bytes 184459 | solution.py:128
  189.8 0.7 fusion.76
  191.3 0.7 fusion.76
  192.8 0.7 fusion.76
  194.3 0.7 fusion.76
  195.7 0.7 fusion.76
  197.2 0.7 fusion.76
  198.7 0.7 fusion.76
  200.2 0.7 fusion.76
  201.6 0.7 fusion.76
  203.1 0.7 fusion.76
  206.8 0.9 copy.40
  209.4 1.3 copy.37
  (112 shorter events, 26.1 us)
Async XLA Ops:
  7.2 0.8 copy-start
  7.2 142.6 %all-gather.9.cloned.1.call-start = ((), (), s32[]{:S(2)}) async-start(), calls=%async_computation.1 | async-start | bytes 1114112 | tf_op jit(solution)/shard_map/all_gather | solution.py:25
  9.7 174.2 %all-gather.7.cloned.1.call-start = ((), (), s32[]{:S(2)}) async-start(), calls=%async_computation | async-start | bytes 1114112 | tf_op jit(solution)/shard_map/all_gather | solution.py:25
  9.7 86.0 %collective-permute-start.2 = (f32[128,128]{1,0:T(8,128)}, f32[128,128]{1,0:T(8,128)}, u32[]{:S(2)}, u32[]{:S(2)}) collective-permute-start(f32[128,128]{1,0:T(8,128)} %param.23), channel_id=1, source_target_pairs={{1,0},{2,1},{3,2},{4,3},{5,4},{6,5},{7,6},{8,7},{9,8},{10,9},{11,1... | collective-permute-start | bytes 196616 | tf_op jit(solution)/shard_map/ppermute | solution.py:43
  12.7 1.1 copy-start.1
  14.7 82.8 %collective-permute-start.1 = (f32[8,3,3,512]{3,2,0,1:T(4,128)}, f32[8,3,3,512]{3,2,0,1:T(4,128)}, u32[]{:S(2)}, u32[]{:S(2)}) collective-permute-start(f32[8,3,3,512]{3,2,0,1:T(4,128)} %get-tuple-element.488), channel_id=1, source_target_pairs={{1,0},{2,1},{3,2},{4,3},{5,4},{6,5},{7,6},{8,7},{9,8},{10,9},{11,1... | collective-permute-start | bytes 442376 | tf_op jit(solution)/shard_map/ppermute | solution.py:18
  16.0 82.6 %collective-permute-start = (f32[8,3,3,512]{3,2,0,1:T(4,128)}, f32[8,3,3,512]{3,2,0,1:T(4,128)}, u32[]{:S(2)}, u32[]{:S(2)}) collective-permute-start(f32[8,3,3,512]{3,2,0,1:T(4,128)} %get-tuple-element.487), channel_id=1, source_target_pairs={{0,1},{1,2},{2,3},{3,4},{4,5},{5,6},{6,7},{7,8},{8,9},{9,10},{10,1... | collective-permute-start | bytes 442376 | tf_op jit(solution)/shard_map/ppermute | solution.py:15
  86.0 2.6 %copy-start.2 = (f32[8,3,32,512]{3,2,0,1:T(8,128)S(1)}, f32[8,3,32,512]{3,2,0,1:T(8,128)}, u32[]{:S(2)}) copy-start(f32[8,3,32,512]{3,2,0,1:T(8,128)} %copy-done.1) | copy-start | bytes 4718596
  88.6 2.3 %copy-start.8 = (f32[32,512]{1,0:T(8,128)S(1)}, f32[32,512]{1,0:T(8,128)}, u32[]{:S(2)}) copy-start(f32[32,512]{1,0:T(8,128)} %param.19) | copy-start | bytes 196612
  91.0 7.6 %copy-start.5 = (f32[3,32,512]{2,1,0:T(8,128)S(1)}, f32[3,32,512]{2,1,0:T(8,128)}, u32[]{:S(2)}) copy-start(f32[3,32,512]{2,1,0:T(8,128)} %param.21) | copy-start | bytes 589828
  105.5 60.2 %copy-start.6 = (f32[128,128]{1,0:T(8,128)S(1)}, f32[128,128]{1,0:T(8,128)}, u32[]{:S(2)}) copy-start(f32[128,128]{1,0:T(8,128)} %convolution_negate_fusion) | copy-start | bytes 196612
  165.7 23.0 %copy-start.7 = (f32[128,128]{1,0:T(8,128)S(1)}, f32[128,128]{1,0:T(8,128)}, u32[]{:S(2)}) copy-start(f32[128,128]{1,0:T(8,128)} %convolution_negate_fusion.1) | copy-start | bytes 196612
  206.8 1.4 copy-start.3
  206.8 1.9 copy-start.4
Sparse Core Ops, SparseCore 0:
  10.2 40.7 all-gather.8
  97.6 41.2 all-gather.6
where the time goes:
time: 221 us; the launch traced here: 218 us
  local copies, waits for them, and re-layouts  96 us (43%)
  matrix products  52.1 us (24%)
  blocking collectives  41.1 us (19%)
  between operations  14.3 us (6%)
  other arithmetic  7.2 us (3%)
  starting transfers between devices  7.01 us (3%)
    unnamed x24, local copies, waits for them, and re-layouts  69.4 us
    dot_general x63, matrix products, matmul(): jnp.dot(left, right, precision=highest, preferred_element_type=jnp.float32)  52.1 us
    all_gather x2, blocking collectives, prefix(): pieces = jax.tree.map(lambda part: lax.all_gather(part, axis), value)  41.1 us
    dynamic_slice x12, local copies, waits for them, and re-layouts, restrict(): labels_block = lax.dynamic_slice_in_dim(labels, first_row, block_rows, 0)  8.68 us
    dynamic_slice x12, local copies, waits for them, and re-layouts, prolong(): labels_block = lax.dynamic_slice_in_dim(labels, first_row, block_rows, 0)  8.68 us
    mul x1, other arithmetic, per_device(): weighted = (basis_weight * residual).reshape(num_cases, cells)  5.86 us
    gather x2, local copies, waits for them, and re-layouts, per_device(): jnp.diagonal(section_stiffness, axis1=1, axis2=2)[:, None, :]  5.62 us
  transfers between devices with their start and end apart: 5, of which 0 were waited for; matrix products, arithmetic and copies ran while one was open for 57% of the time, Pallas kernels for 0%

commit v1 on v0

v1 whole, which is shorter than its diff:
```python
import functools

import jax
import jax.numpy as jnp
from jax import lax
from jax.experimental import pallas as pl
from jax.experimental.pallas import tpu as pltpu
from jax.sharding import PartitionSpec as P

span_weights = (1.5, -0.15, 1.0 / 90.0)
bf16, f32 = jnp.bfloat16, jnp.float32
NN = (((1,), (0,)), ((), ()))
NT = (((1,), (1,)), ((), ()))
TN = (((0,), (0,)), ((), ()))


def split(value):
    high = value.astype(bf16)
    return high, (value - high.astype(f32)).astype(bf16)


def dot(left, right, dims):
    return lax.dot_general(left, right, dims, preferred_element_type=f32)


def dot3(left, right, dims):
    left_high, left_low = left
    right_high, right_low = right
    return dot(left_high, right_high, dims) + (
        dot(left_high, right_low, dims) + dot(left_low, right_high, dims)
    )


def residual_kernel(
    disp_ref, loads_ref, section_ref, modulus_ref, labels_ref, weight_ref, below_ref, above_ref,
    base_ref, rows_ref, padded, weighted,
):
    cases, _, layers, section = disp_ref.shape
    coarse = rows_ref.shape[1]
    tiles = section // 128
    stride = weighted.shape[0] // cases
    comp = pl.program_id(0)

    @pl.when(comp == 0)
    def _():
        rows_ref[...] = jnp.zeros_like(rows_ref)

    for tile in range(tiles):
        lanes = slice(tile * 128, (tile + 1) * 128)
        padded[:, tile, 8 : 8 + layers, :] = disp_ref[:, 0, :, lanes]
        padded[:, tile, 5:8, :] = below_ref[:, 0, :, lanes]
        padded[:, tile, 8 + layers : 11 + layers, :] = above_ref[:, 0, :, lanes]

    disp = split(disp_ref[:, 0].reshape(cases * layers, section))
    across = dot3(disp, split(section_ref[0]), NN).reshape(cases, layers, section)
    same = lax.broadcasted_iota(jnp.int32, (128, 128), 0) == lax.broadcasted_iota(
        jnp.int32, (128, 128), 1
    )
    for tile in range(tiles):
        lanes = slice(tile * 128, (tile + 1) * 128)
        block = section_ref[0, lanes, lanes]
        diagonal = jnp.sum(jnp.where(same, block, 0.0), axis=0, keepdims=True)
        modulus = modulus_ref[:, lanes]
        inverse = 1.0 / (modulus * (2.0 * sum(span_weights)) + diagonal)
        weight = weight_ref[0, :, lanes]
        for case in range(cases):
            own = padded[case, tile, 8 : 8 + layers, :]
            span_sum = jnp.zeros_like(own)
            for offset in range(1, 4):
                low = padded[case, tile, 8 - offset : 8 - offset + layers, :]
                high = padded[case, tile, 8 + offset : 8 + offset + layers, :]
                span_sum = span_sum + span_weights[offset - 1] * (2.0 * own - low - high)
            residual = loads_ref[case, 0, :, lanes] - (
                modulus * span_sum + across[case, :, lanes]
            )
            base_ref[case, 0, :, lanes] = own + residual * inverse
            start = case * stride + tile * layers
            weighted[start : start + layers, :] = weight * residual

    bins = lax.broadcasted_iota(jnp.int32, (coarse, 128), 0).astype(f32).astype(bf16)

    def restrict(group, total):
        first = pl.multiple_of(group * 8, 8)
        block = labels_ref[0, pl.ds(first, 8), :].astype(f32)
        for inner in range(8):
            layer = first + inner
            onehots, values = [], []
            for tile in range(tiles):
                lanes = slice(tile * 128, (tile + 1) * 128)
                label = jnp.broadcast_to(block[inner : inner + 1, lanes], (16, 128)).astype(bf16)
                label = jnp.concatenate([label] * (coarse // 16), axis=0)
                onehots.append(jnp.where(label == bins, bf16(1), bf16(0)))
                value = weighted[pl.ds(tile * layers + layer, cases, stride=stride), :]
                values.append(jnp.concatenate(split(value), axis=0))
            total = total + dot(
                jnp.concatenate(values, axis=1), jnp.concatenate(onehots, axis=1), NT
            )
        return total

    total = lax.fori_loop(0, layers // 8, restrict, jnp.zeros((2 * cases, coarse), f32))
    rows_ref[...] += total[:cases] + total[cases:]


def residual_call(disp, loads, section_stiffness, modulus, labels, weight, below, above, coarse):
    cases, comps, layers, section = disp.shape
    wide = pl.BlockSpec((cases, 1, layers, section), lambda a: (0, a, 0, 0))
    halo = pl.BlockSpec((cases, 1, 3, section), lambda a: (0, a, 0, 0))
    node = pl.BlockSpec((1, layers, section), lambda a: (a, 0, 0))
    tiles = section // 128
    return pl.pallas_call(
        residual_kernel,
        grid=(comps,),
        in_specs=[
            wide,
            wide,
            pl.BlockSpec((1, section, section), lambda a: (a, 0, 0)),
            pl.BlockSpec((layers, section), lambda a: (0, 0)),
            node,
            node,
            halo,
            halo,
        ],
        out_specs=[wide, pl.BlockSpec((cases, coarse), lambda a: (0, 0))],
        out_shape=[
            jax.ShapeDtypeStruct(disp.shape, f32),
            jax.ShapeDtypeStruct((cases, coarse), f32),
        ],
        scratch_shapes=[
            pltpu.VMEM((cases, tiles, layers + 16, 128), f32),
            pltpu.VMEM((cases * (tiles * layers + 8), 128), f32),
        ],
        compiler_params=pltpu.CompilerParams(vmem_limit_bytes=40 << 20),
        name="residual",
    )(disp, loads, section_stiffness, modulus, labels, weight, below, above)


def prolong_kernel(base_ref, labels_ref, weight_ref, solution_ref, updated_ref):
    cases, _, layers, section = base_ref.shape
    tables = [
        jnp.broadcast_to(solution_ref[case : case + 1, :], (layers, 128)) for case in range(cases)
    ]
    for tile in range(section // 128):
        lanes = slice(tile * 128, (tile + 1) * 128)
        label = labels_ref[0, :, lanes]
        weight = weight_ref[0, :, lanes]
        for case in range(cases):
            spread = jnp.take_along_axis(
                tables[case], label, axis=1, mode="promise_in_bounds"
            )
            updated_ref[case, 0, :, lanes] = base_ref[case, 0, :, lanes] + weight * spread


def prolong_call(base, labels, weight, solution_rows):
    cases, comps, layers, section = base.shape
    wide = pl.BlockSpec((cases, 1, layers, section), lambda a: (0, a, 0, 0))
    node = pl.BlockSpec((1, layers, section), lambda a: (a, 0, 0))
    return pl.pallas_call(
        prolong_kernel,
        grid=(comps,),
        in_specs=[wide, node, node, pl.BlockSpec(solution_rows.shape, lambda a: (0, 0))],
        out_specs=wide,
        out_shape=jax.ShapeDtypeStruct(base.shape, f32),
        compiler_params=pltpu.CompilerParams(vmem_limit_bytes=32 << 20),
        name="prolong",
    )(base, labels, weight, solution_rows)


def swap(value, axis, mask):
    count = lax.axis_size(axis)
    return lax.ppermute(value, axis, [(i, i ^ mask) for i in range(count)])


def matmul(left, right, dims):
    return lax.dot_general(
        left, right, dims, precision=lax.Precision.HIGHEST, preferred_element_type=f32
    )


def join_maps(first, second):
    phi_a, gram_a = first
    phi_b, gram_b = second
    return (
        matmul(phi_b, phi_a, NN),
        gram_a + matmul(phi_a, matmul(gram_b, phi_a, NN), TN),
    )


def join_shifts(maps_a, maps_b, first, second):
    ahead_a, back_a = first
    ahead_b, back_b = second
    phi_a, _ = maps_a
    phi_b, gram_b = maps_b
    return (
        matmul(ahead_a, phi_b, NT) + ahead_b,
        back_a + matmul(back_b - matmul(ahead_a, gram_b, NN), phi_a, NN),
    )


def pick(flag, one, other):
    return jax.tree.map(lambda a, b: jnp.where(flag, a, b), one, other)


def per_device(
    displacement, loads, section_stiffness, modulus, aggregate, basis_weight, diag_inverse, sub_factor
):
    layers = displacement.shape[2]
    coarse = diag_inverse.shape[1]
    count = lax.axis_size("row")
    mine = lax.axis_index("row")
    odd = (mine & 1) == 1

    first_layers = displacement[:, :, :3]
    last_layers = displacement[:, :, layers - 3 :]
    near = lax.ppermute(
        jnp.where(odd, first_layers, last_layers), "row", [(i, i ^ 1) for i in range(count)]
    )
    far = lax.ppermute(
        jnp.where(odd, last_layers, first_layers),
        "row",
        [(i, i + 1 if i & 1 else i - 1) for i in range(1, count - 1)],
    )
    below = jnp.where(odd, near, far)
    above = jnp.where(odd, far, near)

    step_map = -matmul(diag_inverse, sub_factor, NN)
    maps = (step_map, matmul(step_map, step_map, TN))
    strides = []
    while 4 << len(strides) < count:
        strides.append(1 << len(strides))
    levels = []
    for stride in strides:
        upper = (mine & stride) != 0
        others = jax.tree.map(lambda part: swap(part, "row", stride), maps)
        pair = pick(upper, others, maps), pick(upper, maps, others)
        levels.append((stride, upper, pair))
        maps = join_maps(*pair)
    width = 1 << len(strides)
    ways = count // width
    all_maps = [maps] + [
        jax.tree.map(lambda part, hop=hop: swap(part, "row", hop * width), maps)
        for hop in range(1, ways)
    ]

    base, rhs_rows = residual_call(
        displacement, loads, section_stiffness, modulus, aggregate, basis_weight, below, above, coarse
    )
    value = matmul(rhs_rows, diag_inverse, NT)
    shifts = (value, -matmul(value, step_map, NN))
    for position, (stride, upper, pair) in enumerate(levels):
        others = jax.tree.map(lambda part: swap(part, "row", stride), shifts)
        halves = pick(upper, others, shifts), pick(upper, shifts, others)
        levels[position] = (stride, upper, pair, halves)
        shifts = join_shifts(*pair, *halves)
    all_shifts = [shifts] + [
        jax.tree.map(lambda part, hop=hop: swap(part, "row", hop * width), shifts)
        for hop in range(1, ways)
    ]
    group = mine // width

    def in_order(parts):
        stacked = jax.tree.map(lambda *leaves: jnp.stack(leaves), *parts)
        return [
            jax.tree.map(lambda leaf, at=at: leaf[at ^ group], stacked) for at in range(ways)
        ]

    ordered_maps, ordered_shifts = in_order(all_maps), in_order(all_shifts)
    ahead = [jnp.zeros_like(value)]
    for (phi, _), (shift, _) in zip(ordered_maps[:-1], ordered_shifts[:-1]):
        ahead.append(matmul(ahead[-1], phi, NT) + shift)
    back = [jnp.zeros_like(value)]
    for at in range(ways - 1, 0, -1):
        phi, gram = ordered_maps[at]
        back.append(
            matmul(back[-1], phi, NN) - matmul(ahead[at], gram, NN) + ordered_shifts[at][1]
        )
    back = back[::-1]
    ahead, back = jnp.stack(ahead)[group], jnp.stack(back)[group]
    for stride, upper, (maps_a, maps_b), (shift_a, shift_b) in levels[::-1]:
        middle = matmul(ahead, maps_a[0], NT) + shift_a[0]
        inner = matmul(back, maps_b[0], NN) - matmul(middle, maps_b[1], NN) + shift_b[1]
        ahead = jnp.where(upper, middle, ahead)
        back = jnp.where(upper, back, inner)
    forward_value = matmul(ahead, step_map, NT) + value
    solution_rows = matmul(forward_value - back, diag_inverse, NN)
    updated = prolong_call(base, aggregate, basis_weight, solution_rows)
    return updated, solution_rows.T


def solution(mesh):
    placed = (
        P("groups", None, "row", None),
        P("groups", None, "row", None),
        P("groups", None, None),
        P("row", "groups"),
        P("groups", "row", None),
        P("groups", "row", None),
        P("row", "groups"),
        P("row", "groups"),
    )
    return jax.shard_map(
        per_device,
        mesh=mesh,
        in_specs=placed,
        out_specs=(P("groups", None, "row", None), P("row", "groups")),
        check_vma=False,
    )
```

time: 221 us -> 68.9 us (0.31); the launches traced: 218 us -> 68.4 us
  local copies, waits for them, and re-layouts: 96 us -> 4.59 us
  matrix products: 52.1 us -> 8.71 us
  blocking collectives: 41.1 us -> 0 us
  starting transfers between devices: 7.01 us -> 26.7 us
  between operations: 14.3 us -> 0.85 us
  waiting for transfers between devices: 0.04 us -> 12.3 us
  Pallas kernels: 0 us -> 10.2 us
    unnamed x24 -> x16, local copies, waits for them, and re-layouts: 69.4 us -> 4.59 us
    dot_general x63 -> x33, matrix products: 52.1 us -> 8.71 us  [matmul(): lax.dot_general(left, right, dims, precision=lax.Precision.HIGHEST, prefe...]
    all_gather x2 -> x0, blocking collectives: 41.1 us -> none  [prefix(): pieces = jax.tree.map(lambda part: lax.all_gather(part, axis), value)]
    ppermute x3 -> x22, starting transfers between devices: 6.93 us -> 26.7 us  [the longest x20 21.7 us: swap(): return lax.ppermute(value, axis, [(i, i ^ mask) for i in range(count)])]
    dynamic_slice x24 -> x0, local copies, waits for them, and re-layouts: 17.4 us -> none  [the longest x12 8.68 us: restrict(): labels_block = lax.dynamic_slice_in_dim(labels, first_row, block_rows, 0)]
    ppermute x3 -> x22, waiting for transfers between devices: 0.01 us -> 12.3 us  [the longest x20 12.3 us: swap(): return lax.ppermute(value, axis, [(i, i ^ mask) for i in range(count)])]
    pallas_call x0 -> x2, Pallas kernels: none -> 10.2 us  [the longest x1 7.66 us: residual_call(): pl.pallas_call(residual_kernel, grid=(comps,), in_specs=[wide, wide, pl.B...]
    mul x2 -> x0, other arithmetic: 5.87 us -> none  [the longest x1 5.86 us: per_device(): weighted = (basis_weight * residual).reshape(num_cases, cells)]
  transfers between devices with their start and end apart: 5 -> 22, of which waited for: 0 -> 9; matrix products, arithmetic and copies ran while one was open for 57% -> 14% of each run, Pallas kernels for 0% -> 0%
where the time goes in v1:
time: 68.9 us; the launch traced here: 68.4 us
  starting transfers between devices  26.7 us (39%)
  waiting for transfers between devices  12.3 us (18%)
  Pallas kernels  10.2 us (15%)
  matrix products  8.71 us (13%)
  other arithmetic  5.01 us (7%)
  local copies, waits for them, and re-layouts  4.59 us (7%)
  between operations  0.85 us (1%)
    ppermute x20, starting transfers between devices, swap(): return lax.ppermute(value, axis, [(i, i ^ mask) for i in range(count)])  21.7 us
    ppermute x20, waiting for transfers between devices, swap(): return lax.ppermute(value, axis, [(i, i ^ mask) for i in range(count)])  12.3 us
    dot_general x33, matrix products, matmul(): lax.dot_general(left, right, dims, precision=lax.Precision.HIGHEST, prefe...  8.71 us
    pallas_call x1, Pallas kernels, residual_call(): pl.pallas_call(residual_kernel, grid=(comps,), in_specs=[wide, wide, pl.B...  7.66 us
    unnamed x16, local copies, waits for them, and re-layouts  4.59 us
    ppermute x1, starting transfers between devices, per_device(): lax.ppermute(jnp.where(odd, first_layers, last_layers), 'row', [(i, i ^ 1...  3.69 us
    pallas_call x1, Pallas kernels, prolong_call(): pl.pallas_call(prolong_kernel, grid=(comps,), in_specs=[wide, node, node,...  2.55 us
    select_n x1, other arithmetic, per_device(): jnp.where(odd, last_layers, first_layers)  2.09 us
  transfers between devices with their start and end apart: 22, of which 9 were waited for; matrix products, arithmetic and copies ran while one was open for 14% of the time, Pallas kernels for 0%

profile of v1, /device:TPU:0, one launch (start us, length us, event | category | flops | bytes accessed | tf_op | source)
XLA Modules:
  0.0 68.4 jit_solution(2359662881546255322)
XLA Ops:
  0.6 0.8 %copy-done = f32[128,128]{1,0:T(8,128)S(1)} copy-done((f32[128,128]{1,0:T(8,128)S(1)}, f32[128,128]{1,0:T(8,128)}, u32[]{:S(2)}) %copy-start) | copy-done | bytes 65560
  1.5 1.0 %convolution_negate_fusion = f32[128,128]{1,0:T(8,128)S(1)} fusion(f32[128,128]{1,0:T(8,128)S(1)} %copy-done, f32[128,128]{1,0:T(8,128)} %param.15), kind=kOutput, calls=%fused_computation | convolution fusion | flops 25182208 | bytes 196608 | tf_op jit(solution)/shard_map/dot_general | solution.py:174
  2.5 0.5 collective-permute-start.2
  3.0 0.9 %fusion.84 = f32[128,128]{1,0:T(8,128)} fusion(f32[128,128]{1,0:T(8,128)S(1)} %convolution_negate_fusion), kind=kOutput, calls=%fused_computation.120 | convolution fusion | flops 25165824 | bytes 131072 | tf_op jit(solution)/shard_map/dot_general | solution.py:174
  4.0 2.1 %slice_select_fusion = (f32[8,3,3,512]{3,2,1,0:T(4,128)}, f32[8,3,3,512]{3,2,1,0:T(4,128)}) fusion(f32[8,3,32,512]{3,2,1,0:T(8,128)} %disp_ref.1, pred[]{:T(512)S(6)} %eq.3), kind=kLoop, calls=%fused_computation.21 | loop fusion | flops 73728 | bytes 589825 | tf_op jit(solution)/shard_map/jit(_where)/select_n | solution.py:218
  6.1 1.3 %collective-permute-start.1 = (f32[8,3,3,512]{3,2,1,0:T(4,128)}, f32[8,3,3,512]{3,2,1,0:T(4,128)}, u32[]{:S(2)}, u32[]{:S(2)}) collective-permute-start(f32[8,3,3,512]{3,2,1,0:T(4,128)} %get-tuple-element.6), channel_id=1, source_target_pairs={{1,2},{2,1},{3,4},{4,3},{5,6},{6,5},{7,8},{8,7},{9,10},{10,9},{11,... | collective-permute-start | bytes 442376 | tf_op jit(solution)/shard_map/ppermute | solution.py:217
  7.4 3.7 %collective-permute-start = (f32[8,3,3,512]{3,2,1,0:T(4,128)}, f32[8,3,3,512]{3,2,1,0:T(4,128)}, u32[]{:S(2)}, u32[]{:S(2)}) collective-permute-start(f32[8,3,3,512]{3,2,1,0:T(4,128)} %get-tuple-element.7), channel_id=1, source_target_pairs={{0,1},{1,0},{2,3},{3,2},{4,5},{5,4},{6,7},{7,6},{8,9},{9,8},{10,11... | collective-permute-start | bytes 442376 | tf_op jit(solution)/shard_map/ppermute | solution.py:214
  11.1 0.9 %broadcast_select_fusion.2 = f32[128,128]{1,0:T(8,128)S(1)} fusion(f32[128,128]{1,0:T(8,128)} %fusion.84, f32[128,128]{1,0:T(8,128)} %collective-permute-done.12, pred[]{:T(512)S(6)} %ne.14), kind=kLoop, calls=%fused_computation.58 | loop fusion | flops 16384 | bytes 196609 | tf_op jit(solution)/shard_map/jit(_where)/select_n | solution.py:200
  12.0 0.9 %broadcast_select_fusion.3 = (f32[128,128]{1,0:T(8,128)S(1)}, f32[128,128]{1,0:T(8,128)S(1)}) fusion(f32[128,128]{1,0:T(8,128)} %collective-permute-done.2, f32[128,128]{1,0:T(8,128)S(1)} %convolution_negate_fusion, pred[]{:T(512)S(6)} %ne.14), kind=kLoop, calls=%fused_computation.59 | loop fusion | flops 32768 | bytes 262145 | tf_op jit(solution)/shard_map/jit(_where)/select_n | solution.py:200
  12.9 0.2 fusion.85
  13.1 1.1 %select_add_fusion.1 = f32[128,128]{1,0:T(8,128)S(1)} fusion(f32[128,128]{1,0:T(8,128)} %collective-permute-done.12, f32[128,128]{1,0:T(8,128)} %fusion.84, pred[]{:T(512)S(6)} %ne.14, f32[128,128]{1,0:T(8,128)S(1)} %get-tuple-element.12, f32[128,128]{1,0:T(8,128)S(1)} %fusion.85), kind=kOutput, calls=%fused_computation.51 | convolution fusion | flops 25198592 | bytes 327681 | tf_op jit(solution)/shard_map/dot_general | solution.py:174
  14.2 1.6 %collective-permute-start.13 = (f32[128,128]{1,0:T(8,128)S(1)}, f32[128,128]{1,0:T(8,128)S(1)}, u32[]{:S(2)}, u32[]{:S(2)}) collective-permute-start(f32[128,128]{1,0:T(8,128)S(1)} %select_add_fusion.1), channel_id=1, source_target_pairs={{0,2},{1,3},{2,0},{3,1},{4,6},{5,7},{6,4},{7,5},{8,10},{9,11},{10,... | collective-permute-start | bytes 196616 | tf_op jit(solution)/shard_map/ppermute | solution.py:170
  15.8 0.2 fusion.81
  16.0 0.5 collective-permute-start.3
  16.6 2.1 %collective-permute-done.13 = f32[128,128]{1,0:T(8,128)S(1)} collective-permute-done((f32[128,128]{1,0:T(8,128)S(1)}, f32[128,128]{1,0:T(8,128)S(1)}, u32[]{:S(2)}, u32[]{:S(2)}) %collective-permute-start.13) | collective-permute-done | bytes 65568 | tf_op jit(solution)/shard_map/ppermute | solution.py:170
  18.7 1.7 %collective-permute-done.3 = f32[128,128]{1,0:T(8,128)S(1)} collective-permute-done((f32[128,128]{1,0:T(8,128)S(1)}, f32[128,128]{1,0:T(8,128)S(1)}, u32[]{:S(2)}, u32[]{:S(2)}) %collective-permute-start.3) | collective-permute-done | bytes 65568 | tf_op jit(solution)/shard_map/ppermute | solution.py:170
  20.4 0.2 fusion.86
  20.6 1.1 %broadcast_select_fusion = (f32[8,3,3,512]{3,2,1,0:T(4,128)S(1)}, f32[8,3,3,512]{3,2,1,0:T(4,128)S(1)}) fusion(f32[8,3,3,512]{3,2,1,0:T(4,128)} %collective-permute-done.1, f32[8,3,3,512]{3,2,1,0:T(4,128)} %collective-permute-done, pred[]{:T(512)S(6)} %eq.3), kind=kLoop, calls=%fused_computation.23 | loop fusion | flops 73728 | bytes 589825 | tf_op jit(solution)/shard_map/jit(_where)/select_n | solution.py:223
  21.8 1.4 %copy-done.2 = f32[8,3,32,512]{3,2,1,0:T(8,128)S(1)} copy-done((f32[8,3,32,512]{3,2,1,0:T(8,128)S(1)}, f32[8,3,32,512]{3,2,1,0:T(8,128)}, u32[]{:S(2)}) %copy-start.2) | copy-done | bytes 1572888
  23.2 1.4 %copy-done.3 = f32[8,3,32,512]{3,2,1,0:T(8,128)S(1)} copy-done((f32[8,3,32,512]{3,2,1,0:T(8,128)S(1)}, f32[8,3,32,512]{3,2,1,0:T(8,128)}, u32[]{:S(2)}) %copy-start.3) | copy-done | bytes 1572888
  24.6 0.9 %copy-done.5 = f32[3,32,512]{2,1,0:T(8,128)S(1)} copy-done((f32[3,32,512]{2,1,0:T(8,128)S(1)}, f32[3,32,512]{2,1,0:T(8,128)}, u32[]{:S(2)}) %copy-start.5) | copy-done | bytes 196632
  25.5 7.7 %residual.1 = (f32[8,3,32,512]{3,2,1,0:T(8,128)S(1)}, f32[8,128]{1,0:T(8,128)S(1)}) custom-call(f32[8,3,32,512]{3,2,1,0:T(8,128)S(1)} %copy-done.2, f32[8,3,32,512]{3,2,1,0:T(8,128)S(1)} %copy-done.3, f32[3,512,512]{2,1,0:T(8,128)S(1)} %copy-done.1, f32[32,512]{1,0:T(8,128)S(1)} %copy-done.6, s32[3,32,512]{2,1,0:T(8,128)S(1)} %copy-done.4, ...), custom_call_target="tpu_custom_call" | custom-call | tf_op jit(solution)/shard_map/residual/pallas_call | solution.py:110
  33.2 0.2 fusion.83
  33.3 0.2 convolution_negate_fusion.1
  33.6 0.5 collective-permute-start.17
  34.1 0.3 select_add_fusion
  34.4 3.2 %collective-permute-start.16 = (f32[128,128]{1,0:T(8,128)S(1)}, f32[128,128]{1,0:T(8,128)S(1)}, u32[]{:S(2)}, u32[]{:S(2)}) collective-permute-start(f32[128,128]{1,0:T(8,128)S(1)} %select_add_fusion), channel_id=1, source_target_pairs={{0,12},{1,13},{2,14},{3,15},{4,8},{5,9},{6,10},{7,11},{8,4},{9,5},... | collective-permute-start | bytes 196616 | tf_op jit(solution)/shard_map/ppermute | solution.py:170
  37.9 1.0 %collective-permute-start.18 = (f32[8,128]{1,0:T(8,128)S(1)}, f32[8,128]{1,0:T(8,128)S(1)}, u32[]{:S(2)}, u32[]{:S(2)}) collective-permute-start(f32[8,128]{1,0:T(8,128)S(1)} %select_add_fusion.3), channel_id=1, source_target_pairs={{0,2},{1,3},{2,0},{3,1},{4,6},{5,7},{6,4},{7,5},{8,10},{9,11},{10,... | collective-permute-start | bytes 12296 | tf_op jit(solution)/shard_map/ppermute | solution.py:170
  38.9 0.2 convolution_add_fusion.4
  39.1 1.1 %collective-permute-start.8 = (f32[8,128]{1,0:T(8,128)S(1)}, f32[8,128]{1,0:T(8,128)S(1)}, u32[]{:S(2)}, u32[]{:S(2)}) collective-permute-start(f32[8,128]{1,0:T(8,128)S(1)} %convolution_add_fusion.4), channel_id=1, source_target_pairs={{0,2},{1,3},{2,0},{3,1},{4,6},{5,7},{6,4},{7,5},{8,10},{9,11},{10,... | collective-permute-start | bytes 12296 | tf_op jit(solution)/shard_map/ppermute | solution.py:170
  40.1 0.2 fusion.82
  40.4 1.1 %collective-permute-done.18 = f32[8,128]{1,0:T(8,128)S(1)} collective-permute-done((f32[8,128]{1,0:T(8,128)S(1)}, f32[8,128]{1,0:T(8,128)S(1)}, u32[]{:S(2)}, u32[]{:S(2)}) %collective-permute-start.18) | collective-permute-done | bytes 4128 | tf_op jit(solution)/shard_map/ppermute | solution.py:170
  41.5 1.2 %collective-permute-done.8 = f32[8,128]{1,0:T(8,128)S(1)} collective-permute-done((f32[8,128]{1,0:T(8,128)S(1)}, f32[8,128]{1,0:T(8,128)S(1)}, u32[]{:S(2)}, u32[]{:S(2)}) %collective-permute-start.8) | collective-permute-done | bytes 4128 | tf_op jit(solution)/shard_map/ppermute | solution.py:170
  42.9 0.2 select_add_fusion.2
  43.0 2.4 %collective-permute-start.21 = (f32[8,128]{1,0:T(8,128)S(1)}, f32[8,128]{1,0:T(8,128)S(1)}, u32[]{:S(2)}, u32[]{:S(2)}) collective-permute-start(f32[8,128]{1,0:T(8,128)S(1)} %select_add_fusion.2), channel_id=1, source_target_pairs={{0,12},{1,13},{2,14},{3,15},{4,8},{5,9},{6,10},{7,11},{8,4},{9,5},... | collective-permute-start | bytes 12296 | tf_op jit(solution)/shard_map/ppermute | solution.py:170
  45.4 0.6 collective-permute-start.20
  46.0 1.4 %collective-permute-start.19 = (f32[8,128]{1,0:T(8,128)S(1)}, f32[8,128]{1,0:T(8,128)S(1)}, u32[]{:S(2)}, u32[]{:S(2)}) collective-permute-start(f32[8,128]{1,0:T(8,128)S(1)} %select_add_fusion.2), channel_id=1, source_target_pairs={{0,4},{1,5},{2,6},{3,7},{4,0},{5,1},{6,2},{7,3},{8,12},{9,13},{10,... | collective-permute-start | bytes 12296 | tf_op jit(solution)/shard_map/ppermute | solution.py:170
  47.5 0.2 convolution_add_fusion.3
  47.6 0.8 %collective-permute-done.21 = f32[8,128]{1,0:T(8,128)S(1)} collective-permute-done((f32[8,128]{1,0:T(8,128)S(1)}, f32[8,128]{1,0:T(8,128)S(1)}, u32[]{:S(2)}, u32[]{:S(2)}) %collective-permute-start.21) | collective-permute-done | bytes 4128 | tf_op jit(solution)/shard_map/ppermute | solution.py:170
  48.5 2.4 %collective-permute-start.11 = (f32[8,128]{1,0:T(8,128)S(1)}, f32[8,128]{1,0:T(8,128)S(1)}, u32[]{:S(2)}, u32[]{:S(2)}) collective-permute-start(f32[8,128]{1,0:T(8,128)S(1)} %convolution_add_fusion.3), channel_id=1, source_target_pairs={{0,12},{1,13},{2,14},{3,15},{4,8},{5,9},{6,10},{7,11},{8,4},{9,5},... | collective-permute-start | bytes 12296 | tf_op jit(solution)/shard_map/ppermute | solution.py:170
  50.8 2.0 %collective-permute-start.9 = (f32[8,128]{1,0:T(8,128)S(1)}, f32[8,128]{1,0:T(8,128)S(1)}, u32[]{:S(2)}, u32[]{:S(2)}) collective-permute-start(f32[8,128]{1,0:T(8,128)S(1)} %convolution_add_fusion.3), channel_id=1, source_target_pairs={{0,4},{1,5},{2,6},{3,7},{4,0},{5,1},{6,2},{7,3},{8,12},{9,13},{10,... | collective-permute-start | bytes 12296 | tf_op jit(solution)/shard_map/ppermute | solution.py:170
  52.9 1.0 %collective-permute-done.11 = f32[8,128]{1,0:T(8,128)S(1)} collective-permute-done((f32[8,128]{1,0:T(8,128)S(1)}, f32[8,128]{1,0:T(8,128)S(1)}, u32[]{:S(2)}, u32[]{:S(2)}) %collective-permute-start.11) | collective-permute-done | bytes 4128 | tf_op jit(solution)/shard_map/ppermute | solution.py:170
  53.9 2.4 %collective-permute-start.6 = (f32[128,128]{1,0:T(8,128)S(1)}, f32[128,128]{1,0:T(8,128)S(1)}, u32[]{:S(2)}, u32[]{:S(2)}) collective-permute-start(f32[128,128]{1,0:T(8,128)S(1)} %fusion.82), channel_id=1, source_target_pairs={{0,12},{1,13},{2,14},{3,15},{4,8},{5,9},{6,10},{7,11},{8,4},{9,5},... | collective-permute-start | bytes 196616 | tf_op jit(solution)/shard_map/ppermute | solution.py:170
  56.2 2.0 %collective-permute-start.4 = (f32[128,128]{1,0:T(8,128)S(1)}, f32[128,128]{1,0:T(8,128)S(1)}, u32[]{:S(2)}, u32[]{:S(2)}) collective-permute-start(f32[128,128]{1,0:T(8,128)S(1)} %fusion.82), channel_id=1, source_target_pairs={{0,4},{1,5},{2,6},{3,7},{4,0},{5,1},{6,2},{7,3},{8,12},{9,13},{10,... | collective-permute-start | bytes 196616 | tf_op jit(solution)/shard_map/ppermute | solution.py:170
  58.3 1.7 %collective-permute-done.6 = f32[128,128]{1,0:T(8,128)S(1)} collective-permute-done((f32[128,128]{1,0:T(8,128)S(1)}, f32[128,128]{1,0:T(8,128)S(1)}, u32[]{:S(2)}, u32[]{:S(2)}) %collective-permute-start.6) | collective-permute-done | bytes 65568 | tf_op jit(solution)/shard_map/ppermute | solution.py:170
  59.9 1.4 %collective-permute-done.5 = f32[128,128]{1,0:T(8,128)S(1)} collective-permute-done((f32[128,128]{1,0:T(8,128)S(1)}, f32[128,128]{1,0:T(8,128)S(1)}, u32[]{:S(2)}, u32[]{:S(2)}) %collective-permute-start.5) | collective-permute-done | bytes 65568 | tf_op jit(solution)/shard_map/ppermute | solution.py:170
  61.4 0.2 fusion.38
  61.6 0.2 fusion.33
  61.8 0.2 fusion.26
  62.1 0.2 convolution_add_fusion.2
  62.3 0.2 fusion.87
  62.5 0.2 convolution_add_fusion.1
  62.7 0.2 fusion.88
  62.9 0.2 fusion.20
  63.1 1.1 %collective-permute-done.14 = f32[128,128]{1,0:T(8,128)S(1)} collective-permute-done((f32[128,128]{1,0:T(8,128)S(1)}, f32[128,128]{1,0:T(8,128)S(1)}, u32[]{:S(2)}, u32[]{:S(2)}) %collective-permute-start.14) | collective-permute-done | bytes 65568 | tf_op jit(solution)/shard_map/ppermute | solution.py:170
  64.4 0.2 fusion.22
  64.6 0.2 fusion.13
  64.7 0.2 fusion.29
  64.9 0.2 fusion.9
  65.1 0.2 fusion.3
  65.3 0.2 fusion.1
  65.4 0.2 fusion.4
  65.6 0.2 fusion.89.solution_ref
  65.8 2.6 %prolong.1 = f32[8,3,32,512]{3,2,1,0:T(8,128)} custom-call(f32[8,3,32,512]{3,2,1,0:T(8,128)S(1)} %get-tuple-element.4.base_ref, s32[3,32,512]{2,1,0:T(8,128)S(1)} %copy-done.4, f32[3,32,512]{2,1,0:T(8,128)S(1)} %copy-done.5, f32[8,128]{1,0:T(8,128)S(1)} %fusion.89.solution_ref), custom_call_target="tpu_custom_call" | custom-call | tf_op jit(solution)/shard_map/prolong/pallas_call | solution.py:157
  (43 shorter events, 0.9 us)
Async XLA Ops:
  0.6 0.8 %copy-start = (f32[128,128]{1,0:T(8,128)S(1)}, f32[128,128]{1,0:T(8,128)}, u32[]{:S(2)}) copy-start(f32[128,128]{1,0:T(8,128)} %param.14) | copy-start | bytes 196612
  2.5 9.5 %collective-permute-start.2 = (f32[128,128]{1,0:T(8,128)S(1)}, f32[128,128]{1,0:T(8,128)}, u32[]{:S(2)}, u32[]{:S(2)}) collective-permute-start(f32[128,128]{1,0:T(8,128)S(1)} %convolution_negate_fusion), channel_id=1, source_target_pairs={{0,1},{1,0},{2,3},{3,2},{4,5},{5,4},{6,7},{7,6},{8,9},{9,8},{10,11... | collective-permute-start | bytes 196616 | tf_op jit(solution)/shard_map/ppermute | solution.py:170
  4.0 7.2 %collective-permute-start.12 = (f32[128,128]{1,0:T(8,128)}, f32[128,128]{1,0:T(8,128)}, u32[]{:S(2)}, u32[]{:S(2)}) collective-permute-start(f32[128,128]{1,0:T(8,128)} %fusion.84), channel_id=1, source_target_pairs={{0,1},{1,0},{2,3},{3,2},{4,5},{5,4},{6,7},{7,6},{8,9},{9,8},{10,11... | collective-permute-start | bytes 196616 | tf_op jit(solution)/shard_map/ppermute | solution.py:170
  4.0 17.7 %copy-start.1 = (f32[3,512,512]{2,1,0:T(8,128)S(1)}, f32[3,512,512]{2,1,0:T(8,128)}, u32[]{:S(2)}) copy-start(f32[3,512,512]{2,1,0:T(8,128)} %section_ref.1) | copy-start | bytes 9437188
  4.0 17.7 %copy-start.4 = (s32[3,32,512]{2,1,0:T(8,128)S(1)}, s32[3,32,512]{2,1,0:T(8,128)}, u32[]{:S(2)}) copy-start(s32[3,32,512]{2,1,0:T(8,128)} %labels_ref.3) | copy-start | bytes 589828
  4.0 17.7 %copy-start.6 = (f32[32,512]{1,0:T(8,128)S(1)}, f32[32,512]{1,0:T(8,128)}, u32[]{:S(2)}) copy-start(f32[32,512]{1,0:T(8,128)} %modulus_ref.1) | copy-start | bytes 196612
  6.1 14.5 %collective-permute-start.1 = (f32[8,3,3,512]{3,2,1,0:T(4,128)}, f32[8,3,3,512]{3,2,1,0:T(4,128)}, u32[]{:S(2)}, u32[]{:S(2)}) collective-permute-start(f32[8,3,3,512]{3,2,1,0:T(4,128)} %get-tuple-element.6), channel_id=1, source_target_pairs={{1,2},{2,1},{3,4},{4,3},{5,6},{6,5},{7,8},{8,7},{9,10},{10,9},{11,... | collective-permute-start | bytes 442376 | tf_op jit(solution)/shard_map/ppermute | solution.py:217
  7.4 13.2 %collective-permute-start = (f32[8,3,3,512]{3,2,1,0:T(4,128)}, f32[8,3,3,512]{3,2,1,0:T(4,128)}, u32[]{:S(2)}, u32[]{:S(2)}) collective-permute-start(f32[8,3,3,512]{3,2,1,0:T(4,128)} %get-tuple-element.7), channel_id=1, source_target_pairs={{0,1},{1,0},{2,3},{3,2},{4,5},{5,4},{6,7},{7,6},{8,9},{9,8},{10,11... | collective-permute-start | bytes 442376 | tf_op jit(solution)/shard_map/ppermute | solution.py:214
  14.2 4.4 %collective-permute-start.13 = (f32[128,128]{1,0:T(8,128)S(1)}, f32[128,128]{1,0:T(8,128)S(1)}, u32[]{:S(2)}, u32[]{:S(2)}) collective-permute-start(f32[128,128]{1,0:T(8,128)S(1)} %select_add_fusion.1), channel_id=1, source_target_pairs={{0,2},{1,3},{2,0},{3,1},{4,6},{5,7},{6,4},{7,5},{8,10},{9,11},{10,... | collective-permute-start | bytes 196616 | tf_op jit(solution)/shard_map/ppermute | solution.py:170
  16.0 4.3 %collective-permute-start.3 = (f32[128,128]{1,0:T(8,128)S(1)}, f32[128,128]{1,0:T(8,128)S(1)}, u32[]{:S(2)}, u32[]{:S(2)}) collective-permute-start(f32[128,128]{1,0:T(8,128)S(1)} %fusion.81), channel_id=1, source_target_pairs={{0,2},{1,3},{2,0},{3,1},{4,6},{5,7},{6,4},{7,5},{8,10},{9,11},{10,... | collective-permute-start | bytes 196616 | tf_op jit(solution)/shard_map/ppermute | solution.py:170
  21.8 1.4 %copy-start.2 = (f32[8,3,32,512]{3,2,1,0:T(8,128)S(1)}, f32[8,3,32,512]{3,2,1,0:T(8,128)}, u32[]{:S(2)}) copy-start(f32[8,3,32,512]{3,2,1,0:T(8,128)} %disp_ref.1) | copy-start | bytes 4718596
  23.2 1.4 %copy-start.3 = (f32[8,3,32,512]{3,2,1,0:T(8,128)S(1)}, f32[8,3,32,512]{3,2,1,0:T(8,128)}, u32[]{:S(2)}) copy-start(f32[8,3,32,512]{3,2,1,0:T(8,128)} %loads_ref.1) | copy-start | bytes 4718596
  24.6 0.9 %copy-start.5 = (f32[3,32,512]{2,1,0:T(8,128)S(1)}, f32[3,32,512]{2,1,0:T(8,128)}, u32[]{:S(2)}) copy-start(f32[3,32,512]{2,1,0:T(8,128)} %weight_ref.3) | copy-start | bytes 589828
  33.5 4.0 %collective-permute-start.7 = (f32[8,128]{1,0:T(8,128)S(1)}, f32[8,128]{1,0:T(8,128)S(1)}, u32[]{:S(2)}, u32[]{:S(2)}) collective-permute-start(f32[8,128]{1,0:T(8,128)S(1)} %fusion.83), channel_id=1, source_target_pairs={{0,1},{1,0},{2,3},{3,2},{4,5},{5,4},{6,7},{7,6},{8,9},{9,8},{10,11... | collective-permute-start | bytes 12296 | tf_op jit(solution)/shard_map/ppermute | solution.py:170
  33.6 4.0 %collective-permute-start.17 = (f32[8,128]{1,0:T(8,128)S(1)}, f32[8,128]{1,0:T(8,128)S(1)}, u32[]{:S(2)}, u32[]{:S(2)}) collective-permute-start(f32[8,128]{1,0:T(8,128)S(1)} %convolution_negate_fusion.1), channel_id=1, source_target_pairs={{0,1},{1,0},{2,3},{3,2},{4,5},{5,4},{6,7},{7,6},{8,9},{9,8},{10,11... | collective-permute-start | bytes 12296 | tf_op jit(solution)/shard_map/ppermute | solution.py:170
  34.4 28.7 %collective-permute-start.16 = (f32[128,128]{1,0:T(8,128)S(1)}, f32[128,128]{1,0:T(8,128)S(1)}, u32[]{:S(2)}, u32[]{:S(2)}) collective-permute-start(f32[128,128]{1,0:T(8,128)S(1)} %select_add_fusion), channel_id=1, source_target_pairs={{0,12},{1,13},{2,14},{3,15},{4,8},{5,9},{6,10},{7,11},{8,4},{9,5},... | collective-permute-start | bytes 196616 | tf_op jit(solution)/shard_map/ppermute | solution.py:170
  37.5 25.5 %collective-permute-start.15 = (f32[128,128]{1,0:T(8,128)S(1)}, f32[128,128]{1,0:T(8,128)S(1)}, u32[]{:S(2)}, u32[]{:S(2)}) collective-permute-start(f32[128,128]{1,0:T(8,128)S(1)} %select_add_fusion), channel_id=1, source_target_pairs={{0,8},{1,9},{2,10},{3,11},{4,12},{5,13},{6,14},{7,15},{8,0},{9,1},... | collective-permute-start | bytes 196616 | tf_op jit(solution)/shard_map/ppermute | solution.py:170
  37.9 3.6 %collective-permute-start.18 = (f32[8,128]{1,0:T(8,128)S(1)}, f32[8,128]{1,0:T(8,128)S(1)}, u32[]{:S(2)}, u32[]{:S(2)}) collective-permute-start(f32[8,128]{1,0:T(8,128)S(1)} %select_add_fusion.3), channel_id=1, source_target_pairs={{0,2},{1,3},{2,0},{3,1},{4,6},{5,7},{6,4},{7,5},{8,10},{9,11},{10,... | collective-permute-start | bytes 12296 | tf_op jit(solution)/shard_map/ppermute | solution.py:170
  39.1 3.7 %collective-permute-start.8 = (f32[8,128]{1,0:T(8,128)S(1)}, f32[8,128]{1,0:T(8,128)S(1)}, u32[]{:S(2)}, u32[]{:S(2)}) collective-permute-start(f32[8,128]{1,0:T(8,128)S(1)} %convolution_add_fusion.4), channel_id=1, source_target_pairs={{0,2},{1,3},{2,0},{3,1},{4,6},{5,7},{6,4},{7,5},{8,10},{9,11},{10,... | collective-permute-start | bytes 12296 | tf_op jit(solution)/shard_map/ppermute | solution.py:170
  43.0 5.4 %collective-permute-start.21 = (f32[8,128]{1,0:T(8,128)S(1)}, f32[8,128]{1,0:T(8,128)S(1)}, u32[]{:S(2)}, u32[]{:S(2)}) collective-permute-start(f32[8,128]{1,0:T(8,128)S(1)} %select_add_fusion.2), channel_id=1, source_target_pairs={{0,12},{1,13},{2,14},{3,15},{4,8},{5,9},{6,10},{7,11},{8,4},{9,5},... | collective-permute-start | bytes 12296 | tf_op jit(solution)/shard_map/ppermute | solution.py:170
  45.4 5.4 %collective-permute-start.20 = (f32[8,128]{1,0:T(8,128)S(1)}, f32[8,128]{1,0:T(8,128)S(1)}, u32[]{:S(2)}, u32[]{:S(2)}) collective-permute-start(f32[8,128]{1,0:T(8,128)S(1)} %select_add_fusion.2), channel_id=1, source_target_pairs={{0,8},{1,9},{2,10},{3,11},{4,12},{5,13},{6,14},{7,15},{8,0},{9,1},... | collective-permute-start | bytes 12296 | tf_op jit(solution)/shard_map/ppermute | solution.py:170
  46.0 4.8 %collective-permute-start.19 = (f32[8,128]{1,0:T(8,128)S(1)}, f32[8,128]{1,0:T(8,128)S(1)}, u32[]{:S(2)}, u32[]{:S(2)}) collective-permute-start(f32[8,128]{1,0:T(8,128)S(1)} %select_add_fusion.2), channel_id=1, source_target_pairs={{0,4},{1,5},{2,6},{3,7},{4,0},{5,1},{6,2},{7,3},{8,12},{9,13},{10,... | collective-permute-start | bytes 12296 | tf_op jit(solution)/shard_map/ppermute | solution.py:170
  48.5 5.4 %collective-permute-start.11 = (f32[8,128]{1,0:T(8,128)S(1)}, f32[8,128]{1,0:T(8,128)S(1)}, u32[]{:S(2)}, u32[]{:S(2)}) collective-permute-start(f32[8,128]{1,0:T(8,128)S(1)} %convolution_add_fusion.3), channel_id=1, source_target_pairs={{0,12},{1,13},{2,14},{3,15},{4,8},{5,9},{6,10},{7,11},{8,4},{9,5},... | collective-permute-start | bytes 12296 | tf_op jit(solution)/shard_map/ppermute | solution.py:170
  50.8 5.4 %collective-permute-start.10 = (f32[8,128]{1,0:T(8,128)S(1)}, f32[8,128]{1,0:T(8,128)S(1)}, u32[]{:S(2)}, u32[]{:S(2)}) collective-permute-start(f32[8,128]{1,0:T(8,128)S(1)} %convolution_add_fusion.3), channel_id=1, source_target_pairs={{0,8},{1,9},{2,10},{3,11},{4,12},{5,13},{6,14},{7,15},{8,0},{9,1},... | collective-permute-start | bytes 12296 | tf_op jit(solution)/shard_map/ppermute | solution.py:170
  50.8 5.4 %collective-permute-start.9 = (f32[8,128]{1,0:T(8,128)S(1)}, f32[8,128]{1,0:T(8,128)S(1)}, u32[]{:S(2)}, u32[]{:S(2)}) collective-permute-start(f32[8,128]{1,0:T(8,128)S(1)} %convolution_add_fusion.3), channel_id=1, source_target_pairs={{0,4},{1,5},{2,6},{3,7},{4,0},{5,1},{6,2},{7,3},{8,12},{9,13},{10,... | collective-permute-start | bytes 12296 | tf_op jit(solution)/shard_map/ppermute | solution.py:170
  53.9 6.1 %collective-permute-start.6 = (f32[128,128]{1,0:T(8,128)S(1)}, f32[128,128]{1,0:T(8,128)S(1)}, u32[]{:S(2)}, u32[]{:S(2)}) collective-permute-start(f32[128,128]{1,0:T(8,128)S(1)} %fusion.82), channel_id=1, source_target_pairs={{0,12},{1,13},{2,14},{3,15},{4,8},{5,9},{6,10},{7,11},{8,4},{9,5},... | collective-permute-start | bytes 196616 | tf_op jit(solution)/shard_map/ppermute | solution.py:170
  56.2 5.2 %collective-permute-start.5 = (f32[128,128]{1,0:T(8,128)S(1)}, f32[128,128]{1,0:T(8,128)S(1)}, u32[]{:S(2)}, u32[]{:S(2)}) collective-permute-start(f32[128,128]{1,0:T(8,128)S(1)} %fusion.82), channel_id=1, source_target_pairs={{0,8},{1,9},{2,10},{3,11},{4,12},{5,13},{6,14},{7,15},{8,0},{9,1},... | collective-permute-start | bytes 196616 | tf_op jit(solution)/shard_map/ppermute | solution.py:170
  56.2 5.2 %collective-permute-start.4 = (f32[128,128]{1,0:T(8,128)S(1)}, f32[128,128]{1,0:T(8,128)S(1)}, u32[]{:S(2)}, u32[]{:S(2)}) collective-permute-start(f32[128,128]{1,0:T(8,128)S(1)} %fusion.82), channel_id=1, source_target_pairs={{0,4},{1,5},{2,6},{3,7},{4,0},{5,1},{6,2},{7,3},{8,12},{9,13},{10,... | collective-permute-start | bytes 196616 | tf_op jit(solution)/shard_map/ppermute | solution.py:170
  59.9 4.3 %collective-permute-start.14 = (f32[128,128]{1,0:T(8,128)S(1)}, f32[128,128]{1,0:T(8,128)S(1)}, u32[]{:S(2)}, u32[]{:S(2)}) collective-permute-start(f32[128,128]{1,0:T(8,128)S(1)} %select_add_fusion), channel_id=1, source_target_pairs={{0,4},{1,5},{2,6},{3,7},{4,0},{5,1},{6,2},{7,3},{8,12},{9,13},{10,... | collective-permute-start | bytes 196616 | tf_op jit(solution)/shard_map/ppermute | solution.py:170
  65.8 2.6 %copy-start.7 = (f32[8,128]{1,0:T(8,128)}, f32[8,128]{1,0:T(8,128)S(1)}, u32[]{:S(2)}) copy-start(f32[8,128]{1,0:T(8,128)S(1)} %fusion.89.solution_ref) | copy-start | bytes 12292

commit v2 on v1

v2 whole, which is shorter than its diff:
```python
import functools

import jax
import jax.numpy as jnp
from jax import lax
from jax.experimental import pallas as pl
from jax.experimental.pallas import tpu as pltpu
from jax.sharding import PartitionSpec as P

span_weights = (1.5, -0.15, 1.0 / 90.0)
bf16, f32 = jnp.bfloat16, jnp.float32
NN = (((1,), (0,)), ((), ()))
NT = (((1,), (1,)), ((), ()))
TN = (((0,), (0,)), ((), ()))


def split(value):
    high = value.astype(bf16)
    return high, (value - high.astype(f32)).astype(bf16)


def dot(left, right, dims):
    return lax.dot_general(left, right, dims, preferred_element_type=f32)


def dot3(left, right, dims):
    left_high, left_low = left
    right_high, right_low = right
    return dot(left_high, right_high, dims) + (
        dot(left_high, right_low, dims) + dot(left_low, right_high, dims)
    )


def dot_rows(rows, weights, dims):
    high, low = split(rows)
    weight_high, weight_low = weights
    count = rows.shape[0]
    both = dot(jnp.concatenate([high, low], axis=0), weight_high, dims)
    return both[:count] + both[count:] + dot(high, weight_low, dims)


def residual_kernel(
    disp_ref, loads_ref, section_ref, modulus_ref, labels_ref, weight_ref, near_ref, far_ref,
    inverse_ref, base_ref, value_ref, padded, weighted, rows_ref,
):
    cases, _, layers, section = disp_ref.shape
    comps = pl.num_programs(0)
    coarse = rows_ref.shape[1]
    mine = lax.axis_index("row")
    odd = (mine & 1) == 1
    lowest, highest = mine == 0, mine == lax.axis_size("row") - 1
    tiles = section // 128
    stride = weighted.shape[0] // cases
    comp = pl.program_id(0)

    @pl.when(comp == 0)
    def _():
        rows_ref[...] = jnp.zeros_like(rows_ref)

    for tile in range(tiles):
        lanes = slice(tile * 128, (tile + 1) * 128)
        padded[:, tile, 8 : 8 + layers, :] = disp_ref[:, 0, :, lanes]
        for row in range(3):
            rows = pl.ds((tile * 3 + row) * cases * 3 + comp * cases, cases)
            near, far = near_ref[rows, :], far_ref[rows, :]
            below = jnp.where(lowest, 0.0, jnp.where(odd, near, far))
            above = jnp.where(highest, 0.0, jnp.where(odd, far, near))
            for case in range(cases):
                padded[case, tile, 5 + row : 6 + row, :] = below[case : case + 1]
                low = 8 + layers + row
                padded[case, tile, low : low + 1, :] = above[case : case + 1]

    disp = split(disp_ref[:, 0].reshape(cases * layers, section))
    across = dot3(disp, split(section_ref[0]), NN).reshape(cases, layers, section)
    same = lax.broadcasted_iota(jnp.int32, (128, 128), 0) == lax.broadcasted_iota(
        jnp.int32, (128, 128), 1
    )
    for tile in range(tiles):
        lanes = slice(tile * 128, (tile + 1) * 128)
        block = section_ref[0, lanes, lanes]
        diagonal = jnp.sum(jnp.where(same, block, 0.0), axis=0, keepdims=True)
        modulus = modulus_ref[:, lanes]
        inverse = 1.0 / (modulus * (2.0 * sum(span_weights)) + diagonal)
        weight = weight_ref[0, :, lanes]
        for case in range(cases):
            own = padded[case, tile, 8 : 8 + layers, :]
            span_sum = jnp.zeros_like(own)
            for offset in range(1, 4):
                low = padded[case, tile, 8 - offset : 8 - offset + layers, :]
                high = padded[case, tile, 8 + offset : 8 + offset + layers, :]
                span_sum = span_sum + span_weights[offset - 1] * (2.0 * own - low - high)
            residual = loads_ref[case, 0, :, lanes] - (
                modulus * span_sum + across[case, :, lanes]
            )
            base_ref[case, 0, :, lanes] = own + residual * inverse
            start = case * stride + tile * layers
            weighted[start : start + layers, :] = weight * residual

    bins = lax.broadcasted_iota(jnp.int32, (coarse, 128), 0).astype(f32).astype(bf16)

    def restrict(group, total):
        first = pl.multiple_of(group * 8, 8)
        block = labels_ref[0, pl.ds(first, 8), :].astype(f32)
        for inner in range(8):
            layer = first + inner
            onehots, values = [], []
            for tile in range(tiles):
                lanes = slice(tile * 128, (tile + 1) * 128)
                label = jnp.broadcast_to(block[inner : inner + 1, lanes], (16, 128)).astype(bf16)
                label = jnp.concatenate([label] * (coarse // 16), axis=0)
                onehots.append(jnp.where(label == bins, bf16(1), bf16(0)))
                value = weighted[pl.ds(tile * layers + layer, cases, stride=stride), :]
                values.append(jnp.concatenate(split(value), axis=0))
            total = total + dot(
                jnp.concatenate(values, axis=1), jnp.concatenate(onehots, axis=1), NT
            )
        return total

    total = lax.fori_loop(0, layers // 8, restrict, jnp.zeros((2 * cases, coarse), f32))
    rows_ref[...] += total[:cases] + total[cases:]

    @pl.when(comp == comps - 1)
    def _():
        value_ref[...] = dot_rows(rows_ref[...], split(inverse_ref[...]), NT)


def residual_call(disp, loads, section_stiffness, modulus, labels, weight, near, far, diag_inverse):
    cases, comps, layers, section = disp.shape
    wide = pl.BlockSpec((cases, 1, layers, section), lambda a: (0, a, 0, 0))
    coarse = diag_inverse.shape[0]
    halo = pl.BlockSpec((cases * comps * 3 * section // 128, 128), lambda a: (0, 0))
    node = pl.BlockSpec((1, layers, section), lambda a: (a, 0, 0))
    tiles = section // 128
    return pl.pallas_call(
        residual_kernel,
        grid=(comps,),
        in_specs=[
            wide,
            wide,
            pl.BlockSpec((1, section, section), lambda a: (a, 0, 0)),
            pl.BlockSpec((layers, section), lambda a: (0, 0)),
            node,
            node,
            halo,
            halo,
            pl.BlockSpec((coarse, coarse), lambda a: (0, 0)),
        ],
        out_specs=[wide, pl.BlockSpec((cases, coarse), lambda a: (0, 0))],
        out_shape=[
            jax.ShapeDtypeStruct(disp.shape, f32),
            jax.ShapeDtypeStruct((cases, coarse), f32),
        ],
        scratch_shapes=[
            pltpu.VMEM((cases, tiles, layers + 16, 128), f32),
            pltpu.VMEM((cases * (tiles * layers + 8), 128), f32),
            pltpu.VMEM((cases, coarse), f32),
        ],
        compiler_params=pltpu.CompilerParams(vmem_limit_bytes=18 << 20),
        name="residual",
    )(disp, loads, section_stiffness, modulus, labels, weight, near, far, diag_inverse)


def small(limit):
    return pltpu.CompilerParams(vmem_limit_bytes=limit << 20)


def start_kernel(
    inverse_hbm, sub_hbm, disp_hbm, step_ref, near_ref, far_ref, inverse, sub, first, last, sems
):
    cases, comps, rows, section = first.shape
    layers = disp_hbm.shape[2]
    copies = [
        pltpu.make_async_copy(inverse_hbm, inverse, sems.at[0]),
        pltpu.make_async_copy(sub_hbm, sub, sems.at[1]),
        pltpu.make_async_copy(disp_hbm.at[:, :, pl.ds(0, rows), :], first, sems.at[2]),
        pltpu.make_async_copy(disp_hbm.at[:, :, pl.ds(layers - rows, rows), :], last, sems.at[3]),
    ]
    for copy in copies:
        copy.start()
    odd = (lax.axis_index("row") & 1) == 1
    copies[0].wait()
    copies[1].wait()
    step_ref[...] = -dot3(split(inverse[...]), split(sub[...]), NN)
    copies[2].wait()
    copies[3].wait()
    for tile in range(section // 128):
        lanes = slice(tile * 128, (tile + 1) * 128)
        for row in range(3):
            for comp in range(comps):
                at = (tile * 3 + row) * cases * comps + comp * cases
                low = first[:, comp, row, lanes]
                high = last[:, comp, rows - 3 + row, lanes]
                near_ref[at : at + cases, :] = jnp.where(odd, low, high)
                far_ref[at : at + cases, :] = jnp.where(odd, high, low)


def start_call(diag_inverse, sub_factor, displacement):
    cases, comps, layers, section = displacement.shape
    packed = jax.ShapeDtypeStruct((cases * comps * 3 * section // 128, 128), f32)
    block = pltpu.VMEM((cases, comps, 8, section), f32)
    square = pltpu.VMEM(diag_inverse.shape, f32)
    return pl.pallas_call(
        start_kernel,
        in_specs=[pl.BlockSpec(memory_space=pltpu.HBM)] * 3,
        out_specs=[pl.BlockSpec(memory_space=pltpu.VMEM)] * 3,
        out_shape=[jax.ShapeDtypeStruct(diag_inverse.shape, f32), packed, packed],
        scratch_shapes=[square, square, block, block, pltpu.SemaphoreType.DMA((4,))],
        compiler_params=small(4),
        name="start",
    )(diag_inverse, sub_factor, displacement)


def pair_maps_kernel(own_ref, other_ref, maps_ref, mixed_ref):
    order = own_ref.shape[0]
    odd = (lax.axis_index("row") & 1) == 1
    own, other = own_ref[...], other_ref[...]
    first = jnp.where(odd, other, own)
    first_split, second_split = split(first), split(jnp.where(odd, own, other))
    phi = dot3(second_split, first_split, NN)
    phi_split = split(phi)
    maps_ref[:order, :] = phi
    maps_ref[order:, :] = dot3(first_split, first_split, TN) + dot3(phi_split, phi_split, TN)
    mixed_ref[...] = first + dot3(second_split, phi_split, TN)


def join_maps_kernel(stride, own_ref, other_ref, maps_ref, mixed_ref):
    order = own_ref.shape[1]
    upper = (lax.axis_index("row") & stride) != 0
    own, other = own_ref[...], other_ref[...]
    first, second = jnp.where(upper, other, own), jnp.where(upper, own, other)
    phi = split(first[:order])
    mixed = dot3(split(second[order:]), phi, NN)
    maps_ref[:order, :] = dot3(split(second[:order]), phi, NN)
    maps_ref[order:, :] = first[order:] + dot3(phi, split(mixed), TN)
    mixed_ref[...] = mixed


def maps_call(kernel, name, own, other):
    order = own.shape[1]
    return pl.pallas_call(
        kernel,
        out_shape=[
            jax.ShapeDtypeStruct((2 * order, order), f32),
            jax.ShapeDtypeStruct((order, order), f32),
        ],
        compiler_params=small(3),
        name=name,
    )(own, other)


def pair_shifts_kernel(own_ref, other_ref, own_step_ref, other_step_ref, maps_ref, mixed_ref, out_ref):
    cases, order = own_ref.shape
    odd = (lax.axis_index("row") & 1) == 1
    own, other = own_ref[...], other_ref[...]
    first, second = jnp.where(odd, other, own), jnp.where(odd, own, other)
    second_step = jnp.where(odd, own_step_ref[...], other_step_ref[...])
    out_ref[:cases, :] = dot_rows(first, split(second_step), NT) + second
    out_ref[cases:, :] = -(
        dot_rows(first, split(mixed_ref[...]), NN)
        + dot_rows(second, split(maps_ref[:order, :]), NN)
    )


def join_shifts_kernel(stride, own_ref, other_ref, own_maps_ref, other_maps_ref, mixed_ref, out_ref):
    order = mixed_ref.shape[0]
    cases = own_ref.shape[0] // 2
    upper = (lax.axis_index("row") & stride) != 0
    own, other = own_ref[...], other_ref[...]
    first, second = jnp.where(upper, other, own), jnp.where(upper, own, other)
    own_phi, other_phi = own_maps_ref[:order, :], other_maps_ref[:order, :]
    first_phi = jnp.where(upper, other_phi, own_phi)
    second_phi = jnp.where(upper, own_phi, other_phi)
    out_ref[:cases, :] = dot_rows(first[:cases], split(second_phi), NT) + second[:cases]
    out_ref[cases:, :] = (
        first[cases:]
        + dot_rows(second[cases:], split(first_phi), NN)
        - dot_rows(first[:cases], split(mixed_ref[...]), NN)
    )


def shifts_call(kernel, name, cases, *operands):
    return pl.pallas_call(
        kernel,
        out_shape=jax.ShapeDtypeStruct((2 * cases, operands[0].shape[1]), f32),
        compiler_params=small(3),
        name=name,
    )(*operands)


def finish_kernel(strides, width, ways, *refs):
    maps, refs = refs[:ways], refs[ways:]
    shifts, refs = refs[:ways], refs[ways:]
    levels = []
    for stride in strides:
        levels.append((stride, *refs[:4]))
        refs = refs[4:]
    (own_step_ref, other_step_ref, own_value_ref, other_value_ref, inverse_ref, base_hbm, labels_ref,
     weight_ref, updated_hbm, solution_hbm, all_maps, all_shifts, ahead_ref, back_ref, base, updated,
     solution, base_sems, out_sems) = refs
    cases, order = own_value_ref.shape
    comps, layers, section = labels_ref.shape
    mine = lax.axis_index("row")
    odd = (mine & 1) == 1
    group = mine // width

    base_copies = [
        pltpu.make_async_copy(base_hbm.at[:, comp], base.at[:, comp], base_sems.at[comp])
        for comp in range(comps)
    ]
    for copy in base_copies:
        copy.start()
    for hop in range(ways):
        all_maps[group ^ hop] = maps[hop][...]
        all_shifts[group ^ hop] = shifts[hop][...]

    ahead = all_shifts[0, :cases]
    ahead_ref[0] = jnp.zeros_like(ahead)
    ahead_ref[1] = ahead
    for at in range(1, ways - 1):
        ahead = dot_rows(ahead, split(all_maps[at, :order]), NT) + all_shifts[at, :cases]
        ahead_ref[at + 1] = ahead
    back = jnp.zeros_like(ahead)
    back_ref[ways - 1] = back
    for at in range(ways - 1, 0, -1):
        own = all_shifts[at, cases:] - dot_rows(ahead_ref[at], split(all_maps[at, order:]), NN)
        last = at == ways - 1
        back = own if last else own + dot_rows(back, split(all_maps[at, :order]), NN)
        back_ref[at - 1] = back
    ahead, back = ahead_ref[group], back_ref[group]

    for stride, own_maps, other_maps, own_shifts, other_shifts in levels[::-1]:
        upper = (mine & stride) != 0
        first_phi = jnp.where(upper, other_maps[:order, :], own_maps[:order, :])
        second_maps = jnp.where(upper, own_maps[...], other_maps[...])
        own, other = own_shifts[...], other_shifts[...]
        first_shift = jnp.where(upper, other[:cases], own[:cases])
        second_shift = jnp.where(upper, own[cases:], other[cases:])
        middle = dot_rows(ahead, split(first_phi), NT) + first_shift
        inner = (
            dot_rows(back, split(second_maps[:order]), NN)
            - dot_rows(middle, split(second_maps[order:]), NN)
            + second_shift
        )
        ahead = jnp.where(upper, middle, ahead)
        back = jnp.where(upper, back, inner)

    own_step, other_step = own_step_ref[...], other_step_ref[...]
    own_value, other_value = own_value_ref[...], other_value_ref[...]
    first_step = split(jnp.where(odd, other_step, own_step))
    second_step = split(jnp.where(odd, own_step, other_step))
    first = dot_rows(ahead, first_step, NT) + jnp.where(odd, other_value, own_value)
    second = dot_rows(first, second_step, NT) + jnp.where(odd, own_value, other_value)
    inner = dot_rows(back - second, second_step, NN)
    solved = dot_rows(
        jnp.where(odd, second - back, first - inner), split(inverse_ref[...]), NN
    )
    solution[...] = solved.T
    out_copies = [pltpu.make_async_copy(solution, solution_hbm, out_sems.at[comps])]
    out_copies[0].start()

    for comp in range(comps):
        base_copies[comp].wait()
        for tile in range(section // 128):
            lanes = slice(tile * 128, (tile + 1) * 128)
            label = labels_ref[comp, :, lanes]
            weight = weight_ref[comp, :, lanes]
            for case in range(cases):
                table = jnp.broadcast_to(solved[case : case + 1, :], (layers, 128))
                spread = jnp.take_along_axis(table, label, axis=1, mode="promise_in_bounds")
                updated[case, comp, :, lanes] = base[case, comp, :, lanes] + weight * spread
        copy = pltpu.make_async_copy(
            updated.at[:, comp], updated_hbm.at[:, comp], out_sems.at[comp]
        )
        copy.start()
        out_copies.append(copy)
    for copy in out_copies:
        copy.wait()


def finish_call(strides, width, maps, shifts, levels, leaf, base, labels, weight):
    cases, comps, layers, section = base.shape
    order = maps[0].shape[1]
    ways = len(maps)
    hbm, local = pl.BlockSpec(memory_space=pltpu.HBM), pl.BlockSpec(memory_space=pltpu.VMEM)
    before = (*maps, *shifts, *levels, *leaf)
    return pl.pallas_call(
        functools.partial(finish_kernel, strides, width, ways),
        in_specs=[local] * len(before) + [hbm, local, local],
        out_specs=[hbm, hbm],
        out_shape=[
            jax.ShapeDtypeStruct(base.shape, f32),
            jax.ShapeDtypeStruct((order, cases), f32),
        ],
        scratch_shapes=[
            pltpu.VMEM((ways, 2 * order, order), f32),
            pltpu.VMEM((ways, 2 * cases, order), f32),
            pltpu.VMEM((ways, cases, order), f32),
            pltpu.VMEM((ways, cases, order), f32),
            pltpu.VMEM(base.shape, f32),
            pltpu.VMEM(base.shape, f32),
            pltpu.VMEM((order, cases), f32),
            pltpu.SemaphoreType.DMA((comps,)),
            pltpu.SemaphoreType.DMA((comps + 1,)),
        ],
        compiler_params=small(10),
        name="finish",
    )(*before, base, labels, weight)


def per_device(
    displacement, loads, section_stiffness, modulus, aggregate, basis_weight, diag_inverse, sub_factor
):
    cases = displacement.shape[0]
    count = lax.axis_size("row")
    ways = 4
    width = count // ways

    def swap(value, mask):
        return lax.ppermute(value, "row", [(i, i ^ mask) for i in range(count)])

    step, near, far = start_call(diag_inverse, sub_factor, displacement)
    other_step = swap(step, 1)
    near = swap(near, 1)
    far = lax.ppermute(
        far, "row", [(i, i + 1 if i & 1 else i - 1) for i in range(1, count - 1)]
    )
    maps, mixed = maps_call(pair_maps_kernel, "pair_maps", step, other_step)
    pair_operands = (step, other_step, maps, mixed)
    strides, joins = [], []
    stride = 2
    while stride < width:
        other_maps = swap(maps, stride)
        joined, mixed = maps_call(
            functools.partial(join_maps_kernel, stride), "join_maps", maps, other_maps
        )
        strides.append(stride)
        joins.append((maps, other_maps, mixed))
        maps = joined
        stride *= 2
    all_maps = [maps] + [swap(maps, hop * width) for hop in range(1, ways)]

    base, value = residual_call(
        displacement, loads, section_stiffness, modulus, aggregate, basis_weight, near, far,
        diag_inverse,
    )
    other_value = swap(value, 1)
    shifts = shifts_call(pair_shifts_kernel, "pair_shifts", cases, value, other_value, *pair_operands)
    levels = []
    for stride, (own_maps, other_maps, mixed) in zip(strides, joins):
        other_shifts = swap(shifts, stride)
        levels += [own_maps, other_maps, shifts, other_shifts]
        shifts = shifts_call(
            functools.partial(join_shifts_kernel, stride), "join_shifts", cases,
            shifts, other_shifts, own_maps, other_maps, mixed,
        )
    all_shifts = [shifts] + [swap(shifts, hop * width) for hop in range(1, ways)]
    leaf = (step, other_step, value, other_value, diag_inverse)
    return finish_call(
        tuple(strides), width, all_maps, all_shifts, levels, leaf, base, aggregate, basis_weight
    )


def solution(mesh):
    placed = (
        P("groups", None, "row", None),
        P("groups", None, "row", None),
        P("groups", None, None),
        P("row", "groups"),
        P("groups", "row", None),
        P("groups", "row", None),
        P("row", "groups"),
        P("row", "groups"),
    )
    return jax.shard_map(
        per_device,
        mesh=mesh,
        in_specs=placed,
        out_specs=(P("groups", None, "row", None), P("row", "groups")),
        check_vma=False,
    )
```

time: 68.9 us -> 48.3 us (0.70)
  starting transfers between devices: 26.7 us -> 14.4 us
  matrix products: 8.71 us -> 0 us
  other arithmetic: 5.01 us -> 0 us
  Pallas kernels: 10.2 us -> 13.4 us
  local copies, waits for them, and re-layouts: 4.59 us -> 7.05 us
    ppermute x22 -> x12, starting transfers between devices: 26.7 us -> 14.4 us  [the longest x11 13.8 us: swap(): return lax.ppermute(value, 'row', [(i, i ^ mask) for i in range(count)])]
    dot_general x33 -> x0, matrix products: 8.71 us -> none  [matmul(): lax.dot_general(left, right, dims, precision=lax.Precision.HIGHEST, prefe...]
    select_n x6 -> x0, other arithmetic: 4.91 us -> none  [the longest x1 2.09 us: per_device(): jnp.where(odd, last_layers, first_layers)]
    pallas_call x1 -> x6, Pallas kernels: 2.55 us -> 5.4 us  [the longest x1 3.68 us: finish_call(): pl.pallas_call(functools.partial(finish_kernel, strides, width, ways), in...]
    unnamed x16 -> x20, local copies, waits for them, and re-layouts: 4.59 us -> 6.39 us
    ppermute x22 -> x12, waiting for transfers between devices: 12.3 us -> 12.4 us  [the longest x11 12.4 us: swap(): return lax.ppermute(value, 'row', [(i, i ^ mask) for i in range(count)])]
  transfers between devices with their start and end apart: 22 -> 12, of which waited for: 9 -> 7; matrix products, arithmetic and copies ran while one was open for 14% -> 0% of each run, Pallas kernels for 0% -> 18%
where the time goes in v2:
time: 48.3 us; the launch traced here: 48 us
  starting transfers between devices  14.4 us (30%)
  Pallas kernels  13.4 us (28%)
  waiting for transfers between devices  12.4 us (26%)
  local copies, waits for them, and re-layouts  7.05 us (15%)
  between operations  0.76 us (2%)
    ppermute x11, starting transfers between devices, swap(): return lax.ppermute(value, 'row', [(i, i ^ mask) for i in range(count)])  13.8 us
    ppermute x11, waiting for transfers between devices, swap(): return lax.ppermute(value, 'row', [(i, i ^ mask) for i in range(count)])  12.4 us
    pallas_call x1, Pallas kernels, residual_call(): pl.pallas_call(residual_kernel, grid=(comps,), in_specs=[wide, wide, pl.B...  7.95 us
    unnamed x20, local copies, waits for them, and re-layouts  6.39 us
    pallas_call x1, Pallas kernels, finish_call(): pl.pallas_call(functools.partial(finish_kernel, strides, width, ways), in...  3.68 us
  transfers between devices with their start and end apart: 12, of which 7 were waited for; matrix products, arithmetic and copies ran while one was open for 0% of the time, Pallas kernels for 18%

profile of v2, /device:TPU:0, one launch (start us, length us, event | category | flops | bytes accessed | tf_op | source)
XLA Modules:
  0.0 48.0 jit_solution(6135873306493166147)
XLA Ops:
  0.6 0.0 copy-start
  0.6 1.4 %copy-done = f32[8,3,32,512]{3,2,1,0:T(8,128)S(1)} copy-done((f32[8,3,32,512]{3,2,1,0:T(8,128)S(1)}, f32[8,3,32,512]{3,2,1,0:T(8,128)}, u32[]{:S(2)}) %copy-start) | copy-done | bytes 1572888
  2.0 0.0 copy-start.6
  2.0 0.8 %copy-done.6 = f32[128,128]{1,0:T(8,128)S(1)} copy-done((f32[128,128]{1,0:T(8,128)S(1)}, f32[128,128]{1,0:T(8,128)}, u32[]{:S(2)}) %copy-start.6) | copy-done | bytes 65560
  2.9 0.0 copy-start.9
  2.9 0.8 %copy-done.9 = f32[128,128]{1,0:T(8,128)S(1)} copy-done((f32[128,128]{1,0:T(8,128)S(1)}, f32[128,128]{1,0:T(8,128)}, u32[]{:S(2)}) %copy-start.9) | copy-done | bytes 65560
  3.7 0.0 copy-start.1
  3.7 0.0 copy-start.4
  3.7 0.0 copy-start.5
  3.7 0.0 copy-start.7
  3.7 0.0 copy-start.8
  3.7 0.6 %start.1 = (f32[128,128]{1,0:T(8,128)S(1)}, f32[288,128]{1,0:T(8,128)S(1)}, f32[288,128]{1,0:T(8,128)S(1)}) custom-call(f32[128,128]{1,0:T(8,128)S(1)} %copy-done.6, f32[128,128]{1,0:T(8,128)S(1)} %copy-done.9, f32[8,3,32,512]{3,2,1,0:T(8,128)S(1)} %copy-done), custom_call_target="tpu_custom_call" | custom-call | tf_op jit(solution)/shard_map/start/pallas_call | solution.py:202
  4.4 0.5 %collective-permute-start = (f32[128,128]{1,0:T(8,128)S(1)}, f32[128,128]{1,0:T(8,128)S(1)}, u32[]{:S(2)}, u32[]{:S(2)}) collective-permute-start(f32[128,128]{1,0:T(8,128)S(1)} %get-tuple-element.11.own_ref.own_step_ref.refs_12_), channel_id=1, source_target_pairs={{0,1},{1,0},{2,3},{3,2},{4,5},{5,4},{6,7},{7,6},{8,9},{9,8},{10,11... | collective-permute-start | bytes 196616 | tf_op jit(solution)/shard_map/ppermute | solution.py:419
  4.9 0.9 %collective-permute-done.other_ref.other_step_ref.refs_13_ = f32[128,128]{1,0:T(8,128)S(1)} collective-permute-done((f32[128,128]{1,0:T(8,128)S(1)}, f32[128,128]{1,0:T(8,128)S(1)}, u32[]{:S(2)}, u32[]{:S(2)}) %collective-permute-start) | collective-permute-done | bytes 65568 | tf_op jit(solution)/shard_map/ppermute | solution.py:419
  5.8 0.4 pair_maps.1
  6.2 2.9 %collective-permute-start.1 = (f32[256,128]{1,0:T(8,128)S(1)}, f32[256,128]{1,0:T(8,128)S(1)}, u32[]{:S(2)}, u32[]{:S(2)}) collective-permute-start(f32[256,128]{1,0:T(8,128)S(1)} %get-tuple-element.12.own_ref.maps_ref.own_maps_ref.refs_8_), channel_id=1, source_target_pairs={{0,2},{1,3},{2,0},{3,1},{4,6},{5,7},{6,4},{7,5},{8,10},{9,11},{10,... | collective-permute-start | bytes 393224 | tf_op jit(solution)/shard_map/ppermute | solution.py:419
  9.1 0.0 collective-permute-start.5
  9.1 0.7 %collective-permute-start.6 = (f32[288,128]{1,0:T(8,128)S(1)}, f32[288,128]{1,0:T(8,128)S(1)}, u32[]{:S(2)}, u32[]{:S(2)}) collective-permute-start(f32[288,128]{1,0:T(8,128)S(1)} %get-tuple-element.15), channel_id=1, source_target_pairs={{1,2},{2,1},{3,4},{4,3},{5,6},{6,5},{7,8},{8,7},{9,10},{10,9},{11,... | collective-permute-start | bytes 442376 | tf_op jit(solution)/shard_map/ppermute | solution.py:424
  9.8 3.1 %collective-permute-done.1.other_ref.other_maps_ref.refs_9_ = f32[256,128]{1,0:T(8,128)S(1)} collective-permute-done((f32[256,128]{1,0:T(8,128)S(1)}, f32[256,128]{1,0:T(8,128)S(1)}, u32[]{:S(2)}, u32[]{:S(2)}) %collective-permute-start.1) | collective-permute-done | bytes 131104 | tf_op jit(solution)/shard_map/ppermute | solution.py:419
  12.9 0.4 join_maps.1
  13.3 3.9 %collective-permute-start.4 = (f32[256,128]{1,0:T(8,128)S(1)}, f32[256,128]{1,0:T(8,128)S(1)}, u32[]{:S(2)}, u32[]{:S(2)}) collective-permute-start(f32[256,128]{1,0:T(8,128)S(1)} %get-tuple-element.13.refs_0_), channel_id=1, source_target_pairs={{0,12},{1,13},{2,14},{3,15},{4,8},{5,9},{6,10},{7,11},{8,4},{9,5},... | collective-permute-start | bytes 393224 | tf_op jit(solution)/shard_map/ppermute | solution.py:419
  17.2 0.0 collective-permute-start.3
  17.2 0.6 %collective-permute-start.2 = (f32[256,128]{1,0:T(8,128)S(1)}, f32[256,128]{1,0:T(8,128)S(1)}, u32[]{:S(2)}, u32[]{:S(2)}) collective-permute-start(f32[256,128]{1,0:T(8,128)S(1)} %get-tuple-element.13.refs_0_), channel_id=1, source_target_pairs={{0,4},{1,5},{2,6},{3,7},{4,0},{5,1},{6,2},{7,3},{8,12},{9,13},{10,... | collective-permute-start | bytes 393224 | tf_op jit(solution)/shard_map/ppermute | solution.py:419
  17.8 0.0 collective-permute-done.5.near_ref
  17.8 0.0 collective-permute-done.6.far_ref
  17.8 0.0 copy-done.1
  17.8 0.0 copy-done.4
  17.8 0.0 copy-done.5
  17.9 0.0 copy-done.7
  17.9 0.0 copy-done.8
  17.9 0.0 copy-start.2
  17.9 1.9 %copy-done.2 = f32[3,512,512]{2,1,0:T(8,128)S(1)} copy-done((f32[3,512,512]{2,1,0:T(8,128)S(1)}, f32[3,512,512]{2,1,0:T(8,128)}, u32[]{:S(2)}) %copy-start.2) | copy-done | bytes 3145752
  19.8 0.0 copy-start.3
  19.8 1.4 %copy-done.3 = f32[8,3,32,512]{3,2,1,0:T(8,128)S(1)} copy-done((f32[8,3,32,512]{3,2,1,0:T(8,128)S(1)}, f32[8,3,32,512]{3,2,1,0:T(8,128)}, u32[]{:S(2)}) %copy-start.3) | copy-done | bytes 1572888
  21.2 8.0 %residual.1 = (f32[8,3,32,512]{3,2,1,0:T(8,128)S(1)}, f32[8,128]{1,0:T(8,128)S(1)}) custom-call(f32[8,3,32,512]{3,2,1,0:T(8,128)S(1)} %copy-done.1, f32[8,3,32,512]{3,2,1,0:T(8,128)S(1)} %copy-done.3, f32[3,512,512]{2,1,0:T(8,128)S(1)} %copy-done.2, f32[32,512]{1,0:T(8,128)S(1)} %copy-done.8, s32[3,32,512]{2,1,0:T(8,128)S(1)} %copy-done.4, ...), custom_call_target="tpu_custom_call" | custom-call | tf_op jit(solution)/shard_map/residual/pallas_call | solution.py:134
  29.1 0.1 collective-permute-start.7
  29.2 1.2 %collective-permute-done.7.other_ref.refs_15_ = f32[8,128]{1,0:T(8,128)S(1)} collective-permute-done((f32[8,128]{1,0:T(8,128)S(1)}, f32[8,128]{1,0:T(8,128)S(1)}, u32[]{:S(2)}, u32[]{:S(2)}) %collective-permute-start.7) | collective-permute-done | bytes 4128 | tf_op jit(solution)/shard_map/ppermute | solution.py:419
  30.4 0.2 pair_shifts.1.own_ref.refs_10_
  30.6 1.9 %collective-permute-start.8 = (f32[16,128]{1,0:T(8,128)S(1)}, f32[16,128]{1,0:T(8,128)S(1)}, u32[]{:S(2)}, u32[]{:S(2)}) collective-permute-start(f32[16,128]{1,0:T(8,128)S(1)} %pair_shifts.1.own_ref.refs_10_), channel_id=1, source_target_pairs={{0,2},{1,3},{2,0},{3,1},{4,6},{5,7},{6,4},{7,5},{8,10},{9,11},{10,... | collective-permute-start | bytes 24584 | tf_op jit(solution)/shard_map/ppermute | solution.py:419
  32.5 1.8 %collective-permute-done.8.other_ref.refs_11_ = f32[16,128]{1,0:T(8,128)S(1)} collective-permute-done((f32[16,128]{1,0:T(8,128)S(1)}, f32[16,128]{1,0:T(8,128)S(1)}, u32[]{:S(2)}, u32[]{:S(2)}) %collective-permute-start.8) | collective-permute-done | bytes 8224 | tf_op jit(solution)/shard_map/ppermute | solution.py:419
  34.3 0.2 join_shifts.1.refs_4_
  34.4 3.8 %collective-permute-start.11 = (f32[16,128]{1,0:T(8,128)S(1)}, f32[16,128]{1,0:T(8,128)S(1)}, u32[]{:S(2)}, u32[]{:S(2)}) collective-permute-start(f32[16,128]{1,0:T(8,128)S(1)} %join_shifts.1.refs_4_), channel_id=1, source_target_pairs={{0,12},{1,13},{2,14},{3,15},{4,8},{5,9},{6,10},{7,11},{8,4},{9,5},... | collective-permute-start | bytes 24584 | tf_op jit(solution)/shard_map/ppermute | solution.py:419
  38.2 0.0 collective-permute-start.10
  38.2 1.7 %collective-permute-done.11.refs_7_ = f32[16,128]{1,0:T(8,128)S(1)} collective-permute-done((f32[16,128]{1,0:T(8,128)S(1)}, f32[16,128]{1,0:T(8,128)S(1)}, u32[]{:S(2)}, u32[]{:S(2)}) %collective-permute-start.11) | collective-permute-done | bytes 8224 | tf_op jit(solution)/shard_map/ppermute | solution.py:419
  39.9 0.0 collective-permute-start.9
  39.9 2.8 %collective-permute-done.10.refs_6_ = f32[16,128]{1,0:T(8,128)S(1)} collective-permute-done((f32[16,128]{1,0:T(8,128)S(1)}, f32[16,128]{1,0:T(8,128)S(1)}, u32[]{:S(2)}, u32[]{:S(2)}) %collective-permute-start.10) | collective-permute-done | bytes 8224 | tf_op jit(solution)/shard_map/ppermute | solution.py:419
  42.8 0.8 %collective-permute-done.9.refs_5_ = f32[16,128]{1,0:T(8,128)S(1)} collective-permute-done((f32[16,128]{1,0:T(8,128)S(1)}, f32[16,128]{1,0:T(8,128)S(1)}, u32[]{:S(2)}, u32[]{:S(2)}) %collective-permute-start.9) | collective-permute-done | bytes 8224 | tf_op jit(solution)/shard_map/ppermute | solution.py:419
  43.6 0.0 collective-permute-done.4.refs_3_
  43.6 0.0 collective-permute-done.3.refs_2_
  43.6 0.0 collective-permute-done.2.refs_1_
  43.6 3.7 %finish.1 = (f32[8,3,32,512]{3,2,1,0:T(8,128)}, f32[128,8]{1,0:T(8,128)S(1)}) custom-call(f32[256,128]{1,0:T(8,128)S(1)} %get-tuple-element.13.refs_0_, f32[256,128]{1,0:T(8,128)S(1)} %collective-permute-done.2.refs_1_, f32[256,128]{1,0:T(8,128)S(1)} %collective-permute-done.3.refs_2_, f32[256,128]{1,0:T(8,128)S(1)} %collective-permute-done.4.refs_3_, ...), custom_call_target="tpu_custom_call" | custom-call | tf_op jit(solution)/shard_map/finish/pallas_call | solution.py:386
  47.3 0.7 %copy.10 = f32[128,8]{0,1:T(8,128)} copy(f32[128,8]{1,0:T(8,128)S(1)} %get-tuple-element.21) | data formatting | bytes 8192 | tf_op jit(solution)/shard_map/finish/pallas_call | solution.py:386
Async XLA Ops:
  0.6 1.4 %copy-start = (f32[8,3,32,512]{3,2,1,0:T(8,128)S(1)}, f32[8,3,32,512]{3,2,1,0:T(8,128)}, u32[]{:S(2)}) copy-start(f32[8,3,32,512]{3,2,1,0:T(8,128)} %disp_ref.1) | copy-start | bytes 4718596
  2.0 0.8 %copy-start.6 = (f32[128,128]{1,0:T(8,128)S(1)}, f32[128,128]{1,0:T(8,128)}, u32[]{:S(2)}) copy-start(f32[128,128]{1,0:T(8,128)} %refs_16_.1) | copy-start | bytes 196612
  2.9 0.8 %copy-start.9 = (f32[128,128]{1,0:T(8,128)S(1)}, f32[128,128]{1,0:T(8,128)}, u32[]{:S(2)}) copy-start(f32[128,128]{1,0:T(8,128)} %sub_hbm.1) | copy-start | bytes 196612
  3.7 14.1 %copy-start.1 = (f32[8,3,32,512]{3,2,1,0:T(8,128)S(1)}, f32[8,3,32,512]{3,2,1,0:T(8,128)}, u32[]{:S(2)}) copy-start(f32[8,3,32,512]{3,2,1,0:T(8,128)} %disp_ref.1) | copy-start | bytes 4718596
  3.7 14.1 %copy-start.4 = (s32[3,32,512]{2,1,0:T(8,128)S(1)}, s32[3,32,512]{2,1,0:T(8,128)}, u32[]{:S(2)}) copy-start(s32[3,32,512]{2,1,0:T(8,128)} %refs_18_.1) | copy-start | bytes 589828
  3.7 14.1 %copy-start.5 = (f32[3,32,512]{2,1,0:T(8,128)S(1)}, f32[3,32,512]{2,1,0:T(8,128)}, u32[]{:S(2)}) copy-start(f32[3,32,512]{2,1,0:T(8,128)} %refs_19_.1) | copy-start | bytes 589828
  3.7 14.1 %copy-start.7 = (f32[128,128]{1,0:T(8,128)S(1)}, f32[128,128]{1,0:T(8,128)}, u32[]{:S(2)}) copy-start(f32[128,128]{1,0:T(8,128)} %refs_16_.1) | copy-start | bytes 196612
  3.7 14.1 %copy-start.8 = (f32[32,512]{1,0:T(8,128)S(1)}, f32[32,512]{1,0:T(8,128)}, u32[]{:S(2)}) copy-start(f32[32,512]{1,0:T(8,128)} %modulus_ref.1) | copy-start | bytes 196612
  4.4 1.4 %collective-permute-start = (f32[128,128]{1,0:T(8,128)S(1)}, f32[128,128]{1,0:T(8,128)S(1)}, u32[]{:S(2)}, u32[]{:S(2)}) collective-permute-start(f32[128,128]{1,0:T(8,128)S(1)} %get-tuple-element.11.own_ref.own_step_ref.refs_12_), channel_id=1, source_target_pairs={{0,1},{1,0},{2,3},{3,2},{4,5},{5,4},{6,7},{7,6},{8,9},{9,8},{10,11... | collective-permute-start | bytes 196616 | tf_op jit(solution)/shard_map/ppermute | solution.py:419
  6.2 6.7 %collective-permute-start.1 = (f32[256,128]{1,0:T(8,128)S(1)}, f32[256,128]{1,0:T(8,128)S(1)}, u32[]{:S(2)}, u32[]{:S(2)}) collective-permute-start(f32[256,128]{1,0:T(8,128)S(1)} %get-tuple-element.12.own_ref.maps_ref.own_maps_ref.refs_8_), channel_id=1, source_target_pairs={{0,2},{1,3},{2,0},{3,1},{4,6},{5,7},{6,4},{7,5},{8,10},{9,11},{10,... | collective-permute-start | bytes 393224 | tf_op jit(solution)/shard_map/ppermute | solution.py:419
  9.1 8.7 %collective-permute-start.5 = (f32[288,128]{1,0:T(8,128)S(1)}, f32[288,128]{1,0:T(8,128)S(1)}, u32[]{:S(2)}, u32[]{:S(2)}) collective-permute-start(f32[288,128]{1,0:T(8,128)S(1)} %get-tuple-element.14), channel_id=1, source_target_pairs={{0,1},{1,0},{2,3},{3,2},{4,5},{5,4},{6,7},{7,6},{8,9},{9,8},{10,11... | collective-permute-start | bytes 442376 | tf_op jit(solution)/shard_map/ppermute | solution.py:419
  9.1 8.7 %collective-permute-start.6 = (f32[288,128]{1,0:T(8,128)S(1)}, f32[288,128]{1,0:T(8,128)S(1)}, u32[]{:S(2)}, u32[]{:S(2)}) collective-permute-start(f32[288,128]{1,0:T(8,128)S(1)} %get-tuple-element.15), channel_id=1, source_target_pairs={{1,2},{2,1},{3,4},{4,3},{5,6},{6,5},{7,8},{8,7},{9,10},{10,9},{11,... | collective-permute-start | bytes 442376 | tf_op jit(solution)/shard_map/ppermute | solution.py:424
  13.3 30.3 %collective-permute-start.4 = (f32[256,128]{1,0:T(8,128)S(1)}, f32[256,128]{1,0:T(8,128)S(1)}, u32[]{:S(2)}, u32[]{:S(2)}) collective-permute-start(f32[256,128]{1,0:T(8,128)S(1)} %get-tuple-element.13.refs_0_), channel_id=1, source_target_pairs={{0,12},{1,13},{2,14},{3,15},{4,8},{5,9},{6,10},{7,11},{8,4},{9,5},... | collective-permute-start | bytes 393224 | tf_op jit(solution)/shard_map/ppermute | solution.py:419
  17.2 26.4 %collective-permute-start.3 = (f32[256,128]{1,0:T(8,128)S(1)}, f32[256,128]{1,0:T(8,128)S(1)}, u32[]{:S(2)}, u32[]{:S(2)}) collective-permute-start(f32[256,128]{1,0:T(8,128)S(1)} %get-tuple-element.13.refs_0_), channel_id=1, source_target_pairs={{0,8},{1,9},{2,10},{3,11},{4,12},{5,13},{6,14},{7,15},{8,0},{9,1},... | collective-permute-start | bytes 393224 | tf_op jit(solution)/shard_map/ppermute | solution.py:419
  17.2 26.4 %collective-permute-start.2 = (f32[256,128]{1,0:T(8,128)S(1)}, f32[256,128]{1,0:T(8,128)S(1)}, u32[]{:S(2)}, u32[]{:S(2)}) collective-permute-start(f32[256,128]{1,0:T(8,128)S(1)} %get-tuple-element.13.refs_0_), channel_id=1, source_target_pairs={{0,4},{1,5},{2,6},{3,7},{4,0},{5,1},{6,2},{7,3},{8,12},{9,13},{10,... | collective-permute-start | bytes 393224 | tf_op jit(solution)/shard_map/ppermute | solution.py:419
  17.9 1.9 %copy-start.2 = (f32[3,512,512]{2,1,0:T(8,128)S(1)}, f32[3,512,512]{2,1,0:T(8,128)}, u32[]{:S(2)}) copy-start(f32[3,512,512]{2,1,0:T(8,128)} %section_ref.1) | copy-start | bytes 9437188
  19.8 1.4 %copy-start.3 = (f32[8,3,32,512]{3,2,1,0:T(8,128)S(1)}, f32[8,3,32,512]{3,2,1,0:T(8,128)}, u32[]{:S(2)}) copy-start(f32[8,3,32,512]{3,2,1,0:T(8,128)} %loads_ref.1) | copy-start | bytes 4718596
  29.1 1.2 %collective-permute-start.7 = (f32[8,128]{1,0:T(8,128)S(1)}, f32[8,128]{1,0:T(8,128)S(1)}, u32[]{:S(2)}, u32[]{:S(2)}) collective-permute-start(f32[8,128]{1,0:T(8,128)S(1)} %get-tuple-element.16.own_ref.refs_14_), channel_id=1, source_target_pairs={{0,1},{1,0},{2,3},{3,2},{4,5},{5,4},{6,7},{7,6},{8,9},{9,8},{10,11... | collective-permute-start | bytes 12296 | tf_op jit(solution)/shard_map/ppermute | solution.py:419
  30.6 3.7 %collective-permute-start.8 = (f32[16,128]{1,0:T(8,128)S(1)}, f32[16,128]{1,0:T(8,128)S(1)}, u32[]{:S(2)}, u32[]{:S(2)}) collective-permute-start(f32[16,128]{1,0:T(8,128)S(1)} %pair_shifts.1.own_ref.refs_10_), channel_id=1, source_target_pairs={{0,2},{1,3},{2,0},{3,1},{4,6},{5,7},{6,4},{7,5},{8,10},{9,11},{10,... | collective-permute-start | bytes 24584 | tf_op jit(solution)/shard_map/ppermute | solution.py:419
  34.4 5.5 %collective-permute-start.11 = (f32[16,128]{1,0:T(8,128)S(1)}, f32[16,128]{1,0:T(8,128)S(1)}, u32[]{:S(2)}, u32[]{:S(2)}) collective-permute-start(f32[16,128]{1,0:T(8,128)S(1)} %join_shifts.1.refs_4_), channel_id=1, source_target_pairs={{0,12},{1,13},{2,14},{3,15},{4,8},{5,9},{6,10},{7,11},{8,4},{9,5},... | collective-permute-start | bytes 24584 | tf_op jit(solution)/shard_map/ppermute | solution.py:419
  38.2 4.5 %collective-permute-start.10 = (f32[16,128]{1,0:T(8,128)S(1)}, f32[16,128]{1,0:T(8,128)S(1)}, u32[]{:S(2)}, u32[]{:S(2)}) collective-permute-start(f32[16,128]{1,0:T(8,128)S(1)} %join_shifts.1.refs_4_), channel_id=1, source_target_pairs={{0,8},{1,9},{2,10},{3,11},{4,12},{5,13},{6,14},{7,15},{8,0},{9,1},... | collective-permute-start | bytes 24584 | tf_op jit(solution)/shard_map/ppermute | solution.py:419
  39.9 3.7 %collective-permute-start.9 = (f32[16,128]{1,0:T(8,128)S(1)}, f32[16,128]{1,0:T(8,128)S(1)}, u32[]{:S(2)}, u32[]{:S(2)}) collective-permute-start(f32[16,128]{1,0:T(8,128)S(1)} %join_shifts.1.refs_4_), channel_id=1, source_target_pairs={{0,4},{1,5},{2,6},{3,7},{4,0},{5,1},{6,2},{7,3},{8,12},{9,13},{10,... | collective-permute-start | bytes 24584 | tf_op jit(solution)/shard_map/ppermute | solution.py:419

commit v3 on v2

v3 whole, which is shorter than its diff:
```python
import functools

import jax
import jax.numpy as jnp
from jax import lax
from jax.experimental import pallas as pl
from jax.experimental.pallas import tpu as pltpu
from jax.sharding import PartitionSpec as P

span_weights = (1.5, -0.15, 1.0 / 90.0)
bf16, f32 = jnp.bfloat16, jnp.float32
NN = (((1,), (0,)), ((), ()))
NT = (((1,), (1,)), ((), ()))
TN = (((0,), (0,)), ((), ()))


def split(value):
    high = value.astype(bf16)
    return high, (value - high.astype(f32)).astype(bf16)


def dot(left, right, dims):
    return lax.dot_general(left, right, dims, preferred_element_type=f32)


def dot3(left, right, dims):
    left_high, left_low = left
    right_high, right_low = right
    return dot(left_high, right_high, dims) + (
        dot(left_high, right_low, dims) + dot(left_low, right_high, dims)
    )


def dot_rows(rows, weights, dims):
    high, low = split(rows)
    weight_high, weight_low = weights
    count = rows.shape[0]
    both = dot(jnp.concatenate([high, low], axis=0), weight_high, dims)
    return both[:count] + both[count:] + dot(high, weight_low, dims)


def node_rows(edge, layers):
    return (0, layers - 8) if edge else tuple(range(8, layers - 8, 8))


def residual_part(
    edge, disp_ref, loads_ref, modulus_ref, labels_ref, weight_ref, across_ref, diagonal_of, padded,
    weighted, base_ref, comp, total,
):
    cases, comps, layers, section = disp_ref.shape
    tiles = section // 128
    groups = node_rows(edge, layers)
    depth = 8 * len(groups)
    stride = weighted.shape[1] // cases
    fine = total.shape[1]
    parts = total.shape[0] // (2 * cases)
    bins = lax.broadcasted_iota(jnp.int32, (fine, 128), 0).astype(f32).astype(bf16)
    for at, first in enumerate(groups):
        rows = slice(first, first + 8)
        out = slice(at * 8, at * 8 + 8)
        for tile in range(tiles):
            lanes = slice(tile * 128, (tile + 1) * 128)
            modulus = modulus_ref[rows, lanes]
            diagonal = diagonal_of(comp, lanes)
            inverse = 1.0 / (modulus * (2.0 * sum(span_weights)) + diagonal)
            weight = weight_ref[comp, rows, lanes]
            for case in range(cases):
                own = padded[comp, case, tile, 8 + first : 16 + first, :]
                span_sum = (2.0 * sum(span_weights)) * own
                for offset in range(1, 4):
                    low = padded[comp, case, tile, 8 + first - offset : 16 + first - offset, :]
                    high = padded[comp, case, tile, 8 + first + offset : 16 + first + offset, :]
                    span_sum = span_sum - span_weights[offset - 1] * (low + high)
                residual = loads_ref[case, comp, rows, lanes] - (
                    modulus * span_sum + across_ref[comp, case, out, lanes]
                )
                base_ref[case, comp, out, lanes] = own + residual * inverse
                start = case * stride + tile * depth + at * 8
                weighted[comp, start : start + 8, :] = weight * residual

    def restrict(group, total):
        at = pl.multiple_of(group * 8, 8)
        first = pl.multiple_of(groups[0] + group * (groups[1] - groups[0]), 8)
        block = labels_ref[comp, pl.ds(first, 8), :]
        big = lax.shift_right_logical(block, fine.bit_length() - 1).astype(f32)
        little = (block & (fine - 1)).astype(f32)
        for inner in range(8):
            onehots, values = [], []
            for tile in range(tiles):
                lanes = slice(tile * 128, (tile + 1) * 128)
                low = jnp.broadcast_to(little[inner : inner + 1, lanes], (16, 128)).astype(bf16)
                low = jnp.concatenate([low] * (fine // 16), axis=0)
                onehots.append(jnp.where(low == bins, bf16(1), bf16(0)))
                high = jnp.broadcast_to(big[inner : inner + 1, lanes], (16, 128)).astype(bf16)
                value = weighted[comp, pl.ds(tile * depth + at + inner, cases, stride=stride), :]
                value = jnp.concatenate(split(value), axis=0)
                values.append(
                    jnp.concatenate(
                        [jnp.where(high == bf16(part), value, bf16(0)) for part in range(parts)],
                        axis=0,
                    )
                )
            total = total + dot(
                jnp.concatenate(values, axis=1), jnp.concatenate(onehots, axis=1), NT
            )
        return total

    return lax.fori_loop(0, len(groups), restrict, total)


def inner_kernel(
    disp_ref, loads_ref, section_ref, modulus_ref, labels_ref, weight_ref,
    base_ref, outer_ref, diagonal_ref, total_ref, padded, weighted, across_ref,
):
    cases, comps, layers, section = disp_ref.shape
    tiles = section // 128
    same = lax.broadcasted_iota(jnp.int32, (128, 128), 0) == lax.broadcasted_iota(
        jnp.int32, (128, 128), 1
    )
    total = jnp.zeros(total_ref.shape, f32)
    for comp in range(comps):
        for tile in range(tiles):
            lanes = slice(tile * 128, (tile + 1) * 128)
            padded[comp, :, tile, 8 : 8 + layers, :] = disp_ref[:, comp, :, lanes]
        high, low = split(disp_ref[:, comp].reshape(cases * layers, section))
        section_high, section_low = split(section_ref[comp])
        across = dot(
            jnp.concatenate([high, high, low], axis=1),
            jnp.concatenate([section_high, section_low, section_high], axis=0),
            NN,
        ).reshape(cases, layers, section)
        across_ref[comp] = across[:, 8 : layers - 8]
        outer_ref[comp, :, :8] = across[:, :8]
        outer_ref[comp, :, 8:] = across[:, layers - 8 :]
        diagonals = []
        for tile in range(tiles):
            lanes = slice(tile * 128, (tile + 1) * 128)
            block = section_ref[comp, lanes, lanes]
            diagonals.append(jnp.sum(jnp.where(same, block, 0.0), axis=0, keepdims=True))
            diagonal_ref[comp, :, lanes] = jnp.broadcast_to(diagonals[-1], (8, 128))
        total = residual_part(
            False, disp_ref, loads_ref, modulus_ref, labels_ref, weight_ref, across_ref,
            lambda _, lanes: diagonals[lanes.start // 128], padded, weighted, base_ref, comp, total,
        )
    total_ref[...] = total


def outer_kernel(
    disp_ref, loads_ref, modulus_ref, labels_ref, weight_ref, inverse_ref, near_ref, far_ref,
    across_ref, diagonal_ref, inner_total_ref, base_ref, value_ref, padded, weighted,
):
    cases, comps, layers, section = disp_ref.shape
    mine = lax.axis_index("row")
    odd = (mine & 1) == 1
    lowest, highest = mine == 0, mine == lax.axis_size("row") - 1
    tiles = section // 128
    total = inner_total_ref[...]
    for comp in range(comps):
        for tile in range(tiles):
            lanes = slice(tile * 128, (tile + 1) * 128)
            padded[comp, :, tile, 8:24, :] = disp_ref[:, comp, :16, lanes]
            padded[comp, :, tile, layers - 8 : layers + 8, :] = disp_ref[
                :, comp, layers - 16 :, lanes
            ]
            for row in range(3):
                at = (tile * 3 + row) * cases * comps + comp * cases
                near, far = near_ref[at : at + cases, :], far_ref[at : at + cases, :]
                below = jnp.where(lowest, 0.0, jnp.where(odd, near, far))
                above = jnp.where(highest, 0.0, jnp.where(odd, far, near))
                for case in range(cases):
                    padded[comp, case, tile, 5 + row : 6 + row, :] = below[case : case + 1]
                    low = 8 + layers + row
                    padded[comp, case, tile, low : low + 1, :] = above[case : case + 1]
        total = residual_part(
            True, disp_ref, loads_ref, modulus_ref, labels_ref, weight_ref, across_ref,
            lambda comp, lanes: diagonal_ref[comp, :, lanes], padded, weighted, base_ref, comp,
            total,
        )
    sums = []
    for at in range(0, total.shape[0], 2 * cases):
        sums.append(total[at : at + cases] + total[at + cases : at + 2 * cases])
    value_ref[...] = dot_rows(jnp.concatenate(sums, axis=1), split(inverse_ref[...]), NT)


def residual_call(kernel, edge, out_shape, scratch_shapes, *operands):
    cases, comps, layers, section = operands[0].shape
    tiles = section // 128
    depth = 8 * len(node_rows(edge, layers))
    local = pl.BlockSpec(memory_space=pltpu.VMEM)
    return pl.pallas_call(
        kernel,
        in_specs=[local] * len(operands),
        out_specs=[local] * len(out_shape),
        out_shape=[jax.ShapeDtypeStruct(shape, f32) for shape in out_shape],
        scratch_shapes=[
            pltpu.VMEM((comps, cases, tiles, layers + 16, 128), f32),
            pltpu.VMEM((comps, cases * (tiles * depth + 8), 128), f32),
            *scratch_shapes,
        ],
        compiler_params=pltpu.CompilerParams(vmem_limit_bytes=14 << 20),
        cost_estimate=pl.CostEstimate(
            flops=3 * cases * comps * layers * section * section,
            bytes_accessed=8 * operands[0].size,
            transcendentals=0,
        ),
        name="outer_residual" if edge else "inner_residual",
    )(*operands)


def small(limit):
    return pltpu.CompilerParams(vmem_limit_bytes=limit << 20)


def in_hbm(*values):
    return [pltpu.with_memory_space_constraint(value, pltpu.HBM) for value in values]


def start_kernel(
    inverse_hbm, sub_hbm, disp_hbm, step_ref, near_ref, far_ref, inverse, sub, first, last, sems
):
    cases, comps, rows, section = first.shape
    layers = disp_hbm.shape[2]
    copies = [
        pltpu.make_async_copy(inverse_hbm, inverse, sems.at[0]),
        pltpu.make_async_copy(sub_hbm, sub, sems.at[1]),
        pltpu.make_async_copy(disp_hbm.at[:, :, pl.ds(0, rows), :], first, sems.at[2]),
        pltpu.make_async_copy(disp_hbm.at[:, :, pl.ds(layers - rows, rows), :], last, sems.at[3]),
    ]
    for copy in copies:
        copy.start()
    odd = (lax.axis_index("row") & 1) == 1
    copies[0].wait()
    copies[1].wait()
    step_ref[...] = -dot3(split(inverse[...]), split(sub[...]), NN)
    copies[2].wait()
    copies[3].wait()
    for tile in range(section // 128):
        lanes = slice(tile * 128, (tile + 1) * 128)
        for row in range(3):
            for comp in range(comps):
                at = (tile * 3 + row) * cases * comps + comp * cases
                low = first[:, comp, row, lanes]
                high = last[:, comp, rows - 3 + row, lanes]
                near_ref[at : at + cases, :] = jnp.where(odd, low, high)
                far_ref[at : at + cases, :] = jnp.where(odd, high, low)


def start_call(diag_inverse, sub_factor, displacement):
    cases, comps, layers, section = displacement.shape
    packed = jax.ShapeDtypeStruct((cases * comps * 3 * section // 128, 128), f32)
    block = pltpu.VMEM((cases, comps, 8, section), f32)
    square = pltpu.VMEM(diag_inverse.shape, f32)
    return pl.pallas_call(
        start_kernel,
        in_specs=[pl.BlockSpec(memory_space=pltpu.HBM)] * 3,
        out_specs=[pl.BlockSpec(memory_space=pltpu.VMEM)] * 3,
        out_shape=[jax.ShapeDtypeStruct(diag_inverse.shape, f32), packed, packed],
        scratch_shapes=[square, square, block, block, pltpu.SemaphoreType.DMA((4,))],
        compiler_params=small(4),
        cost_estimate=pl.CostEstimate(flops=10**10, bytes_accessed=10**6, transcendentals=0),
        name="start",
    )(*in_hbm(diag_inverse, sub_factor, displacement))


def pair_maps_kernel(own_ref, other_ref, maps_ref, mixed_ref):
    order = own_ref.shape[0]
    odd = (lax.axis_index("row") & 1) == 1
    own, other = own_ref[...], other_ref[...]
    first = jnp.where(odd, other, own)
    first_split, second_split = split(first), split(jnp.where(odd, own, other))
    phi = dot3(second_split, first_split, NN)
    phi_split = split(phi)
    gram = dot3(first_split, first_split, TN) + dot3(phi_split, phi_split, TN)
    maps_ref[:order, :] = phi
    maps_ref[order:, :] = gram
    mixed_ref[...] = first + dot3(second_split, phi_split, TN)


def join_maps_kernel(stride, own_ref, other_ref, maps_ref, mixed_ref, half_ref):
    order = own_ref.shape[1]
    upper = (lax.axis_index("row") & stride) != 0
    own, other = own_ref[...], other_ref[...]
    first, second = jnp.where(upper, other, own), jnp.where(upper, own, other)
    first_phi = split(first[:order])
    mixed = dot3(split(second[order:]), first_phi, NN)
    phi = dot3(split(second[:order]), first_phi, NN)
    gram = first[order:] + dot3(first_phi, split(mixed), TN)
    maps_ref[:order, :] = phi
    maps_ref[order:, :] = gram
    mixed_ref[...] = mixed
    odd = (lax.axis_index("row") & 1) == 1
    half_ref[...] = jnp.where(odd, gram, phi)


def maps_call(kernel, name, extra, own, other):
    order = own.shape[1]
    return pl.pallas_call(
        kernel,
        out_shape=[
            jax.ShapeDtypeStruct((2 * order, order), f32),
        ]
        + [jax.ShapeDtypeStruct((order, order), f32)] * extra,
        compiler_params=small(3),
        cost_estimate=pl.CostEstimate(flops=10**10, bytes_accessed=10**6, transcendentals=0),
        name=name,
    )(own, other)


def pair_shifts_kernel(own_ref, other_ref, own_step_ref, other_step_ref, maps_ref, mixed_ref, out_ref):
    cases, order = own_ref.shape
    odd = (lax.axis_index("row") & 1) == 1
    own, other = own_ref[...], other_ref[...]
    first, second = jnp.where(odd, other, own), jnp.where(odd, own, other)
    second_step = jnp.where(odd, own_step_ref[...], other_step_ref[...])
    out_ref[:cases, :] = dot_rows(first, split(second_step), NT) + second
    out_ref[cases:, :] = -(
        dot_rows(first, split(mixed_ref[...]), NN)
        + dot_rows(second, split(maps_ref[:order, :]), NN)
    )


def join_shifts_kernel(stride, own_ref, other_ref, own_maps_ref, other_maps_ref, mixed_ref, out_ref):
    order = mixed_ref.shape[0]
    cases = own_ref.shape[0] // 2
    upper = (lax.axis_index("row") & stride) != 0
    own, other = own_ref[...], other_ref[...]
    first, second = jnp.where(upper, other, own), jnp.where(upper, own, other)
    own_phi, other_phi = own_maps_ref[:order, :], other_maps_ref[:order, :]
    first_phi = jnp.where(upper, other_phi, own_phi)
    second_phi = jnp.where(upper, own_phi, other_phi)
    out_ref[:cases, :] = dot_rows(first[:cases], split(second_phi), NT) + second[:cases]
    out_ref[cases:, :] = (
        first[cases:]
        + dot_rows(second[cases:], split(first_phi), NN)
        - dot_rows(first[:cases], split(mixed_ref[...]), NN)
    )


def shifts_call(kernel, name, cases, *operands):
    return pl.pallas_call(
        kernel,
        out_shape=jax.ShapeDtypeStruct((2 * cases, operands[0].shape[1]), f32),
        compiler_params=small(3),
        name=name,
    )(*operands)


def finish_kernel(strides, width, ways, *refs):
    own_maps_ref, halves, refs = refs[0], refs[1 : 2 * ways - 1], refs[2 * ways - 1 :]
    shifts, refs = refs[:ways], refs[ways:]
    levels = []
    for stride in strides:
        levels.append((stride, *refs[:4]))
        refs = refs[4:]
    (own_step_ref, other_step_ref, own_value_ref, other_value_ref, inverse_ref, inner_base, outer_base,
     labels_ref,
     weight_ref, updated_hbm, solution_hbm, all_maps, all_shifts, ahead_ref, back_ref, updated,
     solution, out_sems) = refs
    cases, order = own_value_ref.shape
    comps, layers, section = labels_ref.shape
    mine = lax.axis_index("row")
    odd = (mine & 1) == 1
    group = mine // width

    all_maps[group] = own_maps_ref[...]
    for hop in range(1, ways):
        got, swapped = halves[2 * hop - 2][...], halves[2 * hop - 1][...]
        all_maps[group ^ hop, :order] = jnp.where(odd, swapped, got)
        all_maps[group ^ hop, order:] = jnp.where(odd, got, swapped)
    for hop in range(ways):
        all_shifts[group ^ hop] = shifts[hop][...]

    ahead = all_shifts[0, :cases]
    ahead_ref[0] = jnp.zeros_like(ahead)
    ahead_ref[1] = ahead
    for at in range(1, ways - 1):
        ahead = dot_rows(ahead, split(all_maps[at, :order]), NT) + all_shifts[at, :cases]
        ahead_ref[at + 1] = ahead
    back = jnp.zeros_like(ahead)
    back_ref[ways - 1] = back
    for at in range(ways - 1, 0, -1):
        own = all_shifts[at, cases:] - dot_rows(ahead_ref[at], split(all_maps[at, order:]), NN)
        last = at == ways - 1
        back = own if last else own + dot_rows(back, split(all_maps[at, :order]), NN)
        back_ref[at - 1] = back
    ahead, back = ahead_ref[group], back_ref[group]

    for stride, own_maps, other_maps, own_shifts, other_shifts in levels[::-1]:
        upper = (mine & stride) != 0
        first_phi = jnp.where(upper, other_maps[:order, :], own_maps[:order, :])
        second_maps = jnp.where(upper, own_maps[...], other_maps[...])
        own, other = own_shifts[...], other_shifts[...]
        first_shift = jnp.where(upper, other[:cases], own[:cases])
        second_shift = jnp.where(upper, own[cases:], other[cases:])
        middle = dot_rows(ahead, split(first_phi), NT) + first_shift
        inner = (
            dot_rows(back, split(second_maps[:order]), NN)
            - dot_rows(middle, split(second_maps[order:]), NN)
            + second_shift
        )
        ahead = jnp.where(upper, middle, ahead)
        back = jnp.where(upper, back, inner)

    own_step, other_step = own_step_ref[...], other_step_ref[...]
    own_value, other_value = own_value_ref[...], other_value_ref[...]
    first_step = split(jnp.where(odd, other_step, own_step))
    second_step = split(jnp.where(odd, own_step, other_step))
    first = dot_rows(ahead, first_step, NT) + jnp.where(odd, other_value, own_value)
    second = dot_rows(first, second_step, NT) + jnp.where(odd, own_value, other_value)
    inner = dot_rows(back - second, second_step, NN)
    solved = dot_rows(
        jnp.where(odd, second - back, first - inner), split(inverse_ref[...]), NN
    )
    solution[...] = solved
    out_copies = [pltpu.make_async_copy(solution, solution_hbm, out_sems.at[comps])]
    out_copies[0].start()

    for comp in range(comps):
        for tile in range(section // 128):
            lanes = slice(tile * 128, (tile + 1) * 128)
            label = labels_ref[comp, :, lanes]
            weight = weight_ref[comp, :, lanes]
            for case in range(cases):
                table = jnp.broadcast_to(solved[case : case + 1, :], (layers, 128))
                spread = jnp.take_along_axis(table, label, axis=1, mode="promise_in_bounds")
                correction = weight * spread
                middle = slice(8, layers - 8)
                updated[case, comp, middle, lanes] = (
                    inner_base[case, comp, :, lanes] + correction[8 : layers - 8]
                )
                updated[case, comp, :8, lanes] = outer_base[case, comp, :8, lanes] + correction[:8]
                updated[case, comp, layers - 8 :, lanes] = (
                    outer_base[case, comp, 8:, lanes] + correction[layers - 8 :]
                )
        copy = pltpu.make_async_copy(
            updated.at[:, comp], updated_hbm.at[:, comp], out_sems.at[comp]
        )
        copy.start()
        out_copies.append(copy)
    for copy in out_copies:
        copy.wait()


def finish_call(strides, width, maps, shifts, levels, leaf, inner, outer, labels, weight):
    cases, comps, _, section = inner.shape
    layers = labels.shape[1]
    whole = (cases, comps, layers, section)
    order = maps[0].shape[1]
    ways = len(shifts)
    hbm, local = pl.BlockSpec(memory_space=pltpu.HBM), pl.BlockSpec(memory_space=pltpu.VMEM)
    before = (*maps, *shifts, *levels, *leaf)
    return pl.pallas_call(
        functools.partial(finish_kernel, strides, width, ways),
        in_specs=[local] * (len(before) + 4),
        out_specs=[hbm, hbm],
        out_shape=[
            jax.ShapeDtypeStruct(whole, f32),
            jax.ShapeDtypeStruct((cases, order), f32),
        ],
        scratch_shapes=[
            pltpu.VMEM((ways, 2 * order, order), f32),
            pltpu.VMEM((ways, 2 * cases, order), f32),
            pltpu.VMEM((ways, cases, order), f32),
            pltpu.VMEM((ways, cases, order), f32),
            pltpu.VMEM(whole, f32),
            pltpu.VMEM((cases, order), f32),
            pltpu.SemaphoreType.DMA((comps + 1,)),
        ],
        compiler_params=small(10),
        name="finish",
    )(*before, inner, outer, labels, weight)


def per_device(
    displacement, loads, section_stiffness, modulus, aggregate, basis_weight, diag_inverse, sub_factor
):
    count = lax.axis_size("row")
    ways = 4
    width = count // ways

    def swap(value, mask):
        return lax.ppermute(value, "row", [(i, i ^ mask) for i in range(count)])

    step, near, far = start_call(diag_inverse, sub_factor, displacement)
    other_step = swap(step, 1)
    near = swap(near, 1)
    far = lax.ppermute(
        far, "row", [(i, i + 1 if i & 1 else i - 1) for i in range(1, count - 1)]
    )
    cases, comps, layers, section = displacement.shape
    order = diag_inverse.shape[0]
    outer = (comps, cases, 16, section)
    node_values = (modulus, aggregate, basis_weight)
    inner_base, outer_across, diagonal, total = residual_call(
        inner_kernel,
        False,
        [
            (cases, comps, layers - 16, section),
            outer,
            (comps, 8, section),
            (4 * cases, order // 2),
        ],
        [pltpu.VMEM((comps, cases, layers - 16, section), f32)],
        displacement, loads, section_stiffness, *node_values,
    )
    maps, mixed = maps_call(pair_maps_kernel, "pair_maps", 1, step, other_step)
    pair_operands = (step, other_step, maps, mixed)
    strides, joins = [], []
    stride = 2
    while stride < width:
        other_maps = swap(maps, stride)
        if not strides:
            other_maps, total = lax.optimization_barrier((other_maps, total))
        joined, mixed, half = maps_call(
            functools.partial(join_maps_kernel, stride), "join_maps", 2, maps, other_maps
        )
        strides.append(stride)
        joins.append((maps, other_maps, mixed))
        maps = joined
        stride *= 2
    halves = [swap(half, hop * width) for hop in range(1, ways)]
    outer_base, value = residual_call(
        outer_kernel,
        True,
        [(cases, comps, 16, section), (cases, order)],
        [],
        displacement, loads, *node_values, diag_inverse, near, far, outer_across, diagonal, total,
    )
    other_value = swap(value, 1)
    shifts = shifts_call(pair_shifts_kernel, "pair_shifts", cases, value, other_value, *pair_operands)
    levels = []
    for stride, (own_maps, other_maps, mixed) in zip(strides, joins):
        other_shifts = swap(shifts, stride)
        levels += [own_maps, other_maps, shifts, other_shifts]
        shifts = shifts_call(
            functools.partial(join_shifts_kernel, stride), "join_shifts", cases,
            shifts, other_shifts, own_maps, other_maps, mixed,
        )
    shifts, *halves = lax.optimization_barrier((shifts, *halves))
    all_maps = [maps]
    for half in halves:
        all_maps += [half, swap(half, 1)]
    all_shifts = [shifts] + [swap(shifts, hop * width) for hop in range(1, ways)]
    leaf = (step, other_step, value, other_value, diag_inverse)
    updated, solution_rows = finish_call(
        tuple(strides), width, all_maps, all_shifts, levels, leaf, inner_base, outer_base, aggregate,
        basis_weight,
    )
    return updated, solution_rows.T


def solution(mesh):
    placed = (
        P("groups", None, "row", None),
        P("groups", None, "row", None),
        P("groups", None, None),
        P("row", "groups"),
        P("groups", "row", None),
        P("groups", "row", None),
        P("row", "groups"),
        P("row", "groups"),
    )
    return jax.shard_map(
        per_device,
        mesh=mesh,
        in_specs=placed,
        out_specs=(P("groups", None, "row", None), P("row", "groups")),
        check_vma=False,
    )
```

time: 48.3 us -> 38.8 us (0.80)
  local copies, waits for them, and re-layouts: 7.05 us -> 0.04 us
  waiting for transfers between devices: 12.4 us -> 9.38 us
  starting transfers between devices: 14.4 us -> 16.4 us
  Pallas kernels: 13.4 us -> 12.1 us
    unnamed x20 -> x14, local copies, waits for them, and re-layouts: 6.39 us -> 0.04 us
    ppermute x11 -> x14, waiting for transfers between devices: 12.4 us -> 9.38 us  [swap(): return lax.ppermute(value, 'row', [(i, i ^ mask) for i in range(count)])]
    ppermute x11 -> x14, starting transfers between devices: 13.8 us -> 15.7 us  [swap(): return lax.ppermute(value, 'row', [(i, i ^ mask) for i in range(count)])]
    pallas_call x1 -> x2, Pallas kernels: 7.95 us -> 6.31 us  [residual_call(): pl.pallas_call(kernel, in_specs=[local] * len(operands), out_specs=[local...]
    pallas_call x1, Pallas kernels: 0.61 us -> 1.38 us  [start_call(): pl.pallas_call(start_kernel, in_specs=[pl.BlockSpec(memory_space=pltpu.HB...]
    pallas_call x1 -> x0, local copies, waits for them, and re-layouts: 0.66 us -> none  [finish_call(): pl.pallas_call(functools.partial(finish_kernel, strides, width, ways), in...]
  transfers between devices with their start and end apart: 12 -> 15, of which waited for: 7 -> 6; matrix products, arithmetic and copies ran while one was open for 0% -> 0% of each run, Pallas kernels for 18% -> 18%
where the time goes in v3:
time: 38.8 us; the launch traced here: 38.7 us
  starting transfers between devices  16.4 us (42%)
  Pallas kernels  12.1 us (31%)
  waiting for transfers between devices  9.38 us (24%)
  between operations  0.81 us (2%)
    ppermute x14, starting transfers between devices, swap(): return lax.ppermute(value, 'row', [(i, i ^ mask) for i in range(count)])  15.7 us
    ppermute x14, waiting for transfers between devices, swap(): return lax.ppermute(value, 'row', [(i, i ^ mask) for i in range(count)])  9.38 us
    pallas_call x2, Pallas kernels, residual_call(): pl.pallas_call(kernel, in_specs=[local] * len(operands), out_specs=[local...  6.31 us
    pallas_call x1, Pallas kernels, finish_call(): pl.pallas_call(functools.partial(finish_kernel, strides, width, ways), in...  3.26 us
    pallas_call x1, Pallas kernels, start_call(): pl.pallas_call(start_kernel, in_specs=[pl.BlockSpec(memory_space=pltpu.HB...  1.38 us
  transfers between devices with their start and end apart: 15, of which 6 were waited for; matrix products, arithmetic and copies ran while one was open for 0% of the time, Pallas kernels for 18%

profile of v3, /device:TPU:0, one launch (start us, length us, event | category | flops | bytes accessed | tf_op | source)
XLA Modules:
  0.0 38.7 jit_solution(7305050776164585155)
XLA Ops:
  0.6 1.4 %start.1 = (f32[128,128]{1,0:T(8,128)S(1)}, f32[288,128]{1,0:T(8,128)S(1)}, f32[288,128]{1,0:T(8,128)S(1)}) custom-call(f32[128,128]{1,0:T(8,128)} %refs_19_.1, f32[128,128]{1,0:T(8,128)} %sub_hbm.1, f32[8,3,32,512]{3,2,1,0:T(8,128)} %disp_ref.3), custom_call_target="tpu_custom_call" | custom-call | flops 10000000000 | bytes 1000000 | tf_op jit(solution)/shard_map/start/pallas_call | solution.py:253
  2.0 0.0 copy-start
  2.0 0.0 copy-start.1
  2.0 0.0 copy-start.3
  2.1 0.0 copy-start.4
  2.1 0.0 copy-start.5
  2.1 0.5 %collective-permute-start = (f32[128,128]{1,0:T(8,128)S(1)}, f32[128,128]{1,0:T(8,128)S(1)}, u32[]{:S(2)}, u32[]{:S(2)}) collective-permute-start(f32[128,128]{1,0:T(8,128)S(1)} %get-tuple-element.24.own_ref.own_step_ref.refs_15_), channel_id=1, source_target_pairs={{0,1},{1,0},{2,3},{3,2},{4,5},{5,4},{6,7},{7,6},{8,9},{9,8},{10,11... | collective-permute-start | bytes 196616 | tf_op jit(solution)/shard_map/ppermute | solution.py:482
  2.6 0.9 %collective-permute-done.other_ref.other_step_ref.refs_16_ = f32[128,128]{1,0:T(8,128)S(1)} collective-permute-done((f32[128,128]{1,0:T(8,128)S(1)}, f32[128,128]{1,0:T(8,128)S(1)}, u32[]{:S(2)}, u32[]{:S(2)}) %collective-permute-start) | collective-permute-done | bytes 65568 | tf_op jit(solution)/shard_map/ppermute | solution.py:482
  3.5 0.0 copy-start.2
  3.5 0.4 %pair_maps.1 = (f32[256,128]{1,0:T(8,128)S(1)}, f32[128,128]{1,0:T(8,128)S(1)}) custom-call(f32[128,128]{1,0:T(8,128)S(1)} %get-tuple-element.24.own_ref.own_step_ref.refs_15_, f32[128,128]{1,0:T(8,128)S(1)} %collective-permute-done.other_ref.other_step_ref.refs_16_), custom_call_target="tpu_custom_call" | custom-call | flops 10000000000 | bytes 1000000 | tf_op jit(solution)/shard_map/pair_maps/pallas_call | solution.py:297
  3.9 2.9 %collective-permute-start.1 = (f32[256,128]{1,0:T(8,128)S(1)}, f32[256,128]{1,0:T(8,128)S(1)}, u32[]{:S(2)}, u32[]{:S(2)}) collective-permute-start(f32[256,128]{1,0:T(8,128)S(1)} %get-tuple-element.25.own_ref.maps_ref.own_maps_ref.refs_11_), channel_id=1, source_target_pairs={{0,2},{1,3},{2,0},{3,1},{4,6},{5,7},{6,4},{7,5},{8,10},{9,11},{10,... | collective-permute-start | bytes 393224 | tf_op jit(solution)/shard_map/ppermute | solution.py:482
  6.8 0.0 collective-permute-start.2
  6.8 0.7 %collective-permute-start.3 = (f32[288,128]{1,0:T(8,128)S(1)}, f32[288,128]{1,0:T(8,128)S(1)}, u32[]{:S(2)}, u32[]{:S(2)}) collective-permute-start(f32[288,128]{1,0:T(8,128)S(1)} %get-tuple-element.30), channel_id=1, source_target_pairs={{1,2},{2,1},{3,4},{4,3},{5,6},{6,5},{7,8},{8,7},{9,10},{10,9},{11,... | collective-permute-start | bytes 442376 | tf_op jit(solution)/shard_map/ppermute | solution.py:487
  7.5 0.0 copy-done
  7.5 0.0 copy-done.1
  7.5 0.0 copy-done.3
  7.5 0.0 copy-done.4
  7.5 0.0 copy-done.5
  7.5 0.0 copy-done.2
  7.5 3.6 %inner_residual.1 = (f32[8,3,16,512]{3,2,1,0:T(8,128)S(1)}, f32[3,8,16,512]{3,2,1,0:T(8,128)S(1)}, f32[3,8,512]{2,1,0:T(8,128)S(1)}, f32[32,64]{1,0:T(8,128)S(1)}) custom-call(f32[8,3,32,512]{3,2,1,0:T(8,128)S(1)} %copy-done, f32[8,3,32,512]{3,2,1,0:T(8,128)S(1)} %copy-done.1, f32[3,512,512]{2,1,0:T(8,128)S(1)} %copy-done.2, f32[32,512]{1,0:T(8,128)S(1)} %copy-done.5, ...), custom_call_target="tpu_custom_call" | custom-call | flops 603979776 | bytes 3145728 | tf_op jit(solution)/shard_map/inner_residual/pallas_call | solution.py:190
  11.2 0.0 collective-permute-done.1.other_ref.other_maps_ref.refs_12_
  11.2 0.0 copy-start.6
  11.2 0.4 join_maps.1
  11.6 5.4 %collective-permute-start.8 = (f32[128,128]{1,0:T(8,128)S(1)}, f32[128,128]{1,0:T(8,128)S(1)}, u32[]{:S(2)}, u32[]{:S(2)}) collective-permute-start(f32[128,128]{1,0:T(8,128)S(1)} %get-tuple-element.37), channel_id=1, source_target_pairs={{0,12},{1,13},{2,14},{3,15},{4,8},{5,9},{6,10},{7,11},{8,4},{9,5},... | collective-permute-start | bytes 196616 | tf_op jit(solution)/shard_map/ppermute | solution.py:482
  17.0 0.0 collective-permute-start.7
  17.0 0.6 %collective-permute-start.6 = (f32[128,128]{1,0:T(8,128)S(1)}, f32[128,128]{1,0:T(8,128)S(1)}, u32[]{:S(2)}, u32[]{:S(2)}) collective-permute-start(f32[128,128]{1,0:T(8,128)S(1)} %get-tuple-element.37), channel_id=1, source_target_pairs={{0,4},{1,5},{2,6},{3,7},{4,0},{5,1},{6,2},{7,3},{8,12},{9,13},{10,... | collective-permute-start | bytes 196616 | tf_op jit(solution)/shard_map/ppermute | solution.py:482
  17.7 0.0 collective-permute-done.2.near_ref
  17.7 0.0 collective-permute-done.3.far_ref
  17.7 0.0 copy-done.6
  17.7 2.7 %outer_residual.1 = (f32[8,3,16,512]{3,2,1,0:T(8,128)S(1)}, f32[8,128]{1,0:T(8,128)S(1)}) custom-call(f32[8,3,32,512]{3,2,1,0:T(8,128)S(1)} %copy-done, f32[8,3,32,512]{3,2,1,0:T(8,128)S(1)} %copy-done.1, f32[32,512]{1,0:T(8,128)S(1)} %copy-done.5, s32[3,32,512]{2,1,0:T(8,128)S(1)} %copy-done.3, f32[3,32,512]{2,1,0:T(8,128)S(1)} %copy-done.4, ...), custom_call_target="tpu_custom_call" | custom-call | flops 603979776 | bytes 3145728 | tf_op jit(solution)/shard_map/outer_residual/pallas_call | solution.py:190
  20.3 0.0 collective-permute-start.4
  20.3 1.2 %collective-permute-done.4.other_ref.refs_18_ = f32[8,128]{1,0:T(8,128)S(1)} collective-permute-done((f32[8,128]{1,0:T(8,128)S(1)}, f32[8,128]{1,0:T(8,128)S(1)}, u32[]{:S(2)}, u32[]{:S(2)}) %collective-permute-start.4) | collective-permute-done | bytes 4128 | tf_op jit(solution)/shard_map/ppermute | solution.py:482
  21.5 0.2 pair_shifts.1.own_ref.refs_13_
  21.7 1.8 %collective-permute-start.5 = (f32[16,128]{1,0:T(8,128)S(1)}, f32[16,128]{1,0:T(8,128)S(1)}, u32[]{:S(2)}, u32[]{:S(2)}) collective-permute-start(f32[16,128]{1,0:T(8,128)S(1)} %pair_shifts.1.own_ref.refs_13_), channel_id=1, source_target_pairs={{0,2},{1,3},{2,0},{3,1},{4,6},{5,7},{6,4},{7,5},{8,10},{9,11},{10,... | collective-permute-start | bytes 24584 | tf_op jit(solution)/shard_map/ppermute | solution.py:482
  23.5 1.9 %collective-permute-done.5.other_ref.refs_14_ = f32[16,128]{1,0:T(8,128)S(1)} collective-permute-done((f32[16,128]{1,0:T(8,128)S(1)}, f32[16,128]{1,0:T(8,128)S(1)}, u32[]{:S(2)}, u32[]{:S(2)}) %collective-permute-start.5) | collective-permute-done | bytes 8224 | tf_op jit(solution)/shard_map/ppermute | solution.py:482
  25.4 0.2 join_shifts.1.refs_7_
  25.6 0.0 collective-permute-done.8.refs_5_
  25.6 0.0 collective-permute-done.7.refs_3_
  25.6 0.0 collective-permute-done.6.refs_1_
  25.6 0.1 collective-permute-start.9
  25.7 0.5 %collective-permute-start.10 = (f32[128,128]{1,0:T(8,128)S(1)}, f32[128,128]{1,0:T(8,128)S(1)}, u32[]{:S(2)}, u32[]{:S(2)}) collective-permute-start(f32[128,128]{1,0:T(8,128)S(1)} %collective-permute-done.7.refs_3_), channel_id=1, source_target_pairs={{0,1},{1,0},{2,3},{3,2},{4,5},{5,4},{6,7},{7,6},{8,9},{9,8},{10,11... | collective-permute-start | bytes 196616 | tf_op jit(solution)/shard_map/ppermute | solution.py:482
  26.2 0.1 collective-permute-start.11
  26.3 3.7 %collective-permute-start.14 = (f32[16,128]{1,0:T(8,128)S(1)}, f32[16,128]{1,0:T(8,128)S(1)}, u32[]{:S(2)}, u32[]{:S(2)}) collective-permute-start(f32[16,128]{1,0:T(8,128)S(1)} %join_shifts.1.refs_7_), channel_id=1, source_target_pairs={{0,12},{1,13},{2,14},{3,15},{4,8},{5,9},{6,10},{7,11},{8,4},{9,5},... | collective-permute-start | bytes 24584 | tf_op jit(solution)/shard_map/ppermute | solution.py:482
  30.0 0.0 collective-permute-start.13
  30.0 1.7 %collective-permute-done.14.refs_10_ = f32[16,128]{1,0:T(8,128)S(1)} collective-permute-done((f32[16,128]{1,0:T(8,128)S(1)}, f32[16,128]{1,0:T(8,128)S(1)}, u32[]{:S(2)}, u32[]{:S(2)}) %collective-permute-start.14) | collective-permute-done | bytes 8224 | tf_op jit(solution)/shard_map/ppermute | solution.py:482
  31.7 0.0 collective-permute-start.12
  31.7 2.8 %collective-permute-done.13.refs_9_ = f32[16,128]{1,0:T(8,128)S(1)} collective-permute-done((f32[16,128]{1,0:T(8,128)S(1)}, f32[16,128]{1,0:T(8,128)S(1)}, u32[]{:S(2)}, u32[]{:S(2)}) %collective-permute-start.13) | collective-permute-done | bytes 8224 | tf_op jit(solution)/shard_map/ppermute | solution.py:482
  34.6 0.8 %collective-permute-done.12.refs_8_ = f32[16,128]{1,0:T(8,128)S(1)} collective-permute-done((f32[16,128]{1,0:T(8,128)S(1)}, f32[16,128]{1,0:T(8,128)S(1)}, u32[]{:S(2)}, u32[]{:S(2)}) %collective-permute-start.12) | collective-permute-done | bytes 8224 | tf_op jit(solution)/shard_map/ppermute | solution.py:482
  35.4 0.0 collective-permute-done.9.refs_2_
  35.4 0.0 collective-permute-done.10.refs_4_
  35.4 0.0 collective-permute-done.11.refs_6_
  35.4 3.3 %finish.1 = (f32[8,3,32,512]{3,2,1,0:T(8,128)}, f32[8,128]{1,0:T(8,128)}) custom-call(f32[256,128]{1,0:T(8,128)S(1)} %get-tuple-element.28.refs_0_, f32[128,128]{1,0:T(8,128)S(1)} %collective-permute-done.6.refs_1_, f32[128,128]{1,0:T(8,128)S(1)} %collective-permute-done.9.refs_2_, f32[128,128]{1,0:T(8,128)S(1)} %collective-permute-done.7.refs_3_, ...), custom_call_target="tpu_custom_call" | custom-call | tf_op jit(solution)/shard_map/finish/pallas_call | solution.py:452
Async XLA Ops:
  2.0 5.5 %copy-start = (f32[8,3,32,512]{3,2,1,0:T(8,128)S(1)}, f32[8,3,32,512]{3,2,1,0:T(8,128)}, u32[]{:S(2)}) copy-start(f32[8,3,32,512]{3,2,1,0:T(8,128)} %disp_ref.3) | copy-start | bytes 4718596
  2.0 5.5 %copy-start.1 = (f32[8,3,32,512]{3,2,1,0:T(8,128)S(1)}, f32[8,3,32,512]{3,2,1,0:T(8,128)}, u32[]{:S(2)}) copy-start(f32[8,3,32,512]{3,2,1,0:T(8,128)} %loads_ref.3) | copy-start | bytes 4718596
  2.0 5.5 %copy-start.3 = (s32[3,32,512]{2,1,0:T(8,128)S(1)}, s32[3,32,512]{2,1,0:T(8,128)}, u32[]{:S(2)}) copy-start(s32[3,32,512]{2,1,0:T(8,128)} %refs_22_.1) | copy-start | bytes 589828
  2.1 5.5 %copy-start.4 = (f32[3,32,512]{2,1,0:T(8,128)S(1)}, f32[3,32,512]{2,1,0:T(8,128)}, u32[]{:S(2)}) copy-start(f32[3,32,512]{2,1,0:T(8,128)} %refs_23_.1) | copy-start | bytes 589828
  2.1 5.5 %copy-start.5 = (f32[32,512]{1,0:T(8,128)S(1)}, f32[32,512]{1,0:T(8,128)}, u32[]{:S(2)}) copy-start(f32[32,512]{1,0:T(8,128)} %modulus_ref.3) | copy-start | bytes 196612
  2.1 1.4 %collective-permute-start = (f32[128,128]{1,0:T(8,128)S(1)}, f32[128,128]{1,0:T(8,128)S(1)}, u32[]{:S(2)}, u32[]{:S(2)}) collective-permute-start(f32[128,128]{1,0:T(8,128)S(1)} %get-tuple-element.24.own_ref.own_step_ref.refs_15_), channel_id=1, source_target_pairs={{0,1},{1,0},{2,3},{3,2},{4,5},{5,4},{6,7},{7,6},{8,9},{9,8},{10,11... | collective-permute-start | bytes 196616 | tf_op jit(solution)/shard_map/ppermute | solution.py:482
  3.5 4.0 %copy-start.2 = (f32[3,512,512]{2,1,0:T(8,128)S(1)}, f32[3,512,512]{2,1,0:T(8,128)}, u32[]{:S(2)}) copy-start(f32[3,512,512]{2,1,0:T(8,128)} %section_ref.1) | copy-start | bytes 9437188
  3.9 7.3 %collective-permute-start.1 = (f32[256,128]{1,0:T(8,128)S(1)}, f32[256,128]{1,0:T(8,128)S(1)}, u32[]{:S(2)}, u32[]{:S(2)}) collective-permute-start(f32[256,128]{1,0:T(8,128)S(1)} %get-tuple-element.25.own_ref.maps_ref.own_maps_ref.refs_11_), channel_id=1, source_target_pairs={{0,2},{1,3},{2,0},{3,1},{4,6},{5,7},{6,4},{7,5},{8,10},{9,11},{10,... | collective-permute-start | bytes 393224 | tf_op jit(solution)/shard_map/ppermute | solution.py:482
  6.8 10.9 %collective-permute-start.2 = (f32[288,128]{1,0:T(8,128)S(1)}, f32[288,128]{1,0:T(8,128)S(1)}, u32[]{:S(2)}, u32[]{:S(2)}) collective-permute-start(f32[288,128]{1,0:T(8,128)S(1)} %get-tuple-element.29), channel_id=1, source_target_pairs={{0,1},{1,0},{2,3},{3,2},{4,5},{5,4},{6,7},{7,6},{8,9},{9,8},{10,11... | collective-permute-start | bytes 442376 | tf_op jit(solution)/shard_map/ppermute | solution.py:482
  6.8 10.9 %collective-permute-start.3 = (f32[288,128]{1,0:T(8,128)S(1)}, f32[288,128]{1,0:T(8,128)S(1)}, u32[]{:S(2)}, u32[]{:S(2)}) collective-permute-start(f32[288,128]{1,0:T(8,128)S(1)} %get-tuple-element.30), channel_id=1, source_target_pairs={{1,2},{2,1},{3,4},{4,3},{5,6},{6,5},{7,8},{8,7},{9,10},{10,9},{11,... | collective-permute-start | bytes 442376 | tf_op jit(solution)/shard_map/ppermute | solution.py:487
  11.2 6.5 %copy-start.6 = (f32[128,128]{1,0:T(8,128)S(1)}, f32[128,128]{1,0:T(8,128)}, u32[]{:S(2)}) copy-start(f32[128,128]{1,0:T(8,128)} %refs_19_.1) | copy-start | bytes 196612
  11.6 14.0 %collective-permute-start.8 = (f32[128,128]{1,0:T(8,128)S(1)}, f32[128,128]{1,0:T(8,128)S(1)}, u32[]{:S(2)}, u32[]{:S(2)}) collective-permute-start(f32[128,128]{1,0:T(8,128)S(1)} %get-tuple-element.37), channel_id=1, source_target_pairs={{0,12},{1,13},{2,14},{3,15},{4,8},{5,9},{6,10},{7,11},{8,4},{9,5},... | collective-permute-start | bytes 196616 | tf_op jit(solution)/shard_map/ppermute | solution.py:482
  17.0 8.6 %collective-permute-start.7 = (f32[128,128]{1,0:T(8,128)S(1)}, f32[128,128]{1,0:T(8,128)S(1)}, u32[]{:S(2)}, u32[]{:S(2)}) collective-permute-start(f32[128,128]{1,0:T(8,128)S(1)} %get-tuple-element.37), channel_id=1, source_target_pairs={{0,8},{1,9},{2,10},{3,11},{4,12},{5,13},{6,14},{7,15},{8,0},{9,1},... | collective-permute-start | bytes 196616 | tf_op jit(solution)/shard_map/ppermute | solution.py:482
  17.0 8.6 %collective-permute-start.6 = (f32[128,128]{1,0:T(8,128)S(1)}, f32[128,128]{1,0:T(8,128)S(1)}, u32[]{:S(2)}, u32[]{:S(2)}) collective-permute-start(f32[128,128]{1,0:T(8,128)S(1)} %get-tuple-element.37), channel_id=1, source_target_pairs={{0,4},{1,5},{2,6},{3,7},{4,0},{5,1},{6,2},{7,3},{8,12},{9,13},{10,... | collective-permute-start | bytes 196616 | tf_op jit(solution)/shard_map/ppermute | solution.py:482
  20.3 1.2 %collective-permute-start.4 = (f32[8,128]{1,0:T(8,128)S(1)}, f32[8,128]{1,0:T(8,128)S(1)}, u32[]{:S(2)}, u32[]{:S(2)}) collective-permute-start(f32[8,128]{1,0:T(8,128)S(1)} %get-tuple-element.34.own_ref.refs_17_), channel_id=1, source_target_pairs={{0,1},{1,0},{2,3},{3,2},{4,5},{5,4},{6,7},{7,6},{8,9},{9,8},{10,11... | collective-permute-start | bytes 12296 | tf_op jit(solution)/shard_map/ppermute | solution.py:482
  21.7 3.7 %collective-permute-start.5 = (f32[16,128]{1,0:T(8,128)S(1)}, f32[16,128]{1,0:T(8,128)S(1)}, u32[]{:S(2)}, u32[]{:S(2)}) collective-permute-start(f32[16,128]{1,0:T(8,128)S(1)} %pair_shifts.1.own_ref.refs_13_), channel_id=1, source_target_pairs={{0,2},{1,3},{2,0},{3,1},{4,6},{5,7},{6,4},{7,5},{8,10},{9,11},{10,... | collective-permute-start | bytes 24584 | tf_op jit(solution)/shard_map/ppermute | solution.py:482
  25.6 9.8 %collective-permute-start.9 = (f32[128,128]{1,0:T(8,128)S(1)}, f32[128,128]{1,0:T(8,128)S(1)}, u32[]{:S(2)}, u32[]{:S(2)}) collective-permute-start(f32[128,128]{1,0:T(8,128)S(1)} %collective-permute-done.6.refs_1_), channel_id=1, source_target_pairs={{0,1},{1,0},{2,3},{3,2},{4,5},{5,4},{6,7},{7,6},{8,9},{9,8},{10,11... | collective-permute-start | bytes 196616 | tf_op jit(solution)/shard_map/ppermute | solution.py:482
  25.7 9.7 %collective-permute-start.10 = (f32[128,128]{1,0:T(8,128)S(1)}, f32[128,128]{1,0:T(8,128)S(1)}, u32[]{:S(2)}, u32[]{:S(2)}) collective-permute-start(f32[128,128]{1,0:T(8,128)S(1)} %collective-permute-done.7.refs_3_), channel_id=1, source_target_pairs={{0,1},{1,0},{2,3},{3,2},{4,5},{5,4},{6,7},{7,6},{8,9},{9,8},{10,11... | collective-permute-start | bytes 196616 | tf_op jit(solution)/shard_map/ppermute | solution.py:482
  26.2 9.2 %collective-permute-start.11 = (f32[128,128]{1,0:T(8,128)S(1)}, f32[128,128]{1,0:T(8,128)S(1)}, u32[]{:S(2)}, u32[]{:S(2)}) collective-permute-start(f32[128,128]{1,0:T(8,128)S(1)} %collective-permute-done.8.refs_5_), channel_id=1, source_target_pairs={{0,1},{1,0},{2,3},{3,2},{4,5},{5,4},{6,7},{7,6},{8,9},{9,8},{10,11... | collective-permute-start | bytes 196616 | tf_op jit(solution)/shard_map/ppermute | solution.py:482
  26.3 5.4 %collective-permute-start.14 = (f32[16,128]{1,0:T(8,128)S(1)}, f32[16,128]{1,0:T(8,128)S(1)}, u32[]{:S(2)}, u32[]{:S(2)}) collective-permute-start(f32[16,128]{1,0:T(8,128)S(1)} %join_shifts.1.refs_7_), channel_id=1, source_target_pairs={{0,12},{1,13},{2,14},{3,15},{4,8},{5,9},{6,10},{7,11},{8,4},{9,5},... | collective-permute-start | bytes 24584 | tf_op jit(solution)/shard_map/ppermute | solution.py:482
  30.0 4.5 %collective-permute-start.13 = (f32[16,128]{1,0:T(8,128)S(1)}, f32[16,128]{1,0:T(8,128)S(1)}, u32[]{:S(2)}, u32[]{:S(2)}) collective-permute-start(f32[16,128]{1,0:T(8,128)S(1)} %join_shifts.1.refs_7_), channel_id=1, source_target_pairs={{0,8},{1,9},{2,10},{3,11},{4,12},{5,13},{6,14},{7,15},{8,0},{9,1},... | collective-permute-start | bytes 24584 | tf_op jit(solution)/shard_map/ppermute | solution.py:482
  31.7 3.7 %collective-permute-start.12 = (f32[16,128]{1,0:T(8,128)S(1)}, f32[16,128]{1,0:T(8,128)S(1)}, u32[]{:S(2)}, u32[]{:S(2)}) collective-permute-start(f32[16,128]{1,0:T(8,128)S(1)} %join_shifts.1.refs_7_), channel_id=1, source_target_pairs={{0,4},{1,5},{2,6},{3,7},{4,0},{5,1},{6,2},{7,3},{8,12},{9,13},{10,... | collective-permute-start | bytes 24584 | tf_op jit(solution)/shard_map/ppermute | solution.py:482

commit v4 on v3

--- a/solution.py
+++ b/solution.py
@@ -8,6 +8,7 @@
 from jax.sharding import PartitionSpec as P
 
 span_weights = (1.5, -0.15, 1.0 / 90.0)
+hop_order = (0, 1, 3, 2)
 bf16, f32 = jnp.bfloat16, jnp.float32
 NN = (((1,), (0,)), ((), ()))
 NT = (((1,), (1,)), ((), ()))
@@ -346,7 +347,8 @@
 
 
 def finish_kernel(strides, width, ways, *refs):
-    own_maps_ref, halves, refs = refs[0], refs[1 : 2 * ways - 1], refs[2 * ways - 1 :]
+    own_maps_ref, got_ref, swapped_ref, *refs = refs
+    order = own_maps_ref.shape[1]
     shifts, refs = refs[:ways], refs[ways:]
     levels = []
     for stride in strides:
@@ -356,7 +358,7 @@
      labels_ref,
      weight_ref, updated_hbm, solution_hbm, all_maps, all_shifts, ahead_ref, back_ref, updated,
      solution, out_sems) = refs
-    cases, order = own_value_ref.shape
+    cases = own_value_ref.shape[0]
     comps, layers, section = labels_ref.shape
     mine = lax.axis_index("row")
     odd = (mine & 1) == 1
@@ -364,11 +366,12 @@
 
     all_maps[group] = own_maps_ref[...]
     for hop in range(1, ways):
-        got, swapped = halves[2 * hop - 2][...], halves[2 * hop - 1][...]
+        part = slice((hop - 1) * order, hop * order)
+        got, swapped = got_ref[part, :], swapped_ref[part, :]
         all_maps[group ^ hop, :order] = jnp.where(odd, swapped, got)
         all_maps[group ^ hop, order:] = jnp.where(odd, got, swapped)
     for hop in range(ways):
-        all_shifts[group ^ hop] = shifts[hop][...]
+        all_shifts[group ^ hop_order[hop]] = shifts[hop][...]
 
     ahead = all_shifts[0, :cases]
     ahead_ref[0] = jnp.zeros_like(ahead)
@@ -448,7 +451,7 @@
     order = maps[0].shape[1]
     ways = len(shifts)
     hbm, local = pl.BlockSpec(memory_space=pltpu.HBM), pl.BlockSpec(memory_space=pltpu.VMEM)
-    before = (*maps, *shifts, *levels, *leaf)
+    before = (*maps, *[shifts[hop] for hop in hop_order], *levels, *leaf)
     return pl.pallas_call(
         functools.partial(finish_kernel, strides, width, ways),
         in_specs=[local] * (len(before) + 4),
@@ -536,10 +539,8 @@
             functools.partial(join_shifts_kernel, stride), "join_shifts", cases,
             shifts, other_shifts, own_maps, other_maps, mixed,
         )
-    shifts, *halves = lax.optimization_barrier((shifts, *halves))
-    all_maps = [maps]
-    for half in halves:
-        all_maps += [half, swap(half, 1)]
+    gathered = jnp.concatenate(lax.optimization_barrier((shifts, *halves))[1:], axis=0)
+    all_maps = [maps, gathered, swap(gathered, 1)]
     all_shifts = [shifts] + [swap(shifts, hop * width) for hop in range(1, ways)]
     leaf = (step, other_step, value, other_value, diag_inverse)
     updated, solution_rows = finish_call(

time: 38.8 us -> 37 us (0.954)
  waiting for transfers between devices: 9.38 us -> 7.51 us
    ppermute x14 -> x12, waiting for transfers between devices: 9.38 us -> 7.51 us  [swap(): return lax.ppermute(value, 'row', [(i, i ^ mask) for i in range(count)])]
    ppermute x14 -> x12, starting transfers between devices: 15.7 us -> 15.8 us  [swap(): return lax.ppermute(value, 'row', [(i, i ^ mask) for i in range(count)])]
  transfers between devices with their start and end apart: 15 -> 13, of which waited for: 6 -> 5; matrix products, arithmetic and copies ran while one was open for 0% -> 0% of each run, Pallas kernels for 18% -> 19%
where the time goes in v4:
time: 37 us; the launch traced here: 36.9 us
  starting transfers between devices  16.4 us (44%)
  Pallas kernels  12.1 us (33%)
  waiting for transfers between devices  7.51 us (20%)
  between operations  0.83 us (2%)
    ppermute x12, starting transfers between devices, swap(): return lax.ppermute(value, 'row', [(i, i ^ mask) for i in range(count)])  15.8 us
    ppermute x12, waiting for transfers between devices, swap(): return lax.ppermute(value, 'row', [(i, i ^ mask) for i in range(count)])  7.51 us
    pallas_call x2, Pallas kernels, residual_call(): pl.pallas_call(kernel, in_specs=[local] * len(operands), out_specs=[local...  6.31 us
    pallas_call x1, Pallas kernels, finish_call(): pl.pallas_call(functools.partial(finish_kernel, strides, width, ways), in...  3.24 us
    pallas_call x1, Pallas kernels, start_call(): pl.pallas_call(start_kernel, in_specs=[pl.BlockSpec(memory_space=pltpu.HB...  1.38 us
    pallas_call x2, Pallas kernels, maps_call(): pl.pallas_call(kernel, out_shape=[jax.ShapeDtypeStruct((2 * order, order)...  0.76 us
  transfers between devices with their start and end apart: 13, of which 5 were waited for; matrix products, arithmetic and copies ran while one was open for 0% of the time, Pallas kernels for 19%

profile of v4, /device:TPU:0, one launch (start us, length us, event | category | flops | bytes accessed | tf_op | source)
XLA Modules:
  0.0 36.9 jit_solution(14752885952739939905)
XLA Ops:
  0.6 1.4 %start.1 = (f32[128,128]{1,0:T(8,128)S(1)}, f32[288,128]{1,0:T(8,128)S(1)}, f32[288,128]{1,0:T(8,128)S(1)}) custom-call(f32[128,128]{1,0:T(8,128)} %refs_15_.1, f32[128,128]{1,0:T(8,128)} %sub_hbm.1, f32[8,3,32,512]{3,2,1,0:T(8,128)} %disp_ref.3), custom_call_target="tpu_custom_call" | custom-call | flops 10000000000 | bytes 1000000 | tf_op jit(solution)/shard_map/start/pallas_call | solution.py:254
  2.0 0.0 copy-start
  2.0 0.0 copy-start.1
  2.0 0.0 copy-start.3
  2.1 0.0 copy-start.4
  2.1 0.0 copy-start.5
  2.1 0.5 %collective-permute-start = (f32[128,128]{1,0:T(8,128)S(1)}, f32[128,128]{1,0:T(8,128)S(1)}, u32[]{:S(2)}, u32[]{:S(2)}) collective-permute-start(f32[128,128]{1,0:T(8,128)S(1)} %get-tuple-element.23.own_ref.own_step_ref.refs_11_), channel_id=1, source_target_pairs={{0,1},{1,0},{2,3},{3,2},{4,5},{5,4},{6,7},{7,6},{8,9},{9,8},{10,11... | collective-permute-start | bytes 196616 | tf_op jit(solution)/shard_map/ppermute | solution.py:485
  2.6 0.9 %collective-permute-done.other_ref.other_step_ref.refs_12_ = f32[128,128]{1,0:T(8,128)S(1)} collective-permute-done((f32[128,128]{1,0:T(8,128)S(1)}, f32[128,128]{1,0:T(8,128)S(1)}, u32[]{:S(2)}, u32[]{:S(2)}) %collective-permute-start) | collective-permute-done | bytes 65568 | tf_op jit(solution)/shard_map/ppermute | solution.py:485
  3.5 0.0 copy-start.2
  3.5 0.4 %pair_maps.1 = (f32[256,128]{1,0:T(8,128)S(1)}, f32[128,128]{1,0:T(8,128)S(1)}) custom-call(f32[128,128]{1,0:T(8,128)S(1)} %get-tuple-element.23.own_ref.own_step_ref.refs_11_, f32[128,128]{1,0:T(8,128)S(1)} %collective-permute-done.other_ref.other_step_ref.refs_12_), custom_call_target="tpu_custom_call" | custom-call | flops 10000000000 | bytes 1000000 | tf_op jit(solution)/shard_map/pair_maps/pallas_call | solution.py:298
  3.9 2.9 %collective-permute-start.1 = (f32[256,128]{1,0:T(8,128)S(1)}, f32[256,128]{1,0:T(8,128)S(1)}, u32[]{:S(2)}, u32[]{:S(2)}) collective-permute-start(f32[256,128]{1,0:T(8,128)S(1)} %get-tuple-element.24.own_ref.maps_ref.own_maps_ref.refs_7_), channel_id=1, source_target_pairs={{0,2},{1,3},{2,0},{3,1},{4,6},{5,7},{6,4},{7,5},{8,10},{9,11},{10,... | collective-permute-start | bytes 393224 | tf_op jit(solution)/shard_map/ppermute | solution.py:485
  6.8 0.0 collective-permute-start.2
  6.8 0.7 %collective-permute-start.3 = (f32[288,128]{1,0:T(8,128)S(1)}, f32[288,128]{1,0:T(8,128)S(1)}, u32[]{:S(2)}, u32[]{:S(2)}) collective-permute-start(f32[288,128]{1,0:T(8,128)S(1)} %get-tuple-element.29), channel_id=1, source_target_pairs={{1,2},{2,1},{3,4},{4,3},{5,6},{6,5},{7,8},{8,7},{9,10},{10,9},{11,... | collective-permute-start | bytes 442376 | tf_op jit(solution)/shard_map/ppermute | solution.py:490
  7.5 0.0 copy-done
  7.5 0.0 copy-done.1
  7.5 0.0 copy-done.3
  7.5 0.0 copy-done.4
  7.5 0.0 copy-done.5
  7.5 0.0 copy-done.2
  7.5 3.6 %inner_residual.1 = (f32[8,3,16,512]{3,2,1,0:T(8,128)S(1)}, f32[3,8,16,512]{3,2,1,0:T(8,128)S(1)}, f32[3,8,512]{2,1,0:T(8,128)S(1)}, f32[32,64]{1,0:T(8,128)S(1)}) custom-call(f32[8,3,32,512]{3,2,1,0:T(8,128)S(1)} %copy-done, f32[8,3,32,512]{3,2,1,0:T(8,128)S(1)} %copy-done.1, f32[3,512,512]{2,1,0:T(8,128)S(1)} %copy-done.2, f32[32,512]{1,0:T(8,128)S(1)} %copy-done.5, ...), custom_call_target="tpu_custom_call" | custom-call | flops 603979776 | bytes 3145728 | tf_op jit(solution)/shard_map/inner_residual/pallas_call | solution.py:191
  11.2 0.0 collective-permute-done.1.other_ref.other_maps_ref.refs_8_
  11.2 0.0 copy-start.6
  11.2 0.4 join_maps.1
  11.6 5.4 %collective-permute-start.8 = (f32[128,128]{1,0:T(8,128)S(1)}, f32[128,128]{1,0:T(8,128)S(1)}, u32[]{:S(2)}, u32[]{:S(2)}) collective-permute-start(f32[128,128]{1,0:T(8,128)S(1)} %get-tuple-element.36), channel_id=1, source_target_pairs={{0,12},{1,13},{2,14},{3,15},{4,8},{5,9},{6,10},{7,11},{8,4},{9,5},... | collective-permute-start | bytes 196616 | tf_op jit(solution)/shard_map/ppermute | solution.py:485
  17.0 0.0 collective-permute-start.7
  17.0 0.6 %collective-permute-start.6 = (f32[128,128]{1,0:T(8,128)S(1)}, f32[128,128]{1,0:T(8,128)S(1)}, u32[]{:S(2)}, u32[]{:S(2)}) collective-permute-start(f32[128,128]{1,0:T(8,128)S(1)} %get-tuple-element.36), channel_id=1, source_target_pairs={{0,4},{1,5},{2,6},{3,7},{4,0},{5,1},{6,2},{7,3},{8,12},{9,13},{10,... | collective-permute-start | bytes 196616 | tf_op jit(solution)/shard_map/ppermute | solution.py:485
  17.7 0.0 collective-permute-done.2.near_ref
  17.7 0.0 collective-permute-done.3.far_ref
  17.7 0.0 copy-done.6
  17.7 2.7 %outer_residual.1 = (f32[8,3,16,512]{3,2,1,0:T(8,128)S(1)}, f32[8,128]{1,0:T(8,128)S(1)}) custom-call(f32[8,3,32,512]{3,2,1,0:T(8,128)S(1)} %copy-done, f32[8,3,32,512]{3,2,1,0:T(8,128)S(1)} %copy-done.1, f32[32,512]{1,0:T(8,128)S(1)} %copy-done.5, s32[3,32,512]{2,1,0:T(8,128)S(1)} %copy-done.3, f32[3,32,512]{2,1,0:T(8,128)S(1)} %copy-done.4, ...), custom_call_target="tpu_custom_call" | custom-call | flops 603979776 | bytes 3145728 | tf_op jit(solution)/shard_map/outer_residual/pallas_call | solution.py:191
  20.3 0.0 collective-permute-start.4
  20.3 1.2 %collective-permute-done.4.other_ref.refs_14_ = f32[8,128]{1,0:T(8,128)S(1)} collective-permute-done((f32[8,128]{1,0:T(8,128)S(1)}, f32[8,128]{1,0:T(8,128)S(1)}, u32[]{:S(2)}, u32[]{:S(2)}) %collective-permute-start.4) | collective-permute-done | bytes 4128 | tf_op jit(solution)/shard_map/ppermute | solution.py:485
  21.5 0.2 pair_shifts.1.own_ref.refs_9_
  21.7 1.8 %collective-permute-start.5 = (f32[16,128]{1,0:T(8,128)S(1)}, f32[16,128]{1,0:T(8,128)S(1)}, u32[]{:S(2)}, u32[]{:S(2)}) collective-permute-start(f32[16,128]{1,0:T(8,128)S(1)} %pair_shifts.1.own_ref.refs_9_), channel_id=1, source_target_pairs={{0,2},{1,3},{2,0},{3,1},{4,6},{5,7},{6,4},{7,5},{8,10},{9,11},{10,... | collective-permute-start | bytes 24584 | tf_op jit(solution)/shard_map/ppermute | solution.py:485
  23.5 1.9 %collective-permute-done.5.other_ref.refs_10_ = f32[16,128]{1,0:T(8,128)S(1)} collective-permute-done((f32[16,128]{1,0:T(8,128)S(1)}, f32[16,128]{1,0:T(8,128)S(1)}, u32[]{:S(2)}, u32[]{:S(2)}) %collective-permute-start.5) | collective-permute-done | bytes 8224 | tf_op jit(solution)/shard_map/ppermute | solution.py:485
  25.4 0.2 join_shifts.1.refs_3_
  25.6 0.0 collective-permute-done.8
  25.6 0.0 collective-permute-done.7
  25.6 0.0 collective-permute-done.6
  25.7 0.1 collective-permute-start.9
  25.8 2.4 %collective-permute-start.12 = (f32[16,128]{1,0:T(8,128)S(1)}, f32[16,128]{1,0:T(8,128)S(1)}, u32[]{:S(2)}, u32[]{:S(2)}) collective-permute-start(f32[16,128]{1,0:T(8,128)S(1)} %join_shifts.1.refs_3_), channel_id=1, source_target_pairs={{0,8},{1,9},{2,10},{3,11},{4,12},{5,13},{6,14},{7,15},{8,0},{9,1},... | collective-permute-start | bytes 24584 | tf_op jit(solution)/shard_map/ppermute | solution.py:485
  28.1 1.5 %collective-permute-start.11 = (f32[16,128]{1,0:T(8,128)S(1)}, f32[16,128]{1,0:T(8,128)S(1)}, u32[]{:S(2)}, u32[]{:S(2)}) collective-permute-start(f32[16,128]{1,0:T(8,128)S(1)} %join_shifts.1.refs_3_), channel_id=1, source_target_pairs={{0,12},{1,13},{2,14},{3,15},{4,8},{5,9},{6,10},{7,11},{8,4},{9,5},... | collective-permute-start | bytes 24584 | tf_op jit(solution)/shard_map/ppermute | solution.py:485
  29.6 0.5 %collective-permute-start.10 = (f32[16,128]{1,0:T(8,128)S(1)}, f32[16,128]{1,0:T(8,128)S(1)}, u32[]{:S(2)}, u32[]{:S(2)}) collective-permute-start(f32[16,128]{1,0:T(8,128)S(1)} %join_shifts.1.refs_3_), channel_id=1, source_target_pairs={{0,4},{1,5},{2,6},{3,7},{4,0},{5,1},{6,2},{7,3},{8,12},{9,13},{10,... | collective-permute-start | bytes 24584 | tf_op jit(solution)/shard_map/ppermute | solution.py:485
  30.1 0.2 collective-permute-done.12.refs_6_
  30.4 3.2 %collective-permute-done.11.refs_5_ = f32[16,128]{1,0:T(8,128)S(1)} collective-permute-done((f32[16,128]{1,0:T(8,128)S(1)}, f32[16,128]{1,0:T(8,128)S(1)}, u32[]{:S(2)}, u32[]{:S(2)}) %collective-permute-start.11) | collective-permute-done | bytes 8224 | tf_op jit(solution)/shard_map/ppermute | solution.py:485
  33.6 0.0 collective-permute-done.10.refs_4_
  33.6 0.0 collective-permute-done.9.refs_2_
  33.6 3.2 %finish.1 = (f32[8,3,32,512]{3,2,1,0:T(8,128)}, f32[8,128]{1,0:T(8,128)}) custom-call(f32[256,128]{1,0:T(8,128)S(1)} %get-tuple-element.27.refs_0_, f32[384,128]{1,0:T(8,128)S(1)} %constant_dynamic-update-slice_fusion.refs_1_, f32[384,128]{1,0:T(8,128)S(1)} %collective-permute-done.9.refs_2_, f32[16,128]{1,0:T(8,128)S(1)} %join_shifts.1.refs_3_, ...), custom_call_target="tpu_custom_call" | custom-call | tf_op jit(solution)/shard_map/finish/pallas_call | solution.py:455
  (3 shorter events, 0.0 us)
Async XLA Ops:
  2.0 5.5 %copy-start = (f32[8,3,32,512]{3,2,1,0:T(8,128)S(1)}, f32[8,3,32,512]{3,2,1,0:T(8,128)}, u32[]{:S(2)}) copy-start(f32[8,3,32,512]{3,2,1,0:T(8,128)} %disp_ref.3) | copy-start | bytes 4718596
  2.0 5.5 %copy-start.1 = (f32[8,3,32,512]{3,2,1,0:T(8,128)S(1)}, f32[8,3,32,512]{3,2,1,0:T(8,128)}, u32[]{:S(2)}) copy-start(f32[8,3,32,512]{3,2,1,0:T(8,128)} %loads_ref.3) | copy-start | bytes 4718596
  2.0 5.5 %copy-start.3 = (s32[3,32,512]{2,1,0:T(8,128)S(1)}, s32[3,32,512]{2,1,0:T(8,128)}, u32[]{:S(2)}) copy-start(s32[3,32,512]{2,1,0:T(8,128)} %refs_18_.1) | copy-start | bytes 589828
  2.1 5.5 %copy-start.4 = (f32[3,32,512]{2,1,0:T(8,128)S(1)}, f32[3,32,512]{2,1,0:T(8,128)}, u32[]{:S(2)}) copy-start(f32[3,32,512]{2,1,0:T(8,128)} %refs_19_.1) | copy-start | bytes 589828
  2.1 5.5 %copy-start.5 = (f32[32,512]{1,0:T(8,128)S(1)}, f32[32,512]{1,0:T(8,128)}, u32[]{:S(2)}) copy-start(f32[32,512]{1,0:T(8,128)} %modulus_ref.3) | copy-start | bytes 196612
  2.1 1.4 %collective-permute-start = (f32[128,128]{1,0:T(8,128)S(1)}, f32[128,128]{1,0:T(8,128)S(1)}, u32[]{:S(2)}, u32[]{:S(2)}) collective-permute-start(f32[128,128]{1,0:T(8,128)S(1)} %get-tuple-element.23.own_ref.own_step_ref.refs_11_), channel_id=1, source_target_pairs={{0,1},{1,0},{2,3},{3,2},{4,5},{5,4},{6,7},{7,6},{8,9},{9,8},{10,11... | collective-permute-start | bytes 196616 | tf_op jit(solution)/shard_map/ppermute | solution.py:485
  3.5 4.0 %copy-start.2 = (f32[3,512,512]{2,1,0:T(8,128)S(1)}, f32[3,512,512]{2,1,0:T(8,128)}, u32[]{:S(2)}) copy-start(f32[3,512,512]{2,1,0:T(8,128)} %section_ref.1) | copy-start | bytes 9437188
  3.9 7.3 %collective-permute-start.1 = (f32[256,128]{1,0:T(8,128)S(1)}, f32[256,128]{1,0:T(8,128)S(1)}, u32[]{:S(2)}, u32[]{:S(2)}) collective-permute-start(f32[256,128]{1,0:T(8,128)S(1)} %get-tuple-element.24.own_ref.maps_ref.own_maps_ref.refs_7_), channel_id=1, source_target_pairs={{0,2},{1,3},{2,0},{3,1},{4,6},{5,7},{6,4},{7,5},{8,10},{9,11},{10,... | collective-permute-start | bytes 393224 | tf_op jit(solution)/shard_map/ppermute | solution.py:485
  6.8 10.9 %collective-permute-start.2 = (f32[288,128]{1,0:T(8,128)S(1)}, f32[288,128]{1,0:T(8,128)S(1)}, u32[]{:S(2)}, u32[]{:S(2)}) collective-permute-start(f32[288,128]{1,0:T(8,128)S(1)} %get-tuple-element.28), channel_id=1, source_target_pairs={{0,1},{1,0},{2,3},{3,2},{4,5},{5,4},{6,7},{7,6},{8,9},{9,8},{10,11... | collective-permute-start | bytes 442376 | tf_op jit(solution)/shard_map/ppermute | solution.py:485
  6.8 10.9 %collective-permute-start.3 = (f32[288,128]{1,0:T(8,128)S(1)}, f32[288,128]{1,0:T(8,128)S(1)}, u32[]{:S(2)}, u32[]{:S(2)}) collective-permute-start(f32[288,128]{1,0:T(8,128)S(1)} %get-tuple-element.29), channel_id=1, source_target_pairs={{1,2},{2,1},{3,4},{4,3},{5,6},{6,5},{7,8},{8,7},{9,10},{10,9},{11,... | collective-permute-start | bytes 442376 | tf_op jit(solution)/shard_map/ppermute | solution.py:490
  11.2 6.5 %copy-start.6 = (f32[128,128]{1,0:T(8,128)S(1)}, f32[128,128]{1,0:T(8,128)}, u32[]{:S(2)}) copy-start(f32[128,128]{1,0:T(8,128)} %refs_15_.1) | copy-start | bytes 196612
  11.6 14.0 %collective-permute-start.8 = (f32[128,128]{1,0:T(8,128)S(1)}, f32[128,128]{1,0:T(8,128)S(1)}, u32[]{:S(2)}, u32[]{:S(2)}) collective-permute-start(f32[128,128]{1,0:T(8,128)S(1)} %get-tuple-element.36), channel_id=1, source_target_pairs={{0,12},{1,13},{2,14},{3,15},{4,8},{5,9},{6,10},{7,11},{8,4},{9,5},... | collective-permute-start | bytes 196616 | tf_op jit(solution)/shard_map/ppermute | solution.py:485
  17.0 8.6 %collective-permute-start.7 = (f32[128,128]{1,0:T(8,128)S(1)}, f32[128,128]{1,0:T(8,128)S(1)}, u32[]{:S(2)}, u32[]{:S(2)}) collective-permute-start(f32[128,128]{1,0:T(8,128)S(1)} %get-tuple-element.36), channel_id=1, source_target_pairs={{0,8},{1,9},{2,10},{3,11},{4,12},{5,13},{6,14},{7,15},{8,0},{9,1},... | collective-permute-start | bytes 196616 | tf_op jit(solution)/shard_map/ppermute | solution.py:485
  17.0 8.6 %collective-permute-start.6 = (f32[128,128]{1,0:T(8,128)S(1)}, f32[128,128]{1,0:T(8,128)S(1)}, u32[]{:S(2)}, u32[]{:S(2)}) collective-permute-start(f32[128,128]{1,0:T(8,128)S(1)} %get-tuple-element.36), channel_id=1, source_target_pairs={{0,4},{1,5},{2,6},{3,7},{4,0},{5,1},{6,2},{7,3},{8,12},{9,13},{10,... | collective-permute-start | bytes 196616 | tf_op jit(solution)/shard_map/ppermute | solution.py:485
  20.3 1.2 %collective-permute-start.4 = (f32[8,128]{1,0:T(8,128)S(1)}, f32[8,128]{1,0:T(8,128)S(1)}, u32[]{:S(2)}, u32[]{:S(2)}) collective-permute-start(f32[8,128]{1,0:T(8,128)S(1)} %get-tuple-element.33.own_ref.refs_13_), channel_id=1, source_target_pairs={{0,1},{1,0},{2,3},{3,2},{4,5},{5,4},{6,7},{7,6},{8,9},{9,8},{10,11... | collective-permute-start | bytes 12296 | tf_op jit(solution)/shard_map/ppermute | solution.py:485
  21.7 3.7 %collective-permute-start.5 = (f32[16,128]{1,0:T(8,128)S(1)}, f32[16,128]{1,0:T(8,128)S(1)}, u32[]{:S(2)}, u32[]{:S(2)}) collective-permute-start(f32[16,128]{1,0:T(8,128)S(1)} %pair_shifts.1.own_ref.refs_9_), channel_id=1, source_target_pairs={{0,2},{1,3},{2,0},{3,1},{4,6},{5,7},{6,4},{7,5},{8,10},{9,11},{10,... | collective-permute-start | bytes 24584 | tf_op jit(solution)/shard_map/ppermute | solution.py:485
  25.7 7.9 %collective-permute-start.9 = (f32[384,128]{1,0:T(8,128)S(1)}, f32[384,128]{1,0:T(8,128)S(1)}, u32[]{:S(2)}, u32[]{:S(2)}) collective-permute-start(f32[384,128]{1,0:T(8,128)S(1)} %constant_dynamic-update-slice_fusion.refs_1_), channel_id=1, source_target_pairs={{0,1},{1,0},{2,3},{3,2},{4,5},{5,4},{6,7},{7,6},{8,9},{9,8},{10,11... | collective-permute-start | bytes 589832 | tf_op jit(solution)/shard_map/ppermute | solution.py:485
  25.8 4.6 %collective-permute-start.12 = (f32[16,128]{1,0:T(8,128)S(1)}, f32[16,128]{1,0:T(8,128)S(1)}, u32[]{:S(2)}, u32[]{:S(2)}) collective-permute-start(f32[16,128]{1,0:T(8,128)S(1)} %join_shifts.1.refs_3_), channel_id=1, source_target_pairs={{0,8},{1,9},{2,10},{3,11},{4,12},{5,13},{6,14},{7,15},{8,0},{9,1},... | collective-permute-start | bytes 24584 | tf_op jit(solution)/shard_map/ppermute | solution.py:485
  28.1 5.5 %collective-permute-start.11 = (f32[16,128]{1,0:T(8,128)S(1)}, f32[16,128]{1,0:T(8,128)S(1)}, u32[]{:S(2)}, u32[]{:S(2)}) collective-permute-start(f32[16,128]{1,0:T(8,128)S(1)} %join_shifts.1.refs_3_), channel_id=1, source_target_pairs={{0,12},{1,13},{2,14},{3,15},{4,8},{5,9},{6,10},{7,11},{8,4},{9,5},... | collective-permute-start | bytes 24584 | tf_op jit(solution)/shard_map/ppermute | solution.py:485
  29.6 4.0 %collective-permute-start.10 = (f32[16,128]{1,0:T(8,128)S(1)}, f32[16,128]{1,0:T(8,128)S(1)}, u32[]{:S(2)}, u32[]{:S(2)}) collective-permute-start(f32[16,128]{1,0:T(8,128)S(1)} %join_shifts.1.refs_3_), channel_id=1, source_target_pairs={{0,4},{1,5},{2,6},{3,7},{4,0},{5,1},{6,2},{7,3},{8,12},{9,13},{10,... | collective-permute-start | bytes 24584 | tf_op jit(solution)/shard_map/ppermute | solution.py:485

commit v5 on v4

--- a/solution.py
+++ b/solution.py
@@ -34,10 +34,16 @@
 
 def dot_rows(rows, weights, dims):
     high, low = split(rows)
-    weight_high, weight_low = weights
     count = rows.shape[0]
-    both = dot(jnp.concatenate([high, low], axis=0), weight_high, dims)
-    return both[:count] + both[count:] + dot(high, weight_low, dims)
+    left = jnp.concatenate(
+        [
+            jnp.concatenate([high, high], axis=1),
+            jnp.concatenate([low, jnp.zeros_like(low)], axis=1),
+        ],
+        axis=0,
+    )
+    both = dot(left, jnp.concatenate(weights, axis=dims[0][1][0]), dims)
+    return both[:count] + both[count:]
 
 
 def node_rows(edge, layers):
@@ -346,19 +352,80 @@
     )(*operands)
 
 
-def finish_kernel(strides, width, ways, *refs):
-    own_maps_ref, got_ref, swapped_ref, *refs = refs
-    order = own_maps_ref.shape[1]
-    shifts, refs = refs[:ways], refs[ways:]
+def local_kernel(strides, *refs):
     levels = []
     for stride in strides:
         levels.append((stride, *refs[:4]))
         refs = refs[4:]
-    (own_step_ref, other_step_ref, own_value_ref, other_value_ref, inverse_ref, inner_base, outer_base,
+    (own_step_ref, other_step_ref, own_value_ref, other_value_ref, inverse_ref, from_ahead_ref,
+     from_back_ref, rest_ref) = refs
+    cases, order = own_value_ref.shape
+    mine = lax.axis_index("row")
+    odd = (mine & 1) == 1
+    eye = (
+        lax.broadcasted_iota(jnp.int32, (order, order), 0)
+        == lax.broadcasted_iota(jnp.int32, (order, order), 1)
+    ).astype(f32)
+    none, last = jnp.zeros((order, order), f32), jnp.zeros((cases, order), f32)
+    ahead = jnp.concatenate([eye, none, last], axis=0)
+    back = jnp.concatenate([none, eye, last], axis=0)
+
+    def shifted(value):
+        return jnp.concatenate([none, none, value], axis=0)
+
+    for stride, own_maps, other_maps, own_shifts, other_shifts in levels[::-1]:
+        upper = (mine & stride) != 0
+        first_phi = jnp.where(upper, other_maps[:order, :], own_maps[:order, :])
+        second_maps = jnp.where(upper, own_maps[...], other_maps[...])
+        own, other = own_shifts[...], other_shifts[...]
+        first_shift = jnp.where(upper, other[:cases], own[:cases])
+        second_shift = jnp.where(upper, own[cases:], other[cases:])
+        middle = dot_rows(ahead, split(first_phi), NT) + shifted(first_shift)
+        inner = (
+            dot_rows(back, split(second_maps[:order]), NN)
+            - dot_rows(middle, split(second_maps[order:]), NN)
+            + shifted(second_shift)
+        )
+        ahead = jnp.where(upper, middle, ahead)
+        back = jnp.where(upper, back, inner)
+
+    own_step, other_step = own_step_ref[...], other_step_ref[...]
+    own_value, other_value = own_value_ref[...], other_value_ref[...]
+    first_step = split(jnp.where(odd, other_step, own_step))
+    second_step = split(jnp.where(odd, own_step, other_step))
+    first = dot_rows(ahead, first_step, NT) + shifted(jnp.where(odd, other_value, own_value))
+    second = dot_rows(first, second_step, NT) + shifted(jnp.where(odd, own_value, other_value))
+    inner = dot_rows(back - second, second_step, NN)
+    solved = dot_rows(
+        jnp.where(odd, second - back, first - inner), split(inverse_ref[...]), NN
+    )
+    from_ahead_ref[...] = solved[:order]
+    from_back_ref[...] = solved[order : 2 * order]
+    rest_ref[...] = solved[2 * order :]
+
+
+def local_call(strides, levels, leaf):
+    order = leaf[0].shape[0]
+    cases = leaf[2].shape[0]
+    square = jax.ShapeDtypeStruct((order, order), f32)
+    return pl.pallas_call(
+        functools.partial(local_kernel, strides),
+        out_shape=[square, square, jax.ShapeDtypeStruct((cases, order), f32)],
+        compiler_params=small(6),
+        cost_estimate=pl.CostEstimate(flops=10**9, bytes_accessed=10**6, transcendentals=0),
+        name="local_solution",
+    )(*levels, *leaf)
+
+
+def finish_kernel(width, ways, *refs):
+    own_maps_ref, got_ref, swapped_ref, *refs = refs
+    order = own_maps_ref.shape[1]
+    shifts, refs = refs[:ways], refs[ways:]
+    (from_ahead_ref, from_back_ref, rest_ref, inner_base, outer_base,
      labels_ref,
      weight_ref, updated_hbm, solution_hbm, all_maps, all_shifts, ahead_ref, back_ref, updated,
      solution, out_sems) = refs
-    cases = own_value_ref.shape[0]
+    cases = rest_ref.shape[0]
     comps, layers, section = labels_ref.shape
     mine = lax.axis_index("row")
     odd = (mine & 1) == 1
@@ -388,31 +455,10 @@
         back_ref[at - 1] = back
     ahead, back = ahead_ref[group], back_ref[group]
 
-    for stride, own_maps, other_maps, own_shifts, other_shifts in levels[::-1]:
-        upper = (mine & stride) != 0
-        first_phi = jnp.where(upper, other_maps[:order, :], own_maps[:order, :])
-        second_maps = jnp.where(upper, own_maps[...], other_maps[...])
-        own, other = own_shifts[...], other_shifts[...]
-        first_shift = jnp.where(upper, other[:cases], own[:cases])
-        second_shift = jnp.where(upper, own[cases:], other[cases:])
-        middle = dot_rows(ahead, split(first_phi), NT) + first_shift
-        inner = (
-            dot_rows(back, split(second_maps[:order]), NN)
-            - dot_rows(middle, split(second_maps[order:]), NN)
-            + second_shift
-        )
-        ahead = jnp.where(upper, middle, ahead)
-        back = jnp.where(upper, back, inner)
-
-    own_step, other_step = own_step_ref[...], other_step_ref[...]
-    own_value, other_value = own_value_ref[...], other_value_ref[...]
-    first_step = split(jnp.where(odd, other_step, own_step))
-    second_step = split(jnp.where(odd, own_step, other_step))
-    first = dot_rows(ahead, first_step, NT) + jnp.where(odd, other_value, own_value)
-    second = dot_rows(first, second_step, NT) + jnp.where(odd, own_value, other_value)
-    inner = dot_rows(back - second, second_step, NN)
-    solved = dot_rows(
-        jnp.where(odd, second - back, first - inner), split(inverse_ref[...]), NN
+    solved = (
+        dot_rows(ahead, split(from_ahead_ref[...]), NN)
+        + dot_rows(back, split(from_back_ref[...]), NN)
+        + rest_ref[...]
     )
     solution[...] = solved
     out_copies = [pltpu.make_async_copy(solution, solution_hbm, out_sems.at[comps])]
@@ -444,16 +490,16 @@
         copy.wait()
 
 
-def finish_call(strides, width, maps, shifts, levels, leaf, inner, outer, labels, weight):
+def finish_call(width, maps, shifts, local_maps, inner, outer, labels, weight):
     cases, comps, _, section = inner.shape
     layers = labels.shape[1]
     whole = (cases, comps, layers, section)
     order = maps[0].shape[1]
     ways = len(shifts)
     hbm, local = pl.BlockSpec(memory_space=pltpu.HBM), pl.BlockSpec(memory_space=pltpu.VMEM)
-    before = (*maps, *[shifts[hop] for hop in hop_order], *levels, *leaf)
+    before = (*maps, *[shifts[hop] for hop in hop_order], *local_maps)
     return pl.pallas_call(
-        functools.partial(finish_kernel, strides, width, ways),
+        functools.partial(finish_kernel, width, ways),
         in_specs=[local] * (len(before) + 4),
         out_specs=[hbm, hbm],
         out_shape=[
@@ -543,9 +589,9 @@
     all_maps = [maps, gathered, swap(gathered, 1)]
     all_shifts = [shifts] + [swap(shifts, hop * width) for hop in range(1, ways)]
     leaf = (step, other_step, value, other_value, diag_inverse)
+    local_maps = local_call(tuple(strides), levels, leaf)
     updated, solution_rows = finish_call(
-        tuple(strides), width, all_maps, all_shifts, levels, leaf, inner_base, outer_base, aggregate,
-        basis_weight,
+        width, all_maps, all_shifts, local_maps, inner_base, outer_base, aggregate, basis_weight
     )
     return updated, solution_rows.T
 

time: 37 us -> 36.6 us (0.989)
  waiting for transfers between devices: 7.51 us -> 6.37 us
  Pallas kernels: 12.1 us -> 12.7 us
    ppermute x12, waiting for transfers between devices: 7.51 us -> 6.37 us  [swap(): return lax.ppermute(value, 'row', [(i, i ^ mask) for i in range(count)])]
    pallas_call x1 -> x2, Pallas kernels: 3.24 us -> 3.92 us  [the longest x1 2.82 us: finish_call(): pl.pallas_call(functools.partial(finish_kernel, width, ways), in_specs=[l...]
  transfers between devices with their start and end apart: 13 -> 13, of which waited for: 5 -> 4; matrix products, arithmetic and copies ran while one was open for 0% -> 0% of each run, Pallas kernels for 19% -> 22%
where the time goes in v5:
time: 36.6 us; the launch traced here: 36.4 us
  starting transfers between devices  16.4 us (45%)
  Pallas kernels  12.7 us (35%)
  waiting for transfers between devices  6.37 us (17%)
  between operations  0.84 us (2%)
    ppermute x12, starting transfers between devices, swap(): return lax.ppermute(value, 'row', [(i, i ^ mask) for i in range(count)])  15.8 us
    ppermute x12, waiting for transfers between devices, swap(): return lax.ppermute(value, 'row', [(i, i ^ mask) for i in range(count)])  6.37 us
    pallas_call x2, Pallas kernels, residual_call(): pl.pallas_call(kernel, in_specs=[local] * len(operands), out_specs=[local...  6.33 us
    pallas_call x1, Pallas kernels, finish_call(): pl.pallas_call(functools.partial(finish_kernel, width, ways), in_specs=[l...  2.82 us
    pallas_call x1, Pallas kernels, start_call(): pl.pallas_call(start_kernel, in_specs=[pl.BlockSpec(memory_space=pltpu.HB...  1.38 us
    pallas_call x1, Pallas kernels, local_call(): pl.pallas_call(functools.partial(local_kernel, strides), out_shape=[squar...  1.1 us
    pallas_call x2, Pallas kernels, maps_call(): pl.pallas_call(kernel, out_shape=[jax.ShapeDtypeStruct((2 * order, order)...  0.76 us
  transfers between devices with their start and end apart: 13, of which 4 were waited for; matrix products, arithmetic and copies ran while one was open for 0% of the time, Pallas kernels for 22%

profile of v5, /device:TPU:0, one launch (start us, length us, event | category | flops | bytes accessed | tf_op | source)
XLA Modules:
  0.0 36.4 jit_solution(8324327105112982977)
XLA Ops:
  0.6 1.4 %start.1 = (f32[128,128]{1,0:T(8,128)S(1)}, f32[288,128]{1,0:T(8,128)S(1)}, f32[288,128]{1,0:T(8,128)S(1)}) custom-call(f32[128,128]{1,0:T(8,128)} %refs_8_.1, f32[128,128]{1,0:T(8,128)} %sub_hbm.1, f32[8,3,32,512]{3,2,1,0:T(8,128)} %disp_ref.3), custom_call_target="tpu_custom_call" | custom-call | flops 10000000000 | bytes 1000000 | tf_op jit(solution)/shard_map/start/pallas_call | solution.py:260
  2.0 0.0 copy-start
  2.0 0.0 copy-start.1
  2.0 0.0 copy-start.3
  2.1 0.0 copy-start.4
  2.1 0.0 copy-start.5
  2.1 0.5 %collective-permute-start = (f32[128,128]{1,0:T(8,128)S(1)}, f32[128,128]{1,0:T(8,128)S(1)}, u32[]{:S(2)}, u32[]{:S(2)}) collective-permute-start(f32[128,128]{1,0:T(8,128)S(1)} %get-tuple-element.26.own_ref.own_step_ref.refs_4_), channel_id=1, source_target_pairs={{0,1},{1,0},{2,3},{3,2},{4,5},{5,4},{6,7},{7,6},{8,9},{9,8},{10,11... | collective-permute-start | bytes 196616 | tf_op jit(solution)/shard_map/ppermute | solution.py:531
  2.6 0.9 %collective-permute-done.other_ref.other_step_ref.refs_5_ = f32[128,128]{1,0:T(8,128)S(1)} collective-permute-done((f32[128,128]{1,0:T(8,128)S(1)}, f32[128,128]{1,0:T(8,128)S(1)}, u32[]{:S(2)}, u32[]{:S(2)}) %collective-permute-start) | collective-permute-done | bytes 65568 | tf_op jit(solution)/shard_map/ppermute | solution.py:531
  3.5 0.0 copy-start.2
  3.5 0.4 %pair_maps.1 = (f32[256,128]{1,0:T(8,128)S(1)}, f32[128,128]{1,0:T(8,128)S(1)}) custom-call(f32[128,128]{1,0:T(8,128)S(1)} %get-tuple-element.26.own_ref.own_step_ref.refs_4_, f32[128,128]{1,0:T(8,128)S(1)} %collective-permute-done.other_ref.other_step_ref.refs_5_), custom_call_target="tpu_custom_call" | custom-call | flops 10000000000 | bytes 1000000 | tf_op jit(solution)/shard_map/pair_maps/pallas_call | solution.py:304
  3.9 2.9 %collective-permute-start.1 = (f32[256,128]{1,0:T(8,128)S(1)}, f32[256,128]{1,0:T(8,128)S(1)}, u32[]{:S(2)}, u32[]{:S(2)}) collective-permute-start(f32[256,128]{1,0:T(8,128)S(1)} %get-tuple-element.27.own_ref.maps_ref.own_maps_ref.refs_0_), channel_id=1, source_target_pairs={{0,2},{1,3},{2,0},{3,1},{4,6},{5,7},{6,4},{7,5},{8,10},{9,11},{10,... | collective-permute-start | bytes 393224 | tf_op jit(solution)/shard_map/ppermute | solution.py:531
  6.8 0.0 collective-permute-start.2
  6.8 0.7 %collective-permute-start.3 = (f32[288,128]{1,0:T(8,128)S(1)}, f32[288,128]{1,0:T(8,128)S(1)}, u32[]{:S(2)}, u32[]{:S(2)}) collective-permute-start(f32[288,128]{1,0:T(8,128)S(1)} %get-tuple-element.32), channel_id=1, source_target_pairs={{1,2},{2,1},{3,4},{4,3},{5,6},{6,5},{7,8},{8,7},{9,10},{10,9},{11,... | collective-permute-start | bytes 442376 | tf_op jit(solution)/shard_map/ppermute | solution.py:536
  7.5 0.0 copy-done
  7.5 0.0 copy-done.1
  7.5 0.0 copy-done.3
  7.5 0.0 copy-done.4
  7.5 0.0 copy-done.5
  7.5 0.0 copy-done.2
  7.5 3.6 %inner_residual.1 = (f32[8,3,16,512]{3,2,1,0:T(8,128)S(1)}, f32[3,8,16,512]{3,2,1,0:T(8,128)S(1)}, f32[3,8,512]{2,1,0:T(8,128)S(1)}, f32[32,64]{1,0:T(8,128)S(1)}) custom-call(f32[8,3,32,512]{3,2,1,0:T(8,128)S(1)} %copy-done, f32[8,3,32,512]{3,2,1,0:T(8,128)S(1)} %copy-done.1, f32[3,512,512]{2,1,0:T(8,128)S(1)} %copy-done.2, f32[32,512]{1,0:T(8,128)S(1)} %copy-done.5, ...), custom_call_target="tpu_custom_call" | custom-call | flops 603979776 | bytes 3145728 | tf_op jit(solution)/shard_map/inner_residual/pallas_call | solution.py:197
  11.2 0.0 collective-permute-done.1.other_ref.other_maps_ref.refs_1_
  11.2 0.0 copy-start.6
  11.2 0.4 join_maps.1
  11.6 5.4 %collective-permute-start.8 = (f32[128,128]{1,0:T(8,128)S(1)}, f32[128,128]{1,0:T(8,128)S(1)}, u32[]{:S(2)}, u32[]{:S(2)}) collective-permute-start(f32[128,128]{1,0:T(8,128)S(1)} %get-tuple-element.39), channel_id=1, source_target_pairs={{0,12},{1,13},{2,14},{3,15},{4,8},{5,9},{6,10},{7,11},{8,4},{9,5},... | collective-permute-start | bytes 196616 | tf_op jit(solution)/shard_map/ppermute | solution.py:531
  17.0 0.0 collective-permute-start.7
  17.0 0.6 %collective-permute-start.6 = (f32[128,128]{1,0:T(8,128)S(1)}, f32[128,128]{1,0:T(8,128)S(1)}, u32[]{:S(2)}, u32[]{:S(2)}) collective-permute-start(f32[128,128]{1,0:T(8,128)S(1)} %get-tuple-element.39), channel_id=1, source_target_pairs={{0,4},{1,5},{2,6},{3,7},{4,0},{5,1},{6,2},{7,3},{8,12},{9,13},{10,... | collective-permute-start | bytes 196616 | tf_op jit(solution)/shard_map/ppermute | solution.py:531
  17.7 0.0 collective-permute-done.2.near_ref
  17.7 0.0 collective-permute-done.3.far_ref
  17.7 0.0 copy-done.6
  17.7 2.7 %outer_residual.1 = (f32[8,3,16,512]{3,2,1,0:T(8,128)S(1)}, f32[8,128]{1,0:T(8,128)S(1)}) custom-call(f32[8,3,32,512]{3,2,1,0:T(8,128)S(1)} %copy-done, f32[8,3,32,512]{3,2,1,0:T(8,128)S(1)} %copy-done.1, f32[32,512]{1,0:T(8,128)S(1)} %copy-done.5, s32[3,32,512]{2,1,0:T(8,128)S(1)} %copy-done.3, f32[3,32,512]{2,1,0:T(8,128)S(1)} %copy-done.4, ...), custom_call_target="tpu_custom_call" | custom-call | flops 603979776 | bytes 3145728 | tf_op jit(solution)/shard_map/outer_residual/pallas_call | solution.py:197
  20.3 0.0 collective-permute-start.4
  20.4 1.2 %collective-permute-done.4.other_ref.refs_7_ = f32[8,128]{1,0:T(8,128)S(1)} collective-permute-done((f32[8,128]{1,0:T(8,128)S(1)}, f32[8,128]{1,0:T(8,128)S(1)}, u32[]{:S(2)}, u32[]{:S(2)}) %collective-permute-start.4) | collective-permute-done | bytes 4128 | tf_op jit(solution)/shard_map/ppermute | solution.py:531
  21.5 0.2 pair_shifts.1.own_ref.refs_2_
  21.7 1.8 %collective-permute-start.5 = (f32[16,128]{1,0:T(8,128)S(1)}, f32[16,128]{1,0:T(8,128)S(1)}, u32[]{:S(2)}, u32[]{:S(2)}) collective-permute-start(f32[16,128]{1,0:T(8,128)S(1)} %pair_shifts.1.own_ref.refs_2_), channel_id=1, source_target_pairs={{0,2},{1,3},{2,0},{3,1},{4,6},{5,7},{6,4},{7,5},{8,10},{9,11},{10,... | collective-permute-start | bytes 24584 | tf_op jit(solution)/shard_map/ppermute | solution.py:531
  23.5 1.9 %collective-permute-done.5.other_ref.refs_3_ = f32[16,128]{1,0:T(8,128)S(1)} collective-permute-done((f32[16,128]{1,0:T(8,128)S(1)}, f32[16,128]{1,0:T(8,128)S(1)}, u32[]{:S(2)}, u32[]{:S(2)}) %collective-permute-start.5) | collective-permute-done | bytes 8224 | tf_op jit(solution)/shard_map/ppermute | solution.py:531
  25.4 0.2 join_shifts.1.refs_3_
  25.6 0.0 collective-permute-done.8
  25.6 0.0 collective-permute-done.7
  25.6 0.0 collective-permute-done.6
  25.6 0.1 collective-permute-start.9
  25.7 2.4 %collective-permute-start.12 = (f32[16,128]{1,0:T(8,128)S(1)}, f32[16,128]{1,0:T(8,128)S(1)}, u32[]{:S(2)}, u32[]{:S(2)}) collective-permute-start(f32[16,128]{1,0:T(8,128)S(1)} %join_shifts.1.refs_3_), channel_id=1, source_target_pairs={{0,8},{1,9},{2,10},{3,11},{4,12},{5,13},{6,14},{7,15},{8,0},{9,1},... | collective-permute-start | bytes 24584 | tf_op jit(solution)/shard_map/ppermute | solution.py:531
  28.1 1.5 %collective-permute-start.11 = (f32[16,128]{1,0:T(8,128)S(1)}, f32[16,128]{1,0:T(8,128)S(1)}, u32[]{:S(2)}, u32[]{:S(2)}) collective-permute-start(f32[16,128]{1,0:T(8,128)S(1)} %join_shifts.1.refs_3_), channel_id=1, source_target_pairs={{0,12},{1,13},{2,14},{3,15},{4,8},{5,9},{6,10},{7,11},{8,4},{9,5},... | collective-permute-start | bytes 24584 | tf_op jit(solution)/shard_map/ppermute | solution.py:531
  29.6 0.5 %collective-permute-start.10 = (f32[16,128]{1,0:T(8,128)S(1)}, f32[16,128]{1,0:T(8,128)S(1)}, u32[]{:S(2)}, u32[]{:S(2)}) collective-permute-start(f32[16,128]{1,0:T(8,128)S(1)} %join_shifts.1.refs_3_), channel_id=1, source_target_pairs={{0,4},{1,5},{2,6},{3,7},{4,0},{5,1},{6,2},{7,3},{8,12},{9,13},{10,... | collective-permute-start | bytes 24584 | tf_op jit(solution)/shard_map/ppermute | solution.py:531
  30.1 1.1 %local_solution.1 = (f32[128,128]{1,0:T(8,128)S(1)}, f32[128,128]{1,0:T(8,128)S(1)}, f32[8,128]{1,0:T(8,128)S(1)}) custom-call(f32[256,128]{1,0:T(8,128)S(1)} %get-tuple-element.27.own_ref.maps_ref.own_maps_ref.refs_0_, f32[256,128]{1,0:T(8,128)S(1)} %collective-permute-done.1.other_ref.other_maps_ref.refs_1_, f32[16,128]{1,0:T(8,128)S(1)} %pair_shifts.1.own_ref.refs_2_, ...), custom_call_target="tpu_custom_call" | custom-call | flops 1000000000 | bytes 1000000 | tf_op jit(solution)/shard_map/local_solution/pallas_call | solution.py:411
  31.2 0.0 collective-permute-done.12.refs_6_
  31.2 2.4 %collective-permute-done.11.refs_5_ = f32[16,128]{1,0:T(8,128)S(1)} collective-permute-done((f32[16,128]{1,0:T(8,128)S(1)}, f32[16,128]{1,0:T(8,128)S(1)}, u32[]{:S(2)}, u32[]{:S(2)}) %collective-permute-start.11) | collective-permute-done | bytes 8224 | tf_op jit(solution)/shard_map/ppermute | solution.py:531
  33.6 0.0 collective-permute-done.10.refs_4_
  33.6 0.0 collective-permute-done.9.refs_2_
  33.6 2.8 %finish.1 = (f32[8,3,32,512]{3,2,1,0:T(8,128)}, f32[8,128]{1,0:T(8,128)}) custom-call(f32[256,128]{1,0:T(8,128)S(1)} %get-tuple-element.30.refs_0_, f32[384,128]{1,0:T(8,128)S(1)} %constant_dynamic-update-slice_fusion.refs_1_, f32[384,128]{1,0:T(8,128)S(1)} %collective-permute-done.9.refs_2_, f32[16,128]{1,0:T(8,128)S(1)} %join_shifts.1.refs_3_, ...), custom_call_target="tpu_custom_call" | custom-call | tf_op jit(solution)/shard_map/finish/pallas_call | solution.py:501
  (3 shorter events, 0.0 us)
Async XLA Ops:
  2.0 5.5 %copy-start = (f32[8,3,32,512]{3,2,1,0:T(8,128)S(1)}, f32[8,3,32,512]{3,2,1,0:T(8,128)}, u32[]{:S(2)}) copy-start(f32[8,3,32,512]{3,2,1,0:T(8,128)} %disp_ref.3) | copy-start | bytes 4718596
  2.0 5.5 %copy-start.1 = (f32[8,3,32,512]{3,2,1,0:T(8,128)S(1)}, f32[8,3,32,512]{3,2,1,0:T(8,128)}, u32[]{:S(2)}) copy-start(f32[8,3,32,512]{3,2,1,0:T(8,128)} %loads_ref.3) | copy-start | bytes 4718596
  2.0 5.5 %copy-start.3 = (s32[3,32,512]{2,1,0:T(8,128)S(1)}, s32[3,32,512]{2,1,0:T(8,128)}, u32[]{:S(2)}) copy-start(s32[3,32,512]{2,1,0:T(8,128)} %refs_12_.1) | copy-start | bytes 589828
  2.1 5.5 %copy-start.4 = (f32[3,32,512]{2,1,0:T(8,128)S(1)}, f32[3,32,512]{2,1,0:T(8,128)}, u32[]{:S(2)}) copy-start(f32[3,32,512]{2,1,0:T(8,128)} %refs_13_.1) | copy-start | bytes 589828
  2.1 5.5 %copy-start.5 = (f32[32,512]{1,0:T(8,128)S(1)}, f32[32,512]{1,0:T(8,128)}, u32[]{:S(2)}) copy-start(f32[32,512]{1,0:T(8,128)} %modulus_ref.3) | copy-start | bytes 196612
  2.1 1.4 %collective-permute-start = (f32[128,128]{1,0:T(8,128)S(1)}, f32[128,128]{1,0:T(8,128)S(1)}, u32[]{:S(2)}, u32[]{:S(2)}) collective-permute-start(f32[128,128]{1,0:T(8,128)S(1)} %get-tuple-element.26.own_ref.own_step_ref.refs_4_), channel_id=1, source_target_pairs={{0,1},{1,0},{2,3},{3,2},{4,5},{5,4},{6,7},{7,6},{8,9},{9,8},{10,11... | collective-permute-start | bytes 196616 | tf_op jit(solution)/shard_map/ppermute | solution.py:531
  3.5 4.0 %copy-start.2 = (f32[3,512,512]{2,1,0:T(8,128)S(1)}, f32[3,512,512]{2,1,0:T(8,128)}, u32[]{:S(2)}) copy-start(f32[3,512,512]{2,1,0:T(8,128)} %section_ref.1) | copy-start | bytes 9437188
  3.9 7.3 %collective-permute-start.1 = (f32[256,128]{1,0:T(8,128)S(1)}, f32[256,128]{1,0:T(8,128)S(1)}, u32[]{:S(2)}, u32[]{:S(2)}) collective-permute-start(f32[256,128]{1,0:T(8,128)S(1)} %get-tuple-element.27.own_ref.maps_ref.own_maps_ref.refs_0_), channel_id=1, source_target_pairs={{0,2},{1,3},{2,0},{3,1},{4,6},{5,7},{6,4},{7,5},{8,10},{9,11},{10,... | collective-permute-start | bytes 393224 | tf_op jit(solution)/shard_map/ppermute | solution.py:531
  6.8 10.9 %collective-permute-start.2 = (f32[288,128]{1,0:T(8,128)S(1)}, f32[288,128]{1,0:T(8,128)S(1)}, u32[]{:S(2)}, u32[]{:S(2)}) collective-permute-start(f32[288,128]{1,0:T(8,128)S(1)} %get-tuple-element.31), channel_id=1, source_target_pairs={{0,1},{1,0},{2,3},{3,2},{4,5},{5,4},{6,7},{7,6},{8,9},{9,8},{10,11... | collective-permute-start | bytes 442376 | tf_op jit(solution)/shard_map/ppermute | solution.py:531
  6.8 10.9 %collective-permute-start.3 = (f32[288,128]{1,0:T(8,128)S(1)}, f32[288,128]{1,0:T(8,128)S(1)}, u32[]{:S(2)}, u32[]{:S(2)}) collective-permute-start(f32[288,128]{1,0:T(8,128)S(1)} %get-tuple-element.32), channel_id=1, source_target_pairs={{1,2},{2,1},{3,4},{4,3},{5,6},{6,5},{7,8},{8,7},{9,10},{10,9},{11,... | collective-permute-start | bytes 442376 | tf_op jit(solution)/shard_map/ppermute | solution.py:536
  11.2 6.5 %copy-start.6 = (f32[128,128]{1,0:T(8,128)S(1)}, f32[128,128]{1,0:T(8,128)}, u32[]{:S(2)}) copy-start(f32[128,128]{1,0:T(8,128)} %refs_8_.1) | copy-start | bytes 196612
  11.6 14.0 %collective-permute-start.8 = (f32[128,128]{1,0:T(8,128)S(1)}, f32[128,128]{1,0:T(8,128)S(1)}, u32[]{:S(2)}, u32[]{:S(2)}) collective-permute-start(f32[128,128]{1,0:T(8,128)S(1)} %get-tuple-element.39), channel_id=1, source_target_pairs={{0,12},{1,13},{2,14},{3,15},{4,8},{5,9},{6,10},{7,11},{8,4},{9,5},... | collective-permute-start | bytes 196616 | tf_op jit(solution)/shard_map/ppermute | solution.py:531
  17.0 8.6 %collective-permute-start.7 = (f32[128,128]{1,0:T(8,128)S(1)}, f32[128,128]{1,0:T(8,128)S(1)}, u32[]{:S(2)}, u32[]{:S(2)}) collective-permute-start(f32[128,128]{1,0:T(8,128)S(1)} %get-tuple-element.39), channel_id=1, source_target_pairs={{0,8},{1,9},{2,10},{3,11},{4,12},{5,13},{6,14},{7,15},{8,0},{9,1},... | collective-permute-start | bytes 196616 | tf_op jit(solution)/shard_map/ppermute | solution.py:531
  17.0 8.6 %collective-permute-start.6 = (f32[128,128]{1,0:T(8,128)S(1)}, f32[128,128]{1,0:T(8,128)S(1)}, u32[]{:S(2)}, u32[]{:S(2)}) collective-permute-start(f32[128,128]{1,0:T(8,128)S(1)} %get-tuple-element.39), channel_id=1, source_target_pairs={{0,4},{1,5},{2,6},{3,7},{4,0},{5,1},{6,2},{7,3},{8,12},{9,13},{10,... | collective-permute-start | bytes 196616 | tf_op jit(solution)/shard_map/ppermute | solution.py:531
  20.3 1.2 %collective-permute-start.4 = (f32[8,128]{1,0:T(8,128)S(1)}, f32[8,128]{1,0:T(8,128)S(1)}, u32[]{:S(2)}, u32[]{:S(2)}) collective-permute-start(f32[8,128]{1,0:T(8,128)S(1)} %get-tuple-element.36.own_ref.refs_6_), channel_id=1, source_target_pairs={{0,1},{1,0},{2,3},{3,2},{4,5},{5,4},{6,7},{7,6},{8,9},{9,8},{10,11... | collective-permute-start | bytes 12296 | tf_op jit(solution)/shard_map/ppermute | solution.py:531
  21.7 3.7 %collective-permute-start.5 = (f32[16,128]{1,0:T(8,128)S(1)}, f32[16,128]{1,0:T(8,128)S(1)}, u32[]{:S(2)}, u32[]{:S(2)}) collective-permute-start(f32[16,128]{1,0:T(8,128)S(1)} %pair_shifts.1.own_ref.refs_2_), channel_id=1, source_target_pairs={{0,2},{1,3},{2,0},{3,1},{4,6},{5,7},{6,4},{7,5},{8,10},{9,11},{10,... | collective-permute-start | bytes 24584 | tf_op jit(solution)/shard_map/ppermute | solution.py:531
  25.6 7.9 %collective-permute-start.9 = (f32[384,128]{1,0:T(8,128)S(1)}, f32[384,128]{1,0:T(8,128)S(1)}, u32[]{:S(2)}, u32[]{:S(2)}) collective-permute-start(f32[384,128]{1,0:T(8,128)S(1)} %constant_dynamic-update-slice_fusion.refs_1_), channel_id=1, source_target_pairs={{0,1},{1,0},{2,3},{3,2},{4,5},{5,4},{6,7},{7,6},{8,9},{9,8},{10,11... | collective-permute-start | bytes 589832 | tf_op jit(solution)/shard_map/ppermute | solution.py:531
  25.7 5.5 %collective-permute-start.12 = (f32[16,128]{1,0:T(8,128)S(1)}, f32[16,128]{1,0:T(8,128)S(1)}, u32[]{:S(2)}, u32[]{:S(2)}) collective-permute-start(f32[16,128]{1,0:T(8,128)S(1)} %join_shifts.1.refs_3_), channel_id=1, source_target_pairs={{0,8},{1,9},{2,10},{3,11},{4,12},{5,13},{6,14},{7,15},{8,0},{9,1},... | collective-permute-start | bytes 24584 | tf_op jit(solution)/shard_map/ppermute | solution.py:531
  28.1 5.5 %collective-permute-start.11 = (f32[16,128]{1,0:T(8,128)S(1)}, f32[16,128]{1,0:T(8,128)S(1)}, u32[]{:S(2)}, u32[]{:S(2)}) collective-permute-start(f32[16,128]{1,0:T(8,128)S(1)} %join_shifts.1.refs_3_), channel_id=1, source_target_pairs={{0,12},{1,13},{2,14},{3,15},{4,8},{5,9},{6,10},{7,11},{8,4},{9,5},... | collective-permute-start | bytes 24584 | tf_op jit(solution)/shard_map/ppermute | solution.py:531
  29.6 4.0 %collective-permute-start.10 = (f32[16,128]{1,0:T(8,128)S(1)}, f32[16,128]{1,0:T(8,128)S(1)}, u32[]{:S(2)}, u32[]{:S(2)}) collective-permute-start(f32[16,128]{1,0:T(8,128)S(1)} %join_shifts.1.refs_3_), channel_id=1, source_target_pairs={{0,4},{1,5},{2,6},{3,7},{4,0},{5,1},{6,2},{7,3},{8,12},{9,13},{10,... | collective-permute-start | bytes 24584 | tf_op jit(solution)/shard_map/ppermute | solution.py:531

commit v6 on v5

--- a/solution.py
+++ b/solution.py
@@ -435,8 +435,8 @@
     for hop in range(1, ways):
         part = slice((hop - 1) * order, hop * order)
         got, swapped = got_ref[part, :], swapped_ref[part, :]
-        all_maps[group ^ hop, :order] = jnp.where(odd, swapped, got)
-        all_maps[group ^ hop, order:] = jnp.where(odd, got, swapped)
+        all_maps[group ^ hop, :order] = jnp.where(odd, got, swapped)
+        all_maps[group ^ hop, order:] = jnp.where(odd, swapped, got)
     for hop in range(ways):
         all_shifts[group ^ hop_order[hop]] = shifts[hop][...]
 
@@ -557,7 +557,7 @@
     strides, joins = [], []
     stride = 2
     while stride < width:
-        other_maps = swap(maps, stride)
+        other_maps = swap(maps, stride ^ 1)
         if not strides:
             other_maps, total = lax.optimization_barrier((other_maps, total))
         joined, mixed, half = maps_call(
@@ -567,7 +567,7 @@
         joins.append((maps, other_maps, mixed))
         maps = joined
         stride *= 2
-    halves = [swap(half, hop * width) for hop in range(1, ways)]
+    halves = [swap(half, hop * width ^ 1) for hop in range(1, ways)]
     outer_base, value = residual_call(
         outer_kernel,
         True,
@@ -579,7 +579,7 @@
     shifts = shifts_call(pair_shifts_kernel, "pair_shifts", cases, value, other_value, *pair_operands)
     levels = []
     for stride, (own_maps, other_maps, mixed) in zip(strides, joins):
-        other_shifts = swap(shifts, stride)
+        other_shifts = swap(shifts, stride ^ 1)
         levels += [own_maps, other_maps, shifts, other_shifts]
         shifts = shifts_call(
             functools.partial(join_shifts_kernel, stride), "join_shifts", cases,
@@ -587,7 +587,7 @@
         )
     gathered = jnp.concatenate(lax.optimization_barrier((shifts, *halves))[1:], axis=0)
     all_maps = [maps, gathered, swap(gathered, 1)]
-    all_shifts = [shifts] + [swap(shifts, hop * width) for hop in range(1, ways)]
+    all_shifts = [shifts] + [swap(shifts, hop * width ^ 1) for hop in range(1, ways)]
     leaf = (step, other_step, value, other_value, diag_inverse)
     local_maps = local_call(tuple(strides), levels, leaf)
     updated, solution_rows = finish_call(

time: 36.6 us -> 35 us (0.956)
  waiting for transfers between devices: 6.37 us -> 5.18 us
    ppermute x12, waiting for transfers between devices: 6.37 us -> 5.18 us  [swap(): return lax.ppermute(value, 'row', [(i, i ^ mask) for i in range(count)])]
  transfers between devices with their start and end apart: 13 -> 13, of which waited for: 4 -> 4; matrix products, arithmetic and copies ran while one was open for 0% -> 0% of each run, Pallas kernels for 22% -> 23%
where the time goes in v6:
time: 35 us; the launch traced here: 34.9 us
  starting transfers between devices  16.1 us (46%)
  Pallas kernels  12.7 us (36%)
  waiting for transfers between devices  5.18 us (15%)
  between operations  0.83 us (2%)
    ppermute x12, starting transfers between devices, swap(): return lax.ppermute(value, 'row', [(i, i ^ mask) for i in range(count)])  15.5 us
    pallas_call x2, Pallas kernels, residual_call(): pl.pallas_call(kernel, in_specs=[local] * len(operands), out_specs=[local...  6.32 us
    ppermute x12, waiting for transfers between devices, swap(): return lax.ppermute(value, 'row', [(i, i ^ mask) for i in range(count)])  5.18 us
    pallas_call x1, Pallas kernels, finish_call(): pl.pallas_call(functools.partial(finish_kernel, width, ways), in_specs=[l...  2.82 us
    pallas_call x1, Pallas kernels, start_call(): pl.pallas_call(start_kernel, in_specs=[pl.BlockSpec(memory_space=pltpu.HB...  1.38 us
    pallas_call x1, Pallas kernels, local_call(): pl.pallas_call(functools.partial(local_kernel, strides), out_shape=[squar...  1.1 us
    pallas_call x2, Pallas kernels, maps_call(): pl.pallas_call(kernel, out_shape=[jax.ShapeDtypeStruct((2 * order, order)...  0.76 us
  transfers between devices with their start and end apart: 13, of which 4 were waited for; matrix products, arithmetic and copies ran while one was open for 0% of the time, Pallas kernels for 23%

profile of v6, /device:TPU:0, one launch (start us, length us, event | category | flops | bytes accessed | tf_op | source)
XLA Modules:
  0.0 34.9 jit_solution(16262192673496832487)
XLA Ops:
  0.6 1.4 %start.1 = (f32[128,128]{1,0:T(8,128)S(1)}, f32[288,128]{1,0:T(8,128)S(1)}, f32[288,128]{1,0:T(8,128)S(1)}) custom-call(f32[128,128]{1,0:T(8,128)} %refs_8_.1, f32[128,128]{1,0:T(8,128)} %sub_hbm.1, f32[8,3,32,512]{3,2,1,0:T(8,128)} %disp_ref.3), custom_call_target="tpu_custom_call" | custom-call | flops 10000000000 | bytes 1000000 | tf_op jit(solution)/shard_map/start/pallas_call | solution.py:260
  2.0 0.0 copy-start
  2.0 0.0 copy-start.1
  2.0 0.0 copy-start.3
  2.1 0.0 copy-start.4
  2.1 0.0 copy-start.5
  2.1 0.5 %collective-permute-start = (f32[128,128]{1,0:T(8,128)S(1)}, f32[128,128]{1,0:T(8,128)S(1)}, u32[]{:S(2)}, u32[]{:S(2)}) collective-permute-start(f32[128,128]{1,0:T(8,128)S(1)} %get-tuple-element.26.own_ref.own_step_ref.refs_4_), channel_id=1, source_target_pairs={{0,1},{1,0},{2,3},{3,2},{4,5},{5,4},{6,7},{7,6},{8,9},{9,8},{10,11... | collective-permute-start | bytes 196616 | tf_op jit(solution)/shard_map/ppermute | solution.py:531
  2.6 0.9 %collective-permute-done.other_ref.other_step_ref.refs_5_ = f32[128,128]{1,0:T(8,128)S(1)} collective-permute-done((f32[128,128]{1,0:T(8,128)S(1)}, f32[128,128]{1,0:T(8,128)S(1)}, u32[]{:S(2)}, u32[]{:S(2)}) %collective-permute-start) | collective-permute-done | bytes 65568 | tf_op jit(solution)/shard_map/ppermute | solution.py:531
  3.5 0.0 copy-start.2
  3.5 0.4 %pair_maps.1 = (f32[256,128]{1,0:T(8,128)S(1)}, f32[128,128]{1,0:T(8,128)S(1)}) custom-call(f32[128,128]{1,0:T(8,128)S(1)} %get-tuple-element.26.own_ref.own_step_ref.refs_4_, f32[128,128]{1,0:T(8,128)S(1)} %collective-permute-done.other_ref.other_step_ref.refs_5_), custom_call_target="tpu_custom_call" | custom-call | flops 10000000000 | bytes 1000000 | tf_op jit(solution)/shard_map/pair_maps/pallas_call | solution.py:304
  3.9 2.7 %collective-permute-start.1 = (f32[256,128]{1,0:T(8,128)S(1)}, f32[256,128]{1,0:T(8,128)S(1)}, u32[]{:S(2)}, u32[]{:S(2)}) collective-permute-start(f32[256,128]{1,0:T(8,128)S(1)} %get-tuple-element.27.own_ref.maps_ref.own_maps_ref.refs_0_), channel_id=1, source_target_pairs={{0,3},{1,2},{2,1},{3,0},{4,7},{5,6},{6,5},{7,4},{8,11},{9,10},{10,... | collective-permute-start | bytes 393224 | tf_op jit(solution)/shard_map/ppermute | solution.py:531
  6.6 0.4 %collective-permute-start.2 = (f32[288,128]{1,0:T(8,128)S(1)}, f32[288,128]{1,0:T(8,128)S(1)}, u32[]{:S(2)}, u32[]{:S(2)}) collective-permute-start(f32[288,128]{1,0:T(8,128)S(1)} %get-tuple-element.31), channel_id=1, source_target_pairs={{0,1},{1,0},{2,3},{3,2},{4,5},{5,4},{6,7},{7,6},{8,9},{9,8},{10,11... | collective-permute-start | bytes 442376 | tf_op jit(solution)/shard_map/ppermute | solution.py:531
  6.9 0.7 %collective-permute-start.3 = (f32[288,128]{1,0:T(8,128)S(1)}, f32[288,128]{1,0:T(8,128)S(1)}, u32[]{:S(2)}, u32[]{:S(2)}) collective-permute-start(f32[288,128]{1,0:T(8,128)S(1)} %get-tuple-element.32), channel_id=1, source_target_pairs={{1,2},{2,1},{3,4},{4,3},{5,6},{6,5},{7,8},{8,7},{9,10},{10,9},{11,... | collective-permute-start | bytes 442376 | tf_op jit(solution)/shard_map/ppermute | solution.py:536
  7.6 0.0 copy-done
  7.6 0.0 copy-done.1
  7.6 0.0 copy-done.3
  7.6 0.0 copy-done.4
  7.6 0.0 copy-done.5
  7.6 0.0 copy-done.2
  7.6 3.6 %inner_residual.1 = (f32[8,3,16,512]{3,2,1,0:T(8,128)S(1)}, f32[3,8,16,512]{3,2,1,0:T(8,128)S(1)}, f32[3,8,512]{2,1,0:T(8,128)S(1)}, f32[32,64]{1,0:T(8,128)S(1)}) custom-call(f32[8,3,32,512]{3,2,1,0:T(8,128)S(1)} %copy-done, f32[8,3,32,512]{3,2,1,0:T(8,128)S(1)} %copy-done.1, f32[3,512,512]{2,1,0:T(8,128)S(1)} %copy-done.2, f32[32,512]{1,0:T(8,128)S(1)} %copy-done.5, ...), custom_call_target="tpu_custom_call" | custom-call | flops 603979776 | bytes 3145728 | tf_op jit(solution)/shard_map/inner_residual/pallas_call | solution.py:197
  11.3 0.0 collective-permute-done.1.other_ref.other_maps_ref.refs_1_
  11.3 0.0 copy-start.6
  11.3 0.4 %join_maps.1 = (f32[256,128]{1,0:T(8,128)S(1)}, f32[128,128]{1,0:T(8,128)S(1)}, f32[128,128]{1,0:T(8,128)S(1)}) custom-call(f32[256,128]{1,0:T(8,128)S(1)} %get-tuple-element.27.own_ref.maps_ref.own_maps_ref.refs_0_, f32[256,128]{1,0:T(8,128)S(1)} %collective-permute-done.1.other_ref.other_maps_ref.refs_1_), custom_call_target="tpu_custom_call" | custom-call | flops 10000000000 | bytes 1000000 | tf_op jit(solution)/shard_map/join_maps/pallas_call | solution.py:304
  11.7 5.2 %collective-permute-start.8 = (f32[128,128]{1,0:T(8,128)S(1)}, f32[128,128]{1,0:T(8,128)S(1)}, u32[]{:S(2)}, u32[]{:S(2)}) collective-permute-start(f32[128,128]{1,0:T(8,128)S(1)} %get-tuple-element.39), channel_id=1, source_target_pairs={{0,13},{1,12},{2,15},{3,14},{4,9},{5,8},{6,11},{7,10},{8,5},{9,4},... | collective-permute-start | bytes 196616 | tf_op jit(solution)/shard_map/ppermute | solution.py:531
  16.8 0.0 collective-permute-start.7
  16.8 0.3 collective-permute-start.6
  17.1 0.0 collective-permute-done.2.near_ref
  17.1 0.0 collective-permute-done.3.far_ref
  17.1 0.0 copy-done.6
  17.1 2.7 %outer_residual.1 = (f32[8,3,16,512]{3,2,1,0:T(8,128)S(1)}, f32[8,128]{1,0:T(8,128)S(1)}) custom-call(f32[8,3,32,512]{3,2,1,0:T(8,128)S(1)} %copy-done, f32[8,3,32,512]{3,2,1,0:T(8,128)S(1)} %copy-done.1, f32[32,512]{1,0:T(8,128)S(1)} %copy-done.5, s32[3,32,512]{2,1,0:T(8,128)S(1)} %copy-done.3, f32[3,32,512]{2,1,0:T(8,128)S(1)} %copy-done.4, ...), custom_call_target="tpu_custom_call" | custom-call | flops 603979776 | bytes 3145728 | tf_op jit(solution)/shard_map/outer_residual/pallas_call | solution.py:197
  19.8 0.5 %collective-permute-start.4 = (f32[8,128]{1,0:T(8,128)S(1)}, f32[8,128]{1,0:T(8,128)S(1)}, u32[]{:S(2)}, u32[]{:S(2)}) collective-permute-start(f32[8,128]{1,0:T(8,128)S(1)} %get-tuple-element.36.own_ref.refs_6_), channel_id=1, source_target_pairs={{0,1},{1,0},{2,3},{3,2},{4,5},{5,4},{6,7},{7,6},{8,9},{9,8},{10,11... | collective-permute-start | bytes 12296 | tf_op jit(solution)/shard_map/ppermute | solution.py:531
  20.3 0.8 %collective-permute-done.4.other_ref.refs_7_ = f32[8,128]{1,0:T(8,128)S(1)} collective-permute-done((f32[8,128]{1,0:T(8,128)S(1)}, f32[8,128]{1,0:T(8,128)S(1)}, u32[]{:S(2)}, u32[]{:S(2)}) %collective-permute-start.4) | collective-permute-done | bytes 4128 | tf_op jit(solution)/shard_map/ppermute | solution.py:531
  21.1 0.2 pair_shifts.1.own_ref.refs_2_
  21.3 2.4 %collective-permute-start.5 = (f32[16,128]{1,0:T(8,128)S(1)}, f32[16,128]{1,0:T(8,128)S(1)}, u32[]{:S(2)}, u32[]{:S(2)}) collective-permute-start(f32[16,128]{1,0:T(8,128)S(1)} %pair_shifts.1.own_ref.refs_2_), channel_id=1, source_target_pairs={{0,3},{1,2},{2,1},{3,0},{4,7},{5,6},{6,5},{7,4},{8,11},{9,10},{10,... | collective-permute-start | bytes 24584 | tf_op jit(solution)/shard_map/ppermute | solution.py:531
  23.7 1.4 %collective-permute-done.5.other_ref.refs_3_ = f32[16,128]{1,0:T(8,128)S(1)} collective-permute-done((f32[16,128]{1,0:T(8,128)S(1)}, f32[16,128]{1,0:T(8,128)S(1)}, u32[]{:S(2)}, u32[]{:S(2)}) %collective-permute-start.5) | collective-permute-done | bytes 8224 | tf_op jit(solution)/shard_map/ppermute | solution.py:531
  25.1 0.2 join_shifts.1.refs_3_
  25.3 0.0 collective-permute-done.8
  25.3 0.0 collective-permute-done.7
  25.3 0.0 collective-permute-done.6
  25.3 0.4 %collective-permute-start.9 = (f32[384,128]{1,0:T(8,128)S(1)}, f32[384,128]{1,0:T(8,128)S(1)}, u32[]{:S(2)}, u32[]{:S(2)}) collective-permute-start(f32[384,128]{1,0:T(8,128)S(1)} %constant_dynamic-update-slice_fusion.refs_1_), channel_id=1, source_target_pairs={{0,1},{1,0},{2,3},{3,2},{4,5},{5,4},{6,7},{7,6},{8,9},{9,8},{10,11... | collective-permute-start | bytes 589832 | tf_op jit(solution)/shard_map/ppermute | solution.py:531
  25.7 1.5 %collective-permute-start.12 = (f32[16,128]{1,0:T(8,128)S(1)}, f32[16,128]{1,0:T(8,128)S(1)}, u32[]{:S(2)}, u32[]{:S(2)}) collective-permute-start(f32[16,128]{1,0:T(8,128)S(1)} %join_shifts.1.refs_3_), channel_id=1, source_target_pairs={{0,9},{1,8},{2,11},{3,10},{4,13},{5,12},{6,15},{7,14},{8,1},{9,0},... | collective-permute-start | bytes 24584 | tf_op jit(solution)/shard_map/ppermute | solution.py:531
  27.2 1.3 %collective-permute-start.11 = (f32[16,128]{1,0:T(8,128)S(1)}, f32[16,128]{1,0:T(8,128)S(1)}, u32[]{:S(2)}, u32[]{:S(2)}) collective-permute-start(f32[16,128]{1,0:T(8,128)S(1)} %join_shifts.1.refs_3_), channel_id=1, source_target_pairs={{0,13},{1,12},{2,15},{3,14},{4,9},{5,8},{6,11},{7,10},{8,5},{9,4},... | collective-permute-start | bytes 24584 | tf_op jit(solution)/shard_map/ppermute | solution.py:531
  28.5 0.3 collective-permute-start.10
  28.9 1.1 %local_solution.1 = (f32[128,128]{1,0:T(8,128)S(1)}, f32[128,128]{1,0:T(8,128)S(1)}, f32[8,128]{1,0:T(8,128)S(1)}) custom-call(f32[256,128]{1,0:T(8,128)S(1)} %get-tuple-element.27.own_ref.maps_ref.own_maps_ref.refs_0_, f32[256,128]{1,0:T(8,128)S(1)} %collective-permute-done.1.other_ref.other_maps_ref.refs_1_, f32[16,128]{1,0:T(8,128)S(1)} %pair_shifts.1.own_ref.refs_2_, ...), custom_call_target="tpu_custom_call" | custom-call | flops 1000000000 | bytes 1000000 | tf_op jit(solution)/shard_map/local_solution/pallas_call | solution.py:411
  30.0 0.0 collective-permute-done.12.refs_6_
  30.0 2.1 %collective-permute-done.11.refs_5_ = f32[16,128]{1,0:T(8,128)S(1)} collective-permute-done((f32[16,128]{1,0:T(8,128)S(1)}, f32[16,128]{1,0:T(8,128)S(1)}, u32[]{:S(2)}, u32[]{:S(2)}) %collective-permute-start.11) | collective-permute-done | bytes 8224 | tf_op jit(solution)/shard_map/ppermute | solution.py:531
  32.1 0.0 collective-permute-done.10.refs_4_
  32.1 0.0 collective-permute-done.9.refs_2_
  32.1 2.8 %finish.1 = (f32[8,3,32,512]{3,2,1,0:T(8,128)}, f32[8,128]{1,0:T(8,128)}) custom-call(f32[256,128]{1,0:T(8,128)S(1)} %get-tuple-element.30.refs_0_, f32[384,128]{1,0:T(8,128)S(1)} %constant_dynamic-update-slice_fusion.refs_1_, f32[384,128]{1,0:T(8,128)S(1)} %collective-permute-done.9.refs_2_, f32[16,128]{1,0:T(8,128)S(1)} %join_shifts.1.refs_3_, ...), custom_call_target="tpu_custom_call" | custom-call | tf_op jit(solution)/shard_map/finish/pallas_call | solution.py:501
  (3 shorter events, 0.0 us)
Async XLA Ops:
  2.0 5.6 %copy-start = (f32[8,3,32,512]{3,2,1,0:T(8,128)S(1)}, f32[8,3,32,512]{3,2,1,0:T(8,128)}, u32[]{:S(2)}) copy-start(f32[8,3,32,512]{3,2,1,0:T(8,128)} %disp_ref.3) | copy-start | bytes 4718596
  2.0 5.6 %copy-start.1 = (f32[8,3,32,512]{3,2,1,0:T(8,128)S(1)}, f32[8,3,32,512]{3,2,1,0:T(8,128)}, u32[]{:S(2)}) copy-start(f32[8,3,32,512]{3,2,1,0:T(8,128)} %loads_ref.3) | copy-start | bytes 4718596
  2.0 5.6 %copy-start.3 = (s32[3,32,512]{2,1,0:T(8,128)S(1)}, s32[3,32,512]{2,1,0:T(8,128)}, u32[]{:S(2)}) copy-start(s32[3,32,512]{2,1,0:T(8,128)} %refs_12_.1) | copy-start | bytes 589828
  2.1 5.6 %copy-start.4 = (f32[3,32,512]{2,1,0:T(8,128)S(1)}, f32[3,32,512]{2,1,0:T(8,128)}, u32[]{:S(2)}) copy-start(f32[3,32,512]{2,1,0:T(8,128)} %refs_13_.1) | copy-start | bytes 589828
  2.1 5.6 %copy-start.5 = (f32[32,512]{1,0:T(8,128)S(1)}, f32[32,512]{1,0:T(8,128)}, u32[]{:S(2)}) copy-start(f32[32,512]{1,0:T(8,128)} %modulus_ref.3) | copy-start | bytes 196612
  2.1 1.4 %collective-permute-start = (f32[128,128]{1,0:T(8,128)S(1)}, f32[128,128]{1,0:T(8,128)S(1)}, u32[]{:S(2)}, u32[]{:S(2)}) collective-permute-start(f32[128,128]{1,0:T(8,128)S(1)} %get-tuple-element.26.own_ref.own_step_ref.refs_4_), channel_id=1, source_target_pairs={{0,1},{1,0},{2,3},{3,2},{4,5},{5,4},{6,7},{7,6},{8,9},{9,8},{10,11... | collective-permute-start | bytes 196616 | tf_op jit(solution)/shard_map/ppermute | solution.py:531
  3.5 4.1 %copy-start.2 = (f32[3,512,512]{2,1,0:T(8,128)S(1)}, f32[3,512,512]{2,1,0:T(8,128)}, u32[]{:S(2)}) copy-start(f32[3,512,512]{2,1,0:T(8,128)} %section_ref.1) | copy-start | bytes 9437188
  3.9 7.4 %collective-permute-start.1 = (f32[256,128]{1,0:T(8,128)S(1)}, f32[256,128]{1,0:T(8,128)S(1)}, u32[]{:S(2)}, u32[]{:S(2)}) collective-permute-start(f32[256,128]{1,0:T(8,128)S(1)} %get-tuple-element.27.own_ref.maps_ref.own_maps_ref.refs_0_), channel_id=1, source_target_pairs={{0,3},{1,2},{2,1},{3,0},{4,7},{5,6},{6,5},{7,4},{8,11},{9,10},{10,... | collective-permute-start | bytes 393224 | tf_op jit(solution)/shard_map/ppermute | solution.py:531
  6.6 10.6 %collective-permute-start.2 = (f32[288,128]{1,0:T(8,128)S(1)}, f32[288,128]{1,0:T(8,128)S(1)}, u32[]{:S(2)}, u32[]{:S(2)}) collective-permute-start(f32[288,128]{1,0:T(8,128)S(1)} %get-tuple-element.31), channel_id=1, source_target_pairs={{0,1},{1,0},{2,3},{3,2},{4,5},{5,4},{6,7},{7,6},{8,9},{9,8},{10,11... | collective-permute-start | bytes 442376 | tf_op jit(solution)/shard_map/ppermute | solution.py:531
  6.9 10.2 %collective-permute-start.3 = (f32[288,128]{1,0:T(8,128)S(1)}, f32[288,128]{1,0:T(8,128)S(1)}, u32[]{:S(2)}, u32[]{:S(2)}) collective-permute-start(f32[288,128]{1,0:T(8,128)S(1)} %get-tuple-element.32), channel_id=1, source_target_pairs={{1,2},{2,1},{3,4},{4,3},{5,6},{6,5},{7,8},{8,7},{9,10},{10,9},{11,... | collective-permute-start | bytes 442376 | tf_op jit(solution)/shard_map/ppermute | solution.py:536
  11.3 5.8 %copy-start.6 = (f32[128,128]{1,0:T(8,128)S(1)}, f32[128,128]{1,0:T(8,128)}, u32[]{:S(2)}) copy-start(f32[128,128]{1,0:T(8,128)} %refs_8_.1) | copy-start | bytes 196612
  11.7 13.6 %collective-permute-start.8 = (f32[128,128]{1,0:T(8,128)S(1)}, f32[128,128]{1,0:T(8,128)S(1)}, u32[]{:S(2)}, u32[]{:S(2)}) collective-permute-start(f32[128,128]{1,0:T(8,128)S(1)} %get-tuple-element.39), channel_id=1, source_target_pairs={{0,13},{1,12},{2,15},{3,14},{4,9},{5,8},{6,11},{7,10},{8,5},{9,4},... | collective-permute-start | bytes 196616 | tf_op jit(solution)/shard_map/ppermute | solution.py:531
  16.8 8.4 %collective-permute-start.7 = (f32[128,128]{1,0:T(8,128)S(1)}, f32[128,128]{1,0:T(8,128)S(1)}, u32[]{:S(2)}, u32[]{:S(2)}) collective-permute-start(f32[128,128]{1,0:T(8,128)S(1)} %get-tuple-element.39), channel_id=1, source_target_pairs={{0,9},{1,8},{2,11},{3,10},{4,13},{5,12},{6,15},{7,14},{8,1},{9,0},... | collective-permute-start | bytes 196616 | tf_op jit(solution)/shard_map/ppermute | solution.py:531
  16.8 8.4 %collective-permute-start.6 = (f32[128,128]{1,0:T(8,128)S(1)}, f32[128,128]{1,0:T(8,128)S(1)}, u32[]{:S(2)}, u32[]{:S(2)}) collective-permute-start(f32[128,128]{1,0:T(8,128)S(1)} %get-tuple-element.39), channel_id=1, source_target_pairs={{0,5},{1,4},{2,7},{3,6},{4,1},{5,0},{6,3},{7,2},{8,13},{9,12},{10,... | collective-permute-start | bytes 196616 | tf_op jit(solution)/shard_map/ppermute | solution.py:531
  19.8 1.3 %collective-permute-start.4 = (f32[8,128]{1,0:T(8,128)S(1)}, f32[8,128]{1,0:T(8,128)S(1)}, u32[]{:S(2)}, u32[]{:S(2)}) collective-permute-start(f32[8,128]{1,0:T(8,128)S(1)} %get-tuple-element.36.own_ref.refs_6_), channel_id=1, source_target_pairs={{0,1},{1,0},{2,3},{3,2},{4,5},{5,4},{6,7},{7,6},{8,9},{9,8},{10,11... | collective-permute-start | bytes 12296 | tf_op jit(solution)/shard_map/ppermute | solution.py:531
  21.3 3.8 %collective-permute-start.5 = (f32[16,128]{1,0:T(8,128)S(1)}, f32[16,128]{1,0:T(8,128)S(1)}, u32[]{:S(2)}, u32[]{:S(2)}) collective-permute-start(f32[16,128]{1,0:T(8,128)S(1)} %pair_shifts.1.own_ref.refs_2_), channel_id=1, source_target_pairs={{0,3},{1,2},{2,1},{3,0},{4,7},{5,6},{6,5},{7,4},{8,11},{9,10},{10,... | collective-permute-start | bytes 24584 | tf_op jit(solution)/shard_map/ppermute | solution.py:531
  25.3 6.8 %collective-permute-start.9 = (f32[384,128]{1,0:T(8,128)S(1)}, f32[384,128]{1,0:T(8,128)S(1)}, u32[]{:S(2)}, u32[]{:S(2)}) collective-permute-start(f32[384,128]{1,0:T(8,128)S(1)} %constant_dynamic-update-slice_fusion.refs_1_), channel_id=1, source_target_pairs={{0,1},{1,0},{2,3},{3,2},{4,5},{5,4},{6,7},{7,6},{8,9},{9,8},{10,11... | collective-permute-start | bytes 589832 | tf_op jit(solution)/shard_map/ppermute | solution.py:531
  25.7 4.3 %collective-permute-start.12 = (f32[16,128]{1,0:T(8,128)S(1)}, f32[16,128]{1,0:T(8,128)S(1)}, u32[]{:S(2)}, u32[]{:S(2)}) collective-permute-start(f32[16,128]{1,0:T(8,128)S(1)} %join_shifts.1.refs_3_), channel_id=1, source_target_pairs={{0,9},{1,8},{2,11},{3,10},{4,13},{5,12},{6,15},{7,14},{8,1},{9,0},... | collective-permute-start | bytes 24584 | tf_op jit(solution)/shard_map/ppermute | solution.py:531
  27.2 4.9 %collective-permute-start.11 = (f32[16,128]{1,0:T(8,128)S(1)}, f32[16,128]{1,0:T(8,128)S(1)}, u32[]{:S(2)}, u32[]{:S(2)}) collective-permute-start(f32[16,128]{1,0:T(8,128)S(1)} %join_shifts.1.refs_3_), channel_id=1, source_target_pairs={{0,13},{1,12},{2,15},{3,14},{4,9},{5,8},{6,11},{7,10},{8,5},{9,4},... | collective-permute-start | bytes 24584 | tf_op jit(solution)/shard_map/ppermute | solution.py:531
  28.5 3.5 %collective-permute-start.10 = (f32[16,128]{1,0:T(8,128)S(1)}, f32[16,128]{1,0:T(8,128)S(1)}, u32[]{:S(2)}, u32[]{:S(2)}) collective-permute-start(f32[16,128]{1,0:T(8,128)S(1)} %join_shifts.1.refs_3_), channel_id=1, source_target_pairs={{0,5},{1,4},{2,7},{3,6},{4,1},{5,0},{6,3},{7,2},{8,13},{9,12},{10,... | collective-permute-start | bytes 24584 | tf_op jit(solution)/shard_map/ppermute | solution.py:531

commit v7 on v6

--- a/solution.py
+++ b/solution.py
@@ -567,7 +567,14 @@
         joins.append((maps, other_maps, mixed))
         maps = joined
         stride *= 2
-    halves = [swap(half, hop * width ^ 1) for hop in range(1, ways)]
+    def needed(source, target):
+        block = source // width
+        return target // width < block if source & 1 else 0 < block < ways - 1
+
+    halves = []
+    for hop in range(1, ways):
+        moves = [(i, i ^ (hop * width ^ 1)) for i in range(count)]
+        halves.append(lax.ppermute(half, "row", [move for move in moves if needed(*move)]))
     outer_base, value = residual_call(
         outer_kernel,
         True,

time: 35 us -> 40.8 us (1.17)
  starting transfers between devices: 16.1 us -> 20.6 us
  waiting for transfers between devices: 5.18 us -> 6.38 us
    ppermute x0 -> x3, starting transfers between devices: none -> 3.88 us  [per_device(): lax.ppermute(half, 'row', [move for move in moves if needed(*move)])]
    ppermute x12 -> x9, waiting for transfers between devices: 5.18 us -> 6.37 us  [swap(): return lax.ppermute(value, 'row', [(i, i ^ mask) for i in range(count)])]
    ppermute x12 -> x9, starting transfers between devices: 15.5 us -> 16.1 us  [swap(): return lax.ppermute(value, 'row', [(i, i ^ mask) for i in range(count)])]
  transfers between devices with their start and end apart: 13 -> 13, of which waited for: 4 -> 4; matrix products, arithmetic and copies ran while one was open for 0% -> 0% of each run, Pallas kernels for 23% -> 20%
where the time goes in v7:
time: 40.8 us; the launch traced here: 40.6 us
  starting transfers between devices  20.6 us (50%)
  Pallas kernels  12.7 us (31%)
  waiting for transfers between devices  6.38 us (16%)
  between operations  0.88 us (2%)
    ppermute x9, starting transfers between devices, swap(): return lax.ppermute(value, 'row', [(i, i ^ mask) for i in range(count)])  16.1 us
    ppermute x9, waiting for transfers between devices, swap(): return lax.ppermute(value, 'row', [(i, i ^ mask) for i in range(count)])  6.37 us
    pallas_call x2, Pallas kernels, residual_call(): pl.pallas_call(kernel, in_specs=[local] * len(operands), out_specs=[local...  6.32 us
    ppermute x3, starting transfers between devices, per_device(): lax.ppermute(half, 'row', [move for move in moves if needed(*move)])  3.88 us
    pallas_call x1, Pallas kernels, finish_call(): pl.pallas_call(functools.partial(finish_kernel, width, ways), in_specs=[l...  2.82 us
    pallas_call x1, Pallas kernels, start_call(): pl.pallas_call(start_kernel, in_specs=[pl.BlockSpec(memory_space=pltpu.HB...  1.38 us
    pallas_call x1, Pallas kernels, local_call(): pl.pallas_call(functools.partial(local_kernel, strides), out_shape=[squar...  1.1 us
  transfers between devices with their start and end apart: 13, of which 4 were waited for; matrix products, arithmetic and copies ran while one was open for 0% of the time, Pallas kernels for 20%

profile of v7, /device:TPU:0, one launch (start us, length us, event | category | flops | bytes accessed | tf_op | source)
XLA Modules:
  0.0 40.6 jit_solution(13681022596333299411)
XLA Ops:
  0.6 1.4 %start.1 = (f32[128,128]{1,0:T(8,128)S(1)}, f32[288,128]{1,0:T(8,128)S(1)}, f32[288,128]{1,0:T(8,128)S(1)}) custom-call(f32[128,128]{1,0:T(8,128)} %refs_8_.1, f32[128,128]{1,0:T(8,128)} %sub_hbm.1, f32[8,3,32,512]{3,2,1,0:T(8,128)} %disp_ref.3), custom_call_target="tpu_custom_call" | custom-call | flops 10000000000 | bytes 1000000 | tf_op jit(solution)/shard_map/start/pallas_call | solution.py:260
  2.0 0.0 copy-start
  2.0 0.0 copy-start.1
  2.0 0.0 copy-start.3
  2.1 0.0 copy-start.4
  2.1 0.0 copy-start.5
  2.1 0.5 %collective-permute-start = (f32[128,128]{1,0:T(8,128)S(1)}, f32[128,128]{1,0:T(8,128)S(1)}, u32[]{:S(2)}, u32[]{:S(2)}) collective-permute-start(f32[128,128]{1,0:T(8,128)S(1)} %get-tuple-element.26.own_ref.own_step_ref.refs_4_), channel_id=1, source_target_pairs={{0,1},{1,0},{2,3},{3,2},{4,5},{5,4},{6,7},{7,6},{8,9},{9,8},{10,11... | collective-permute-start | bytes 196616 | tf_op jit(solution)/shard_map/ppermute | solution.py:531
  2.6 0.9 %collective-permute-done.other_ref.other_step_ref.refs_5_ = f32[128,128]{1,0:T(8,128)S(1)} collective-permute-done((f32[128,128]{1,0:T(8,128)S(1)}, f32[128,128]{1,0:T(8,128)S(1)}, u32[]{:S(2)}, u32[]{:S(2)}) %collective-permute-start) | collective-permute-done | bytes 65568 | tf_op jit(solution)/shard_map/ppermute | solution.py:531
  3.5 0.0 copy-start.2
  3.5 0.4 pair_maps.1
  3.9 2.7 %collective-permute-start.1 = (f32[256,128]{1,0:T(8,128)S(1)}, f32[256,128]{1,0:T(8,128)S(1)}, u32[]{:S(2)}, u32[]{:S(2)}) collective-permute-start(f32[256,128]{1,0:T(8,128)S(1)} %get-tuple-element.27.own_ref.maps_ref.own_maps_ref.refs_0_), channel_id=1, source_target_pairs={{0,3},{1,2},{2,1},{3,0},{4,7},{5,6},{6,5},{7,4},{8,11},{9,10},{10,... | collective-permute-start | bytes 393224 | tf_op jit(solution)/shard_map/ppermute | solution.py:531
  6.6 0.4 collective-permute-start.2
  6.9 0.7 %collective-permute-start.3 = (f32[288,128]{1,0:T(8,128)S(1)}, f32[288,128]{1,0:T(8,128)S(1)}, u32[]{:S(2)}, u32[]{:S(2)}) collective-permute-start(f32[288,128]{1,0:T(8,128)S(1)} %get-tuple-element.32), channel_id=1, source_target_pairs={{1,2},{2,1},{3,4},{4,3},{5,6},{6,5},{7,8},{8,7},{9,10},{10,9},{11,... | collective-permute-start | bytes 442376 | tf_op jit(solution)/shard_map/ppermute | solution.py:536
  7.6 0.0 copy-done
  7.6 0.0 copy-done.1
  7.6 0.0 copy-done.3
  7.6 0.0 copy-done.4
  7.6 0.0 copy-done.5
  7.6 0.0 copy-done.2
  7.6 3.6 %inner_residual.1 = (f32[8,3,16,512]{3,2,1,0:T(8,128)S(1)}, f32[3,8,16,512]{3,2,1,0:T(8,128)S(1)}, f32[3,8,512]{2,1,0:T(8,128)S(1)}, f32[32,64]{1,0:T(8,128)S(1)}) custom-call(f32[8,3,32,512]{3,2,1,0:T(8,128)S(1)} %copy-done, f32[8,3,32,512]{3,2,1,0:T(8,128)S(1)} %copy-done.1, f32[3,512,512]{2,1,0:T(8,128)S(1)} %copy-done.2, f32[32,512]{1,0:T(8,128)S(1)} %copy-done.5, ...), custom_call_target="tpu_custom_call" | custom-call | flops 603979776 | bytes 3145728 | tf_op jit(solution)/shard_map/inner_residual/pallas_call | solution.py:197
  11.3 0.0 collective-permute-done.1.other_ref.other_maps_ref.refs_1_
  11.3 0.0 copy-start.6
  11.3 0.4 join_maps.1
  11.7 1.3 %collective-permute-start.8 = (f32[128,128]{1,0:T(8,128)S(1)}, f32[128,128]{1,0:T(8,128)S(1)}, u32[]{:S(2)}, u32[]{:S(2)}) collective-permute-start(f32[128,128]{1,0:T(8,128)S(1)} %get-tuple-element.39), channel_id=1, source_target_pairs={{4,9},{6,11},{8,5},{9,4},{10,7},{11,6},{13,0},{15,2},{20,25},{22,2... | collective-permute-start | bytes 196616 | tf_op jit(solution)/shard_map/ppermute | solution.py:577
  13.0 1.3 %collective-permute-start.7 = (f32[128,128]{1,0:T(8,128)S(1)}, f32[128,128]{1,0:T(8,128)S(1)}, u32[]{:S(2)}, u32[]{:S(2)}) collective-permute-start(f32[128,128]{1,0:T(8,128)S(1)} %get-tuple-element.39), channel_id=1, source_target_pairs={{4,13},{6,15},{8,1},{9,0},{10,3},{11,2},{13,4},{15,6},{20,29},{22,... | collective-permute-start | bytes 196616 | tf_op jit(solution)/shard_map/ppermute | solution.py:577
  14.3 1.3 %collective-permute-start.6 = (f32[128,128]{1,0:T(8,128)S(1)}, f32[128,128]{1,0:T(8,128)S(1)}, u32[]{:S(2)}, u32[]{:S(2)}) collective-permute-start(f32[128,128]{1,0:T(8,128)S(1)} %get-tuple-element.39), channel_id=1, source_target_pairs={{4,1},{5,0},{6,3},{7,2},{8,13},{10,15},{13,8},{15,10},{20,17},{21,... | collective-permute-start | bytes 196616 | tf_op jit(solution)/shard_map/ppermute | solution.py:577
  15.6 0.0 collective-permute-done.2.near_ref
  15.6 0.0 collective-permute-done.3.far_ref
  15.6 0.0 copy-done.6
  15.6 2.7 %outer_residual.1 = (f32[8,3,16,512]{3,2,1,0:T(8,128)S(1)}, f32[8,128]{1,0:T(8,128)S(1)}) custom-call(f32[8,3,32,512]{3,2,1,0:T(8,128)S(1)} %copy-done, f32[8,3,32,512]{3,2,1,0:T(8,128)S(1)} %copy-done.1, f32[32,512]{1,0:T(8,128)S(1)} %copy-done.5, s32[3,32,512]{2,1,0:T(8,128)S(1)} %copy-done.3, f32[3,32,512]{2,1,0:T(8,128)S(1)} %copy-done.4, ...), custom_call_target="tpu_custom_call" | custom-call | flops 603979776 | bytes 3145728 | tf_op jit(solution)/shard_map/outer_residual/pallas_call | solution.py:197
  18.3 1.0 %collective-permute-start.4 = (f32[8,128]{1,0:T(8,128)S(1)}, f32[8,128]{1,0:T(8,128)S(1)}, u32[]{:S(2)}, u32[]{:S(2)}) collective-permute-start(f32[8,128]{1,0:T(8,128)S(1)} %get-tuple-element.36.own_ref.refs_6_), channel_id=1, source_target_pairs={{0,1},{1,0},{2,3},{3,2},{4,5},{5,4},{6,7},{7,6},{8,9},{9,8},{10,11... | collective-permute-start | bytes 12296 | tf_op jit(solution)/shard_map/ppermute | solution.py:531
  19.3 0.8 %collective-permute-done.4.other_ref.refs_7_ = f32[8,128]{1,0:T(8,128)S(1)} collective-permute-done((f32[8,128]{1,0:T(8,128)S(1)}, f32[8,128]{1,0:T(8,128)S(1)}, u32[]{:S(2)}, u32[]{:S(2)}) %collective-permute-start.4) | collective-permute-done | bytes 4128 | tf_op jit(solution)/shard_map/ppermute | solution.py:531
  20.1 0.2 pair_shifts.1.own_ref.refs_2_
  20.3 2.8 %collective-permute-start.5 = (f32[16,128]{1,0:T(8,128)S(1)}, f32[16,128]{1,0:T(8,128)S(1)}, u32[]{:S(2)}, u32[]{:S(2)}) collective-permute-start(f32[16,128]{1,0:T(8,128)S(1)} %pair_shifts.1.own_ref.refs_2_), channel_id=1, source_target_pairs={{0,3},{1,2},{2,1},{3,0},{4,7},{5,6},{6,5},{7,4},{8,11},{9,10},{10,... | collective-permute-start | bytes 24584 | tf_op jit(solution)/shard_map/ppermute | solution.py:531
  23.1 1.4 %collective-permute-done.5.other_ref.refs_3_ = f32[16,128]{1,0:T(8,128)S(1)} collective-permute-done((f32[16,128]{1,0:T(8,128)S(1)}, f32[16,128]{1,0:T(8,128)S(1)}, u32[]{:S(2)}, u32[]{:S(2)}) %collective-permute-start.5) | collective-permute-done | bytes 8224 | tf_op jit(solution)/shard_map/ppermute | solution.py:531
  24.4 0.2 join_shifts.1.refs_3_
  24.6 0.0 collective-permute-done.8
  24.6 0.0 collective-permute-done.7
  24.6 0.0 collective-permute-done.6
  24.7 0.2 collective-permute-start.9
  24.9 8.0 %collective-permute-start.12 = (f32[16,128]{1,0:T(8,128)S(1)}, f32[16,128]{1,0:T(8,128)S(1)}, u32[]{:S(2)}, u32[]{:S(2)}) collective-permute-start(f32[16,128]{1,0:T(8,128)S(1)} %join_shifts.1.refs_3_), channel_id=1, source_target_pairs={{0,9},{1,8},{2,11},{3,10},{4,13},{5,12},{6,15},{7,14},{8,1},{9,0},... | collective-permute-start | bytes 24584 | tf_op jit(solution)/shard_map/ppermute | solution.py:531
  32.9 0.0 collective-permute-start.11
  32.9 0.5 %collective-permute-start.10 = (f32[16,128]{1,0:T(8,128)S(1)}, f32[16,128]{1,0:T(8,128)S(1)}, u32[]{:S(2)}, u32[]{:S(2)}) collective-permute-start(f32[16,128]{1,0:T(8,128)S(1)} %join_shifts.1.refs_3_), channel_id=1, source_target_pairs={{0,5},{1,4},{2,7},{3,6},{4,1},{5,0},{6,3},{7,2},{8,13},{9,12},{10,... | collective-permute-start | bytes 24584 | tf_op jit(solution)/shard_map/ppermute | solution.py:531
  33.4 1.1 %local_solution.1 = (f32[128,128]{1,0:T(8,128)S(1)}, f32[128,128]{1,0:T(8,128)S(1)}, f32[8,128]{1,0:T(8,128)S(1)}) custom-call(f32[256,128]{1,0:T(8,128)S(1)} %get-tuple-element.27.own_ref.maps_ref.own_maps_ref.refs_0_, f32[256,128]{1,0:T(8,128)S(1)} %collective-permute-done.1.other_ref.other_maps_ref.refs_1_, f32[16,128]{1,0:T(8,128)S(1)} %pair_shifts.1.own_ref.refs_2_, ...), custom_call_target="tpu_custom_call" | custom-call | flops 1000000000 | bytes 1000000 | tf_op jit(solution)/shard_map/local_solution/pallas_call | solution.py:411
  34.5 0.0 collective-permute-done.12.refs_6_
  34.5 3.3 %collective-permute-done.11.refs_5_ = f32[16,128]{1,0:T(8,128)S(1)} collective-permute-done((f32[16,128]{1,0:T(8,128)S(1)}, f32[16,128]{1,0:T(8,128)S(1)}, u32[]{:S(2)}, u32[]{:S(2)}) %collective-permute-start.11) | collective-permute-done | bytes 8224 | tf_op jit(solution)/shard_map/ppermute | solution.py:531
  37.8 0.0 collective-permute-done.10.refs_4_
  37.8 0.0 collective-permute-done.9.refs_2_
  37.8 2.8 %finish.1 = (f32[8,3,32,512]{3,2,1,0:T(8,128)}, f32[8,128]{1,0:T(8,128)}) custom-call(f32[256,128]{1,0:T(8,128)S(1)} %get-tuple-element.30.refs_0_, f32[384,128]{1,0:T(8,128)S(1)} %constant_dynamic-update-slice_fusion.refs_1_, f32[384,128]{1,0:T(8,128)S(1)} %collective-permute-done.9.refs_2_, f32[16,128]{1,0:T(8,128)S(1)} %join_shifts.1.refs_3_, ...), custom_call_target="tpu_custom_call" | custom-call | tf_op jit(solution)/shard_map/finish/pallas_call | solution.py:501
  (3 shorter events, 0.0 us)
Async XLA Ops:
  2.0 5.6 %copy-start = (f32[8,3,32,512]{3,2,1,0:T(8,128)S(1)}, f32[8,3,32,512]{3,2,1,0:T(8,128)}, u32[]{:S(2)}) copy-start(f32[8,3,32,512]{3,2,1,0:T(8,128)} %disp_ref.3) | copy-start | bytes 4718596
  2.0 5.6 %copy-start.1 = (f32[8,3,32,512]{3,2,1,0:T(8,128)S(1)}, f32[8,3,32,512]{3,2,1,0:T(8,128)}, u32[]{:S(2)}) copy-start(f32[8,3,32,512]{3,2,1,0:T(8,128)} %loads_ref.3) | copy-start | bytes 4718596
  2.0 5.6 %copy-start.3 = (s32[3,32,512]{2,1,0:T(8,128)S(1)}, s32[3,32,512]{2,1,0:T(8,128)}, u32[]{:S(2)}) copy-start(s32[3,32,512]{2,1,0:T(8,128)} %refs_12_.1) | copy-start | bytes 589828
  2.1 5.6 %copy-start.4 = (f32[3,32,512]{2,1,0:T(8,128)S(1)}, f32[3,32,512]{2,1,0:T(8,128)}, u32[]{:S(2)}) copy-start(f32[3,32,512]{2,1,0:T(8,128)} %refs_13_.1) | copy-start | bytes 589828
  2.1 5.6 %copy-start.5 = (f32[32,512]{1,0:T(8,128)S(1)}, f32[32,512]{1,0:T(8,128)}, u32[]{:S(2)}) copy-start(f32[32,512]{1,0:T(8,128)} %modulus_ref.3) | copy-start | bytes 196612
  2.1 1.4 %collective-permute-start = (f32[128,128]{1,0:T(8,128)S(1)}, f32[128,128]{1,0:T(8,128)S(1)}, u32[]{:S(2)}, u32[]{:S(2)}) collective-permute-start(f32[128,128]{1,0:T(8,128)S(1)} %get-tuple-element.26.own_ref.own_step_ref.refs_4_), channel_id=1, source_target_pairs={{0,1},{1,0},{2,3},{3,2},{4,5},{5,4},{6,7},{7,6},{8,9},{9,8},{10,11... | collective-permute-start | bytes 196616 | tf_op jit(solution)/shard_map/ppermute | solution.py:531
  3.5 4.1 %copy-start.2 = (f32[3,512,512]{2,1,0:T(8,128)S(1)}, f32[3,512,512]{2,1,0:T(8,128)}, u32[]{:S(2)}) copy-start(f32[3,512,512]{2,1,0:T(8,128)} %section_ref.1) | copy-start | bytes 9437188
  3.9 7.4 %collective-permute-start.1 = (f32[256,128]{1,0:T(8,128)S(1)}, f32[256,128]{1,0:T(8,128)S(1)}, u32[]{:S(2)}, u32[]{:S(2)}) collective-permute-start(f32[256,128]{1,0:T(8,128)S(1)} %get-tuple-element.27.own_ref.maps_ref.own_maps_ref.refs_0_), channel_id=1, source_target_pairs={{0,3},{1,2},{2,1},{3,0},{4,7},{5,6},{6,5},{7,4},{8,11},{9,10},{10,... | collective-permute-start | bytes 393224 | tf_op jit(solution)/shard_map/ppermute | solution.py:531
  6.6 9.0 %collective-permute-start.2 = (f32[288,128]{1,0:T(8,128)S(1)}, f32[288,128]{1,0:T(8,128)S(1)}, u32[]{:S(2)}, u32[]{:S(2)}) collective-permute-start(f32[288,128]{1,0:T(8,128)S(1)} %get-tuple-element.31), channel_id=1, source_target_pairs={{0,1},{1,0},{2,3},{3,2},{4,5},{5,4},{6,7},{7,6},{8,9},{9,8},{10,11... | collective-permute-start | bytes 442376 | tf_op jit(solution)/shard_map/ppermute | solution.py:531
  6.9 8.7 %collective-permute-start.3 = (f32[288,128]{1,0:T(8,128)S(1)}, f32[288,128]{1,0:T(8,128)S(1)}, u32[]{:S(2)}, u32[]{:S(2)}) collective-permute-start(f32[288,128]{1,0:T(8,128)S(1)} %get-tuple-element.32), channel_id=1, source_target_pairs={{1,2},{2,1},{3,4},{4,3},{5,6},{6,5},{7,8},{8,7},{9,10},{10,9},{11,... | collective-permute-start | bytes 442376 | tf_op jit(solution)/shard_map/ppermute | solution.py:536
  11.3 4.3 %copy-start.6 = (f32[128,128]{1,0:T(8,128)S(1)}, f32[128,128]{1,0:T(8,128)}, u32[]{:S(2)}) copy-start(f32[128,128]{1,0:T(8,128)} %refs_8_.1) | copy-start | bytes 196612
  11.7 12.9 %collective-permute-start.8 = (f32[128,128]{1,0:T(8,128)S(1)}, f32[128,128]{1,0:T(8,128)S(1)}, u32[]{:S(2)}, u32[]{:S(2)}) collective-permute-start(f32[128,128]{1,0:T(8,128)S(1)} %get-tuple-element.39), channel_id=1, source_target_pairs={{4,9},{6,11},{8,5},{9,4},{10,7},{11,6},{13,0},{15,2},{20,25},{22,2... | collective-permute-start | bytes 196616 | tf_op jit(solution)/shard_map/ppermute | solution.py:577
  13.0 11.6 %collective-permute-start.7 = (f32[128,128]{1,0:T(8,128)S(1)}, f32[128,128]{1,0:T(8,128)S(1)}, u32[]{:S(2)}, u32[]{:S(2)}) collective-permute-start(f32[128,128]{1,0:T(8,128)S(1)} %get-tuple-element.39), channel_id=1, source_target_pairs={{4,13},{6,15},{8,1},{9,0},{10,3},{11,2},{13,4},{15,6},{20,29},{22,... | collective-permute-start | bytes 196616 | tf_op jit(solution)/shard_map/ppermute | solution.py:577
  14.3 10.3 %collective-permute-start.6 = (f32[128,128]{1,0:T(8,128)S(1)}, f32[128,128]{1,0:T(8,128)S(1)}, u32[]{:S(2)}, u32[]{:S(2)}) collective-permute-start(f32[128,128]{1,0:T(8,128)S(1)} %get-tuple-element.39), channel_id=1, source_target_pairs={{4,1},{5,0},{6,3},{7,2},{8,13},{10,15},{13,8},{15,10},{20,17},{21,... | collective-permute-start | bytes 196616 | tf_op jit(solution)/shard_map/ppermute | solution.py:577
  18.3 1.8 %collective-permute-start.4 = (f32[8,128]{1,0:T(8,128)S(1)}, f32[8,128]{1,0:T(8,128)S(1)}, u32[]{:S(2)}, u32[]{:S(2)}) collective-permute-start(f32[8,128]{1,0:T(8,128)S(1)} %get-tuple-element.36.own_ref.refs_6_), channel_id=1, source_target_pairs={{0,1},{1,0},{2,3},{3,2},{4,5},{5,4},{6,7},{7,6},{8,9},{9,8},{10,11... | collective-permute-start | bytes 12296 | tf_op jit(solution)/shard_map/ppermute | solution.py:531
  20.3 4.2 %collective-permute-start.5 = (f32[16,128]{1,0:T(8,128)S(1)}, f32[16,128]{1,0:T(8,128)S(1)}, u32[]{:S(2)}, u32[]{:S(2)}) collective-permute-start(f32[16,128]{1,0:T(8,128)S(1)} %pair_shifts.1.own_ref.refs_2_), channel_id=1, source_target_pairs={{0,3},{1,2},{2,1},{3,0},{4,7},{5,6},{6,5},{7,4},{8,11},{9,10},{10,... | collective-permute-start | bytes 24584 | tf_op jit(solution)/shard_map/ppermute | solution.py:531
  24.7 13.1 %collective-permute-start.9 = (f32[384,128]{1,0:T(8,128)S(1)}, f32[384,128]{1,0:T(8,128)S(1)}, u32[]{:S(2)}, u32[]{:S(2)}) collective-permute-start(f32[384,128]{1,0:T(8,128)S(1)} %constant_dynamic-update-slice_fusion.refs_1_), channel_id=1, source_target_pairs={{0,1},{1,0},{2,3},{3,2},{4,5},{5,4},{6,7},{7,6},{8,9},{9,8},{10,11... | collective-permute-start | bytes 589832 | tf_op jit(solution)/shard_map/ppermute | solution.py:531
  24.9 9.6 %collective-permute-start.12 = (f32[16,128]{1,0:T(8,128)S(1)}, f32[16,128]{1,0:T(8,128)S(1)}, u32[]{:S(2)}, u32[]{:S(2)}) collective-permute-start(f32[16,128]{1,0:T(8,128)S(1)} %join_shifts.1.refs_3_), channel_id=1, source_target_pairs={{0,9},{1,8},{2,11},{3,10},{4,13},{5,12},{6,15},{7,14},{8,1},{9,0},... | collective-permute-start | bytes 24584 | tf_op jit(solution)/shard_map/ppermute | solution.py:531
  32.9 4.9 %collective-permute-start.11 = (f32[16,128]{1,0:T(8,128)S(1)}, f32[16,128]{1,0:T(8,128)S(1)}, u32[]{:S(2)}, u32[]{:S(2)}) collective-permute-start(f32[16,128]{1,0:T(8,128)S(1)} %join_shifts.1.refs_3_), channel_id=1, source_target_pairs={{0,13},{1,12},{2,15},{3,14},{4,9},{5,8},{6,11},{7,10},{8,5},{9,4},... | collective-permute-start | bytes 24584 | tf_op jit(solution)/shard_map/ppermute | solution.py:531
  32.9 4.9 %collective-permute-start.10 = (f32[16,128]{1,0:T(8,128)S(1)}, f32[16,128]{1,0:T(8,128)S(1)}, u32[]{:S(2)}, u32[]{:S(2)}) collective-permute-start(f32[16,128]{1,0:T(8,128)S(1)} %join_shifts.1.refs_3_), channel_id=1, source_target_pairs={{0,5},{1,4},{2,7},{3,6},{4,1},{5,0},{6,3},{7,2},{8,13},{9,12},{10,... | collective-permute-start | bytes 24584 | tf_op jit(solution)/shard_map/ppermute | solution.py:531
